TPU v7x, 32 devices: a whole 2x2x4 slice. The times are simulated.
32 devices in a mesh: groups: 2 (over y), rows: 4 (over z), cols: 4 (over x, core).
Axes of the slice: x: 2, y: 2, z: 4, core: 2. Of those that a mesh axis runs over, the one named last changes fastest.
Arguments:
- coupling: bfloat16 [6, 8192, 8192], P('groups', 'cols', 'rows'), parts along dimension 0, may hold values from -0.0625 to 0.0625
- diag_inverse: bfloat16 [6, 8192, 8192], P('groups', 'rows', 'cols'), parts along dimension 0, as said below
- loads: bfloat16 [6, 128, 8192], P('groups', None, 'cols'), parts along dimension 0, may hold values from -6 to 6
- axle_index: int32 [64], P('groups'), parts along dimension 0, may hold values from 0 to 127
Outputs:
- influence: float32 [6, 32, 8192], P('groups', None, 'cols'), parts along dimension 0
- forward: float32 [6, 32, 8192], P('groups', None, 'rows'), parts along dimension 0
There are 2 independent parts, one for each index of `groups`. A program takes and returns all parts, laid end to end along the dimension named above; each array names one. Nothing has to cross between parts.
Inputs may be any that keep to these rules, and one draw needn't show every extreme that they name: `diag_inverse`: lower triangular with a positive diagonal.
All inputs are finite; a program needn't handle non-finite values.
Results may differ from a plain program's by a relative error of at most 0.0065.
Values sent between devices are 32-bit elements; how exact they have to be, the bound alone decides.
No kernel may reach another device: no remote copies, remote signals or barrier semaphores. Data moves between devices by JAX's collectives and lax.ppermute only.
A program may use at most 128 MiB of HBM per device.

v0:
```python
import jax
import jax.numpy as jnp
from jax import lax
from jax.sharding import PartitionSpec as P

LEVELS = 3


def pair_index(high, low):
    return high * (high - 1) // 2 + low


def forward_couple(partial_value):
    return lax.psum(partial_value, "rows")


def forward_diag(resid, tile):
    partial_value = jnp.einsum(
        "lm,im->li", resid.astype(jnp.bfloat16), tile, preferred_element_type=jnp.float32
    )
    return lax.psum(partial_value, "cols")


def backward_couple(partial_value):
    return lax.psum(partial_value, "cols")


def backward_diag(resid, tile):
    partial_value = jnp.einsum(
        "li,im->lm", resid.astype(jnp.bfloat16), tile, preferred_element_type=jnp.float32
    )
    return lax.psum(partial_value, "rows")


def lower_term(vector_bf, block):
    return jnp.einsum("lj,ij->li", vector_bf, block, preferred_element_type=jnp.float32)


def upper_term(vector_bf, block):
    return jnp.einsum("li,ij->lj", vector_bf, block, preferred_element_type=jnp.float32)


def solve_batch(rhs, coupling, diag_inverse):
    solved = []
    solved_bf = []
    for level in range(LEVELS):
        resid = rhs[level]
        if level > 0:
            partial_value = lower_term(solved_bf[0], coupling[pair_index(level, 0)])
            for lower in range(1, level):
                partial_value = partial_value + lower_term(
                    solved_bf[lower], coupling[pair_index(level, lower)]
                )
            resid = resid - forward_couple(partial_value)
        value = forward_diag(resid, diag_inverse[level])
        solved.append(value)
        solved_bf.append(value.astype(jnp.bfloat16))
    answers = [None] * LEVELS
    answers_bf = [None] * LEVELS
    for level in range(LEVELS - 1, -1, -1):
        resid = solved[level]
        if level < LEVELS - 1:
            partial_value = upper_term(
                answers_bf[LEVELS - 1], coupling[pair_index(LEVELS - 1, level)]
            )
            for upper in range(level + 1, LEVELS - 1):
                partial_value = partial_value + upper_term(
                    answers_bf[upper], coupling[pair_index(upper, level)]
                )
            resid = resid - backward_couple(partial_value)
        value = backward_diag(resid, diag_inverse[level])
        answers[level] = value
        answers_bf[level] = value.astype(jnp.bfloat16)
    return (jnp.stack(answers), jnp.stack(solved))


def body(coupling, diag_inverse, loads, axle_index):
    positions = loads.shape[1]
    selector = (axle_index[:, None] == jnp.arange(positions, dtype=jnp.int32)[None, :]).astype(
        jnp.bfloat16
    )
    rhs = jnp.einsum("lp,kpc->klc", selector, loads, preferred_element_type=jnp.float32)
    answer, solved = solve_batch(rhs, coupling, diag_inverse)
    return (answer, solved)


def solution(mesh):
    placed = (
        P("groups", "cols", "rows"),
        P("groups", "rows", "cols"),
        P("groups", None, "cols"),
        P("groups"),
    )
    return jax.shard_map(
        body,
        mesh=mesh,
        in_specs=placed,
        out_specs=(P("groups", None, "cols"), P("groups", None, "rows")),
        check_vma=False,
    )
```

profile of v0, /device:TPU:0, one launch (start us, length us, event | category | flops | bytes accessed | tf_op | source)
XLA Modules:
  0.0 431.7 jit_solution(7310455258160250758)
XLA Ops:
  7.2 1.4 copy-done
  8.6 1.0 convolution_bitcast_fusion
  9.6 6.7 %fusion.22 = f32[32,2048]{1,0:T(8,128)} fusion(bf16[3,2048,2048]{2,1,0:T(8,128)(2,1)} %param.5, f32[3,32,2048]{2,1,0:T(8,128)S(1)} %convolution_bitcast_fusion), kind=kOutput, calls=%fused_computation.22 | convolution fusion | flops 268435456 | bytes 8781824 | tf_op jit(solution)/shard_map/lm,im->li/dot_general | solution.py:18
  16.3 0.0 all-reduce.13.cloned.1.call-start
  16.4 34.8 %all-reduce.11.cloned.1.call-done = f32[32,2048]{1,0:T(8,128)} async-done(((f32[32,2048]{1,0:T(8,128)}), f32[32,2048]{1,0:T(8,128)}) %all-reduce.11.cloned.1.call-update) | async-done | bytes 262160 | tf_op jit(solution)/shard_map/psum | solution.py:21
  51.1 6.8 %fusion.14 = f32[32,2048]{1,0:T(8,128)} fusion(bf16[3,2048,2048]{2,1,0:T(8,128)(2,1)} %param.4, f32[32,2048]{1,0:T(8,128)} %all-reduce.11.cloned.1.call-done), kind=kOutput, calls=%fused_computation.14 | convolution fusion | flops 268500992 | bytes 8912896 | tf_op jit(solution)/shard_map/lj,ij->li/dot_general | solution.py:36
  58.0 0.0 all-reduce.15.cloned.1.call-start
  58.0 35.4 %all-reduce.13.cloned.1.call-done = f32[32,2048]{1,0:T(8,128)} async-done(((f32[32,2048]{1,0:T(8,128)}), f32[32,2048]{1,0:T(8,128)}) %all-reduce.13.cloned.1.call-update) | async-done | bytes 262160 | tf_op jit(solution)/shard_map/psum | solution.py:14
  93.4 6.8 %fusion.10 = f32[32,2048]{1,0:T(8,128)} fusion(bf16[3,2048,2048]{2,1,0:T(8,128)(2,1)} %param.5, f32[32,2048]{1,0:T(8,128)} %all-reduce.13.cloned.1.call-done, f32[3,32,2048]{2,1,0:T(8,128)S(1)} %convolution_bitcast_fusion), kind=kOutput, calls=%fused_computation.10 | convolution fusion | flops 268566528 | bytes 9175040 | tf_op jit(solution)/shard_map/lm,im->li/dot_general | solution.py:18
  100.3 31.8 %all-reduce.15.cloned.1.call-done = f32[32,2048]{1,0:T(8,128)} async-done(((f32[32,2048]{1,0:T(8,128)}), f32[32,2048]{1,0:T(8,128)}) %all-reduce.15.cloned.1.call-update) | async-done | bytes 262160 | tf_op jit(solution)/shard_map/psum | solution.py:21
  132.1 6.1 %fusion.6 = f32[32,2048]{1,0:T(8,128)S(1)} fusion(bf16[3,2048,2048]{2,1,0:T(8,128)(2,1)} %param.4, f32[32,2048]{1,0:T(8,128)} %all-reduce.15.cloned.1.call-done), kind=kOutput, calls=%fused_computation.6 | convolution fusion | flops 268500992 | bytes 8912896 | tf_op jit(solution)/shard_map/lj,ij->li/dot_general | solution.py:36
  138.2 6.7 %fusion.39 = f32[32,2048]{1,0:T(8,128)} fusion(f32[32,2048]{1,0:T(8,128)S(1)} %fusion.6, bf16[3,2048,2048]{2,1,0:T(8,128)(2,1)} %param.4, f32[32,2048]{1,0:T(8,128)S(1)} %copy-done.1), kind=kOutput, calls=%fused_computation.38 | convolution fusion | flops 268566528 | bytes 9175040 | tf_op jit(solution)/shard_map/lj,ij->li/dot_general | solution.py:36
  144.9 0.2 all-reduce.19.cloned.1.call-start
  145.1 35.3 %all-reduce.17.cloned.1.call-done = f32[32,2048]{1,0:T(8,128)} async-done(((f32[32,2048]{1,0:T(8,128)}), f32[32,2048]{1,0:T(8,128)}) %all-reduce.17.cloned.1.call-update) | async-done | bytes 262160 | tf_op jit(solution)/shard_map/psum | solution.py:14
  180.4 6.8 %fusion.2 = f32[32,2048]{1,0:T(8,128)} fusion(bf16[3,2048,2048]{2,1,0:T(8,128)(2,1)} %param.5, f32[32,2048]{1,0:T(8,128)} %all-reduce.17.cloned.1.call-done, f32[3,32,2048]{2,1,0:T(8,128)S(1)} %convolution_bitcast_fusion), kind=kOutput, calls=%fused_computation.2 | convolution fusion | flops 268566528 | bytes 9175040 | tf_op jit(solution)/shard_map/lm,im->li/dot_general | solution.py:18
  187.2 31.8 %all-reduce.19.cloned.1.call-done = f32[32,2048]{1,0:T(8,128)} async-done(((f32[32,2048]{1,0:T(8,128)}), f32[32,2048]{1,0:T(8,128)}) %all-reduce.19.cloned.1.call-update) | async-done | bytes 262160 | tf_op jit(solution)/shard_map/psum | solution.py:21
  219.0 5.7 %fusion = f32[32,2048]{1,0:T(8,128)} fusion(bf16[3,2048,2048]{2,1,0:T(8,128)(2,1)} %param.5, f32[32,2048]{1,0:T(8,128)} %all-reduce.19.cloned.1.call-done), kind=kOutput, calls=%fused_computation | convolution fusion | flops 268500992 | bytes 8912896 | tf_op jit(solution)/shard_map/li,im->lm/dot_general | solution.py:29
  224.8 35.4 %all-reduce.21.cloned.1.call-done = f32[32,2048]{1,0:T(8,128)} async-done(((f32[32,2048]{1,0:T(8,128)}), f32[32,2048]{1,0:T(8,128)}) %all-reduce.21.cloned.1.call-update) | async-done | bytes 262160 | tf_op jit(solution)/shard_map/psum | solution.py:32
  260.3 5.7 %fusion.4 = f32[32,2048]{1,0:T(8,128)} fusion(bf16[3,2048,2048]{2,1,0:T(8,128)(2,1)} %param.4, f32[32,2048]{1,0:T(8,128)} %all-reduce.21.cloned.1.call-done), kind=kOutput, calls=%fused_computation.4 | convolution fusion | flops 268500992 | bytes 8912896 | tf_op jit(solution)/shard_map/li,ij->lj/dot_general | solution.py:40
  266.0 0.0 all-reduce.25.cloned.1.call-start
  266.1 31.8 %all-reduce.23.cloned.1.call-done = f32[32,2048]{1,0:T(8,128)} async-done(((f32[32,2048]{1,0:T(8,128)}), f32[32,2048]{1,0:T(8,128)}) %all-reduce.23.cloned.1.call-update) | async-done | bytes 262160 | tf_op jit(solution)/shard_map/psum | solution.py:25
  297.9 5.7 %fusion.8 = f32[32,2048]{1,0:T(8,128)} fusion(bf16[3,2048,2048]{2,1,0:T(8,128)(2,1)} %param.5, f32[32,2048]{1,0:T(8,128)S(1)} %copy-done.2, f32[32,2048]{1,0:T(8,128)} %all-reduce.23.cloned.1.call-done), kind=kOutput, calls=%fused_computation.8 | convolution fusion | flops 268566528 | bytes 9175040 | tf_op jit(solution)/shard_map/li,im->lm/dot_general | solution.py:29
  303.6 0.0 all-reduce.27.cloned.1.call-start
  303.7 35.4 %all-reduce.25.cloned.1.call-done = f32[32,2048]{1,0:T(8,128)} async-done(((f32[32,2048]{1,0:T(8,128)}), f32[32,2048]{1,0:T(8,128)}) %all-reduce.25.cloned.1.call-update) | async-done | bytes 262160 | tf_op jit(solution)/shard_map/psum | solution.py:32
  339.1 5.0 %fusion.12 = f32[32,2048]{1,0:T(8,128)S(1)} fusion(bf16[3,2048,2048]{2,1,0:T(8,128)(2,1)} %param.4, f32[32,2048]{1,0:T(8,128)} %all-reduce.25.cloned.1.call-done), kind=kOutput, calls=%fused_computation.12 | convolution fusion | flops 268500992 | bytes 8912896 | tf_op jit(solution)/shard_map/li,ij->lj/dot_general | solution.py:40
  344.2 5.7 %fusion.42 = f32[32,2048]{1,0:T(8,128)} fusion(f32[32,2048]{1,0:T(8,128)S(1)} %fusion.12, bf16[3,2048,2048]{2,1,0:T(8,128)(2,1)} %param.4, f32[32,2048]{1,0:T(8,128)S(1)} %copy-done.3), kind=kOutput, calls=%fused_computation.39 | convolution fusion | flops 268566528 | bytes 9175040 | tf_op jit(solution)/shard_map/li,ij->lj/dot_general | solution.py:40
  349.9 0.0 all-reduce.29.cloned.1.call-start
  349.9 31.8 %all-reduce.27.cloned.1.call-done = f32[32,2048]{1,0:T(8,128)} async-done(((f32[32,2048]{1,0:T(8,128)}), f32[32,2048]{1,0:T(8,128)}) %all-reduce.27.cloned.1.call-update) | async-done | bytes 262160 | tf_op jit(solution)/shard_map/psum | solution.py:25
  381.7 5.7 %fusion.36 = f32[1,32,2048]{2,1,0:T(8,128)} fusion(bf16[3,2048,2048]{2,1,0:T(8,128)(2,1)} %param.5, f32[32,2048]{1,0:T(8,128)S(1)} %copy-done.1, f32[32,2048]{1,0:T(8,128)} %all-reduce.27.cloned.1.call-done), kind=kOutput, calls=%fused_computation.37 | convolution fusion | flops 268566528 | bytes 9175040 | tf_op jit(solution)/shard_map/li,im->lm/dot_general | solution.py:29
  387.5 0.9 pad_maximum_fusion.1
  388.4 34.5 %all-reduce.29.cloned.1.call-done = f32[1,32,2048]{2,1,0:T(8,128)} async-done(((f32[1,32,2048]{2,1,0:T(8,128)}), f32[1,32,2048]{2,1,0:T(8,128)}) %all-reduce.29.cloned.1.call-update) | async-done | bytes 262160 | tf_op jit(solution)/shard_map/psum | solution.py:32
  423.0 1.9 pad_maximum_fusion
  (25 shorter events, 0.4 us)
Async XLA Ops:
  7.2 1.4 copy-start
  7.2 44.0 %all-reduce.11.cloned.1.call-start = ((), (), s32[]{:S(2)}) async-start(), calls=%async_computation | async-start | bytes 524288 | tf_op jit(solution)/shard_map/psum | solution.py:21
  16.3 77.1 %all-reduce.13.cloned.1.call-start = ((), (), s32[]{:S(2)}) async-start(), calls=%async_computation.1 | async-start | bytes 524288 | tf_op jit(solution)/shard_map/psum | solution.py:14
  57.9 80.2 %copy-start.1 = (f32[32,2048]{1,0:T(8,128)S(1)}, f32[32,2048]{1,0:T(8,128)}, u32[]{:S(2)}) copy-start(f32[32,2048]{1,0:T(8,128)} %all-reduce.11.cloned.1.call-done) | copy-start | bytes 786436
  58.0 74.1 %all-reduce.15.cloned.1.call-start = ((), (), s32[]{:S(2)}) async-start(), calls=%async_computation.2 | async-start | bytes 524288 | tf_op jit(solution)/shard_map/psum | solution.py:21
  100.2 80.1 %all-reduce.17.cloned.1.call-start = ((), (), s32[]{:S(2)}) async-start(), calls=%async_computation.3 | async-start | bytes 524288 | tf_op jit(solution)/shard_map/psum | solution.py:14
  144.9 74.1 %all-reduce.19.cloned.1.call-start = ((), (), s32[]{:S(2)}) async-start(), calls=%async_computation.4 | async-start | bytes 524288 | tf_op jit(solution)/shard_map/psum | solution.py:21
  187.2 110.7 %copy-start.2 = (f32[32,2048]{1,0:T(8,128)S(1)}, f32[32,2048]{1,0:T(8,128)}, u32[]{:S(2)}) copy-start(f32[32,2048]{1,0:T(8,128)} %all-reduce.15.cloned.1.call-done) | copy-start | bytes 786436
  187.2 73.1 %all-reduce.21.cloned.1.call-start = ((), (), s32[]{:S(2)}) async-start(), calls=%async_computation.5 | async-start | bytes 524288 | tf_op jit(solution)/shard_map/psum | solution.py:32
  224.8 73.1 %all-reduce.23.cloned.1.call-start = ((), (), s32[]{:S(2)}) async-start(), calls=%async_computation.6 | async-start | bytes 524288 | tf_op jit(solution)/shard_map/psum | solution.py:25
  266.0 78.1 %copy-start.3 = (f32[32,2048]{1,0:T(8,128)S(1)}, f32[32,2048]{1,0:T(8,128)}, u32[]{:S(2)}) copy-start(f32[32,2048]{1,0:T(8,128)} %all-reduce.21.cloned.1.call-done) | copy-start | bytes 786436
  266.0 73.1 %all-reduce.25.cloned.1.call-start = ((), (), s32[]{:S(2)}) async-start(), calls=%async_computation.7 | async-start | bytes 524288 | tf_op jit(solution)/shard_map/psum | solution.py:32
  303.6 78.1 %all-reduce.27.cloned.1.call-start = ((), (), s32[]{:S(2)}) async-start(), calls=%async_computation.8 | async-start | bytes 524288 | tf_op jit(solution)/shard_map/psum | solution.py:25
  344.2 43.3 %copy-start.4 = (f32[32,2048]{1,0:T(8,128)S(1)}, f32[32,2048]{1,0:T(8,128)}, u32[]{:S(2)}) copy-start(f32[32,2048]{1,0:T(8,128)} %all-reduce.19.cloned.1.call-done) | copy-start | bytes 786436
  344.2 78.8 %copy-start.5 = (f32[32,2048]{1,0:T(8,128)S(1)}, f32[32,2048]{1,0:T(8,128)}, u32[]{:S(2)}) copy-start(f32[32,2048]{1,0:T(8,128)} %all-reduce.25.cloned.1.call-done) | copy-start | bytes 786436
  349.9 73.1 %all-reduce.29.cloned.1.call-start = ((), (), s32[]{:S(2)}) async-start(), calls=%async_computation.9 | async-start | bytes 524288 | tf_op jit(solution)/shard_map/psum | solution.py:32
Sparse Core Ops, SparseCore 0:
  16.4 34.6 all-reduce.10
  58.1 35.3 all-reduce.12
  100.4 31.6 all-reduce.14
  145.0 35.3 all-reduce.16
  187.3 31.6 all-reduce.18
  224.9 35.3 all-reduce.20
  266.1 31.6 all-reduce.22
  303.8 35.3 all-reduce.24
  350.0 31.6 all-reduce.26
  387.6 35.2 all-reduce.28
where the time goes:
time: 432 us
  waiting for transfers between devices  338 us (78%)
  matrix products  74.4 us (17%)
  between operations  14.2 us (3%)
    psum x3, waiting for transfers between devices, backward_diag(): return lax.psum(partial_value, 'rows')  105 us
    psum x3, waiting for transfers between devices, forward_diag(): return lax.psum(partial_value, 'cols')  98.4 us
    psum x2, waiting for transfers between devices, forward_couple(): return lax.psum(partial_value, 'rows')  70.7 us
    psum x2, waiting for transfers between devices, backward_couple(): return lax.psum(partial_value, 'cols')  63.6 us
    dot_general x3, matrix products, forward_diag(): jnp.einsum('lm,im->li', resid.astype(jnp.bfloat16), tile, preferred_eleme...  20.2 us
    dot_general x3, matrix products, lower_term(): jnp.einsum('lj,ij->li', vector_bf, block, preferred_element_type=jnp.floa...  19.5 us
    dot_general x3, matrix products, backward_diag(): jnp.einsum('li,im->lm', resid.astype(jnp.bfloat16), tile, preferred_eleme...  17.2 us
    dot_general x3, matrix products, upper_term(): jnp.einsum('li,ij->lj', vector_bf, block, preferred_element_type=jnp.floa...  16.4 us
  transfers between devices with their start and end apart: 10, of which 10 were waited for; matrix products, arithmetic and copies ran while one was open for 0% of the time, Pallas kernels for 0%

commit v1 on v0

v1 whole, which is shorter than its diff:
```python
import jax
import jax.numpy as jnp
from jax import lax
from jax.sharding import PartitionSpec as P

LEVELS = 3
DIRECT_MAX = 8


def pair_index(high, low):
    return high * (high - 1) // 2 + low


def swap(value, axis, size, step):
    return lax.ppermute(value, axis, [(i, i ^ step) for i in range(size)])


def sum_direct(value, axis, size):
    me = lax.axis_index(axis)
    width = value.shape[1] // size

    def chunk(step):
        return lax.dynamic_slice_in_dim(value, (me ^ step) * width, width, axis=1)

    got = [swap(chunk(step), axis, size, step) for step in range(1, size)]
    total = chunk(0)
    for piece in got:
        total = total + piece
    out = lax.dynamic_update_slice_in_dim(jnp.zeros_like(value), total, me * width, axis=1)
    for step in range(1, size):
        out = lax.dynamic_update_slice_in_dim(
            out, swap(total, axis, size, step), (me ^ step) * width, axis=1
        )
    return out


def sum_halves(value, axis, size):
    if size == 1:
        return value
    me = lax.axis_index(axis)
    odd = me % 2 == 1
    half = value.shape[1] // 2
    low, high = value[:, :half], value[:, half:]
    kept = jnp.where(odd, high, low) + swap(jnp.where(odd, low, high), axis, size, 1)
    step = 2
    while step < size:
        kept = kept + swap(kept, axis, size, step)
        step *= 2
    other = swap(kept, axis, size, 1)
    return jnp.concatenate([jnp.where(odd, other, kept), jnp.where(odd, kept, other)], axis=1)


def power_of_two(size):
    return size & (size - 1) == 0


def lower_term(vector_bf, block):
    return jnp.einsum("lj,ij->li", vector_bf, block, preferred_element_type=jnp.float32)


def upper_term(vector_bf, block):
    return jnp.einsum("li,ij->lj", vector_bf, block, preferred_element_type=jnp.float32)


def body(coupling, diag_inverse, loads, axle_index, *, n_rows, n_cols):
    def over_rows(value):
        if power_of_two(n_rows) and n_rows <= DIRECT_MAX:
            return sum_direct(value, "rows", n_rows)
        return lax.psum(value, "rows")

    def over_cols(value):
        if power_of_two(n_cols):
            return sum_halves(value, "cols", n_cols)
        return lax.psum(value, "cols")

    positions = loads.shape[1]
    selector = (axle_index[:, None] == jnp.arange(positions, dtype=jnp.int32)[None, :]).astype(
        jnp.bfloat16
    )
    rhs = jnp.einsum("lp,kpc->klc", selector, loads, preferred_element_type=jnp.float32)
    solved = []
    solved_bf = []
    for level in range(LEVELS):
        resid = rhs[level]
        if level > 0:
            partial_value = lower_term(solved_bf[0], coupling[pair_index(level, 0)])
            for lower in range(1, level):
                partial_value = partial_value + lower_term(
                    solved_bf[lower], coupling[pair_index(level, lower)]
                )
            resid = resid - over_rows(partial_value)
        value = over_cols(lower_term(resid.astype(jnp.bfloat16), diag_inverse[level]))
        solved.append(value)
        solved_bf.append(value.astype(jnp.bfloat16))
    answers = [None] * LEVELS
    answers_bf = [None] * LEVELS
    for level in range(LEVELS - 1, -1, -1):
        resid = solved[level]
        if level < LEVELS - 1:
            partial_value = upper_term(
                answers_bf[LEVELS - 1], coupling[pair_index(LEVELS - 1, level)]
            )
            for upper in range(level + 1, LEVELS - 1):
                partial_value = partial_value + upper_term(
                    answers_bf[upper], coupling[pair_index(upper, level)]
                )
            resid = resid - over_cols(partial_value)
        value = over_rows(upper_term(resid.astype(jnp.bfloat16), diag_inverse[level]))
        answers[level] = value
        answers_bf[level] = value.astype(jnp.bfloat16)
    return jnp.stack(answers), jnp.stack(solved)


def solution(mesh):
    placed = (
        P("groups", "cols", "rows"),
        P("groups", "rows", "cols"),
        P("groups", None, "cols"),
        P("groups"),
    )

    def local(coupling, diag_inverse, loads, axle_index):
        return body(
            coupling,
            diag_inverse,
            loads,
            axle_index,
            n_rows=mesh.shape["rows"],
            n_cols=mesh.shape["cols"],
        )

    return jax.shard_map(
        local,
        mesh=mesh,
        in_specs=placed,
        out_specs=(P("groups", None, "cols"), P("groups", None, "rows")),
        check_vma=False,
    )
```

time: 432 us -> 199 us (0.46)
  waiting for transfers between devices: 338 us -> 80.8 us
  starting transfers between devices: 0.6 us -> 54.8 us
  matrix products: 74.4 us -> 57 us
  between operations: 14.2 us -> 1.22 us
    psum x10 -> x0, waiting for transfers between devices: 338 us -> none  [the longest x3 105 us: backward_diag(): return lax.psum(partial_value, 'rows')]
    ppermute x0 -> x45, waiting for transfers between devices: none -> 80.8 us  [swap(): return lax.ppermute(value, axis, [(i, i ^ step) for i in range(size)])]
    ppermute x0 -> x45, starting transfers between devices: none -> 54.8 us  [swap(): return lax.ppermute(value, axis, [(i, i ^ step) for i in range(size)])]
    dot_general x6 -> x0, matrix products: 37.4 us -> none  [the longest x3 20.2 us: forward_diag(): jnp.einsum('lm,im->li', resid.astype(jnp.bfloat16), tile, preferred_eleme...]
    dot_general x3 -> x6, matrix products: 19.5 us -> 36.4 us  [lower_term(): jnp.einsum('lj,ij->li', vector_bf, block, preferred_element_type=jnp.floa...]
    dot_general x3 -> x6, matrix products: 16.4 us -> 19.6 us  [upper_term(): jnp.einsum('li,ij->lj', vector_bf, block, preferred_element_type=jnp.floa...]
  transfers between devices with their start and end apart: 10 -> 45, of which waited for: 10 -> 30; matrix products, arithmetic and copies ran while one was open for 0% -> 1% of each run, Pallas kernels for 0% -> 0%
where the time goes in v1:
time: 199 us; the launch traced here: 198 us
  waiting for transfers between devices  80.8 us (41%)
  matrix products  57 us (29%)
  starting transfers between devices  54.8 us (28%)
  other arithmetic  2.51 us (1%)
    ppermute x45, waiting for transfers between devices, swap(): return lax.ppermute(value, axis, [(i, i ^ step) for i in range(size)])  80.8 us
    ppermute x45, starting transfers between devices, swap(): return lax.ppermute(value, axis, [(i, i ^ step) for i in range(size)])  54.8 us
    dot_general x6, matrix products, lower_term(): jnp.einsum('lj,ij->li', vector_bf, block, preferred_element_type=jnp.floa...  36.4 us
    dot_general x6, matrix products, upper_term(): jnp.einsum('li,ij->lj', vector_bf, block, preferred_element_type=jnp.floa...  19.6 us
  transfers between devices with their start and end apart: 45, of which 30 were waited for; matrix products, arithmetic and copies ran while one was open for 1% of the time, Pallas kernels for 0%

profile of v1, /device:TPU:0, one launch (start us, length us, event | category | flops | bytes accessed | tf_op | source)
XLA Modules:
  0.0 198.3 jit_solution(8563072728214858420)
XLA Ops:
  3.1 6.0 %fusion.22 = f32[32,2048]{1,0:T(8,128)S(1)} fusion(bf16[3,2048,2048]{2,1,0:T(8,128)(2,1)} %param.5, f32[3,32,2048]{2,1,0:T(8,128)S(1)} %convolution_bitcast_fusion), kind=kOutput, calls=%fused_computation.22 | convolution fusion | flops 268435456 | bytes 8781824 | tf_op jit(solution)/shard_map/lj,ij->li/dot_general | solution.py:58
  10.6 2.9 %collective-permute-start.1 = (f32[32,1024]{1,0:T(8,128)S(1)}, f32[32,1024]{1,0:T(8,128)S(1)}, u32[]{:S(2)}, u32[]{:S(2)}) collective-permute-start(f32[32,1024]{1,0:T(8,128)S(1)} %select_add_fusion.4), channel_id=1, source_target_pairs={{0,2},{1,3},{2,0},{3,1},{4,6},{5,7},{6,4},{7,5},{8,10},{9,11},{10,... | collective-permute-start | bytes 393224 | tf_op jit(solution)/shard_map/ppermute | solution.py:15
  13.5 3.8 %collective-permute-done.1 = f32[32,1024]{1,0:T(8,128)S(1)} collective-permute-done((f32[32,1024]{1,0:T(8,128)S(1)}, f32[32,1024]{1,0:T(8,128)S(1)}, u32[]{:S(2)}, u32[]{:S(2)}) %collective-permute-start.1) | collective-permute-done | bytes 131104 | tf_op jit(solution)/shard_map/ppermute | solution.py:15
  18.8 6.0 %fusion.14 = f32[32,2048]{1,0:T(8,128)S(1)} fusion(bf16[3,2048,2048]{2,1,0:T(8,128)(2,1)} %param.4, f32[32,1024]{1,0:T(8,128)S(1)} %get-tuple-element.36, f32[32,1024]{1,0:T(8,128)S(1)} %get-tuple-element.35), kind=kOutput, calls=%fused_computation.14 | convolution fusion | flops 268697600 | bytes 8912896 | tf_op jit(solution)/shard_map/lj,ij->li/dot_general | solution.py:58
  26.7 2.6 %collective-permute-start.4 = (f32[32,512]{1,0:T(8,128)S(1)}, f32[32,512]{1,0:T(8,128)S(1)}, u32[]{:S(2)}, u32[]{:S(2)}) collective-permute-start(f32[32,512]{1,0:T(8,128)S(1)} %get-tuple-element.34), channel_id=1, source_target_pairs={{0,8},{4,12},{8,0},{12,4},{1,9},{5,13},{9,1},{13,5},{2,10},{6,14},... | collective-permute-start | bytes 196616 | tf_op jit(solution)/shard_map/ppermute | solution.py:15
  29.3 4.9 %collective-permute-done.4 = f32[32,512]{1,0:T(8,128)S(1)} collective-permute-done((f32[32,512]{1,0:T(8,128)S(1)}, f32[32,512]{1,0:T(8,128)S(1)}, u32[]{:S(2)}, u32[]{:S(2)}) %collective-permute-start.4) | collective-permute-done | bytes 65568 | tf_op jit(solution)/shard_map/ppermute | solution.py:15
  40.1 2.6 %collective-permute-done.7 = f32[32,512]{1,0:T(8,128)S(1)} collective-permute-done((f32[32,512]{1,0:T(8,128)S(1)}, f32[32,512]{1,0:T(8,128)S(1)}, u32[]{:S(2)}, u32[]{:S(2)}) %collective-permute-start.7) | collective-permute-done | bytes 65568 | tf_op jit(solution)/shard_map/ppermute | solution.py:15
  44.2 6.1 %fusion.10 = f32[32,2048]{1,0:T(8,128)S(1)} fusion(bf16[3,2048,2048]{2,1,0:T(8,128)(2,1)} %param.5, f32[32,2048]{1,0:T(8,128)S(1)} %constant_dynamic-update-slice_fusion.12, f32[3,32,2048]{2,1,0:T(8,128)S(1)} %convolution_bitcast_fusion), kind=kOutput, calls=%fused_computation.10 | convolution fusion | flops 268566528 | bytes 9175040 | tf_op jit(solution)/shard_map/lj,ij->li/dot_general | solution.py:58
  53.4 4.1 %collective-permute-done.10 = f32[32,1024]{1,0:T(8,128)S(1)} collective-permute-done((f32[32,1024]{1,0:T(8,128)S(1)}, f32[32,1024]{1,0:T(8,128)S(1)}, u32[]{:S(2)}, u32[]{:S(2)}) %collective-permute-start.10) | collective-permute-done | bytes 131104 | tf_op jit(solution)/shard_map/ppermute | solution.py:15
  58.9 6.1 %fusion.6 = f32[32,2048]{1,0:T(8,128)S(1)} fusion(bf16[3,2048,2048]{2,1,0:T(8,128)(2,1)} %param.4, f32[32,1024]{1,0:T(8,128)S(1)} %get-tuple-element.31, f32[32,1024]{1,0:T(8,128)S(1)} %get-tuple-element.30), kind=kOutput, calls=%fused_computation.6 | convolution fusion | flops 268697600 | bytes 8912896 | tf_op jit(solution)/shard_map/lj,ij->li/dot_general | solution.py:58
  65.0 6.1 %fusion.36 = f32[32,2048]{1,0:T(8,128)S(1)} fusion(f32[32,2048]{1,0:T(8,128)S(1)} %fusion.6, bf16[3,2048,2048]{2,1,0:T(8,128)(2,1)} %param.4, f32[32,1024]{1,0:T(8,128)S(1)} %get-tuple-element.36, f32[32,1024]{1,0:T(8,128)S(1)} %get-tuple-element.35), kind=kOutput, calls=%fused_computation.37 | convolution fusion | flops 268763136 | bytes 9175040 | tf_op jit(solution)/shard_map/lj,ij->li/dot_general | solution.py:58
  71.3 2.5 %collective-permute-start.13 = (f32[32,512]{1,0:T(8,128)S(1)}, f32[32,512]{1,0:T(8,128)S(1)}, u32[]{:S(2)}, u32[]{:S(2)}) collective-permute-start(f32[32,512]{1,0:T(8,128)S(1)} %get-tuple-element.29), channel_id=1, source_target_pairs={{0,8},{4,12},{8,0},{12,4},{1,9},{5,13},{9,1},{13,5},{2,10},{6,14},... | collective-permute-start | bytes 196616 | tf_op jit(solution)/shard_map/ppermute | solution.py:15
  76.5 2.6 %collective-permute-done.13 = f32[32,512]{1,0:T(8,128)S(1)} collective-permute-done((f32[32,512]{1,0:T(8,128)S(1)}, f32[32,512]{1,0:T(8,128)S(1)}, u32[]{:S(2)}, u32[]{:S(2)}) %collective-permute-start.13) | collective-permute-done | bytes 65568 | tf_op jit(solution)/shard_map/ppermute | solution.py:15
  84.5 4.6 %collective-permute-done.16 = f32[32,512]{1,0:T(8,128)S(1)} collective-permute-done((f32[32,512]{1,0:T(8,128)S(1)}, f32[32,512]{1,0:T(8,128)S(1)}, u32[]{:S(2)}, u32[]{:S(2)}) %collective-permute-start.16) | collective-permute-done | bytes 65568 | tf_op jit(solution)/shard_map/ppermute | solution.py:15
  89.1 6.1 %fusion.2 = f32[32,2048]{1,0:T(8,128)S(1)} fusion(bf16[3,2048,2048]{2,1,0:T(8,128)(2,1)} %param.5, f32[32,2048]{1,0:T(8,128)S(1)} %constant_dynamic-update-slice_fusion.8, f32[3,32,2048]{2,1,0:T(8,128)S(1)} %convolution_bitcast_fusion), kind=kOutput, calls=%fused_computation.2 | convolution fusion | flops 268566528 | bytes 9175040 | tf_op jit(solution)/shard_map/lj,ij->li/dot_general | solution.py:58
  98.3 4.1 %collective-permute-done.19 = f32[32,1024]{1,0:T(8,128)S(1)} collective-permute-done((f32[32,1024]{1,0:T(8,128)S(1)}, f32[32,1024]{1,0:T(8,128)S(1)}, u32[]{:S(2)}, u32[]{:S(2)}) %collective-permute-start.19) | collective-permute-done | bytes 131104 | tf_op jit(solution)/shard_map/ppermute | solution.py:15
  103.8 5.1 %fusion = f32[32,2048]{1,0:T(8,128)S(1)} fusion(bf16[3,2048,2048]{2,1,0:T(8,128)(2,1)} %param.5, f32[32,1024]{1,0:T(8,128)S(1)} %get-tuple-element.26, f32[32,1024]{1,0:T(8,128)S(1)} %get-tuple-element.25), kind=kOutput, calls=%fused_computation | convolution fusion | flops 268697600 | bytes 8912896 | tf_op jit(solution)/shard_map/li,ij->lj/dot_general | solution.py:62
  111.1 2.3 %collective-permute-start.23 = (f32[32,512]{1,0:T(8,128)S(1)}, f32[32,512]{1,0:T(8,128)S(1)}, u32[]{:S(2)}, u32[]{:S(2)}) collective-permute-start(f32[32,512]{1,0:T(8,128)S(1)} %get-tuple-element.23), channel_id=1, source_target_pairs={{0,12},{4,8},{8,4},{12,0},{1,13},{5,9},{9,5},{13,1},{2,14},{6,10},... | collective-permute-start | bytes 196616 | tf_op jit(solution)/shard_map/ppermute | solution.py:15
  113.4 4.9 %collective-permute-done.22 = f32[32,512]{1,0:T(8,128)S(1)} collective-permute-done((f32[32,512]{1,0:T(8,128)S(1)}, f32[32,512]{1,0:T(8,128)S(1)}, u32[]{:S(2)}, u32[]{:S(2)}) %collective-permute-start.22) | collective-permute-done | bytes 65568 | tf_op jit(solution)/shard_map/ppermute | solution.py:15
  120.6 2.1 %collective-permute-start.26 = (f32[32,512]{1,0:T(8,128)S(1)}, f32[32,512]{1,0:T(8,128)S(1)}, u32[]{:S(2)}, u32[]{:S(2)}) collective-permute-start(f32[32,512]{1,0:T(8,128)S(1)} %get-tuple-element.7), channel_id=1, source_target_pairs={{0,12},{4,8},{8,4},{12,0},{1,13},{5,9},{9,5},{13,1},{2,14},{6,10},... | collective-permute-start | bytes 196616 | tf_op jit(solution)/shard_map/ppermute | solution.py:15
  122.7 4.8 %collective-permute-done.25 = f32[32,512]{1,0:T(8,128)S(1)} collective-permute-done((f32[32,512]{1,0:T(8,128)S(1)}, f32[32,512]{1,0:T(8,128)S(1)}, u32[]{:S(2)}, u32[]{:S(2)}) %collective-permute-start.25) | collective-permute-done | bytes 65568 | tf_op jit(solution)/shard_map/ppermute | solution.py:15
  132.2 4.1 %collective-permute-done.28 = f32[32,1024]{1,0:T(8,128)S(1)} collective-permute-done((f32[32,1024]{1,0:T(8,128)S(1)}, f32[32,1024]{1,0:T(8,128)S(1)}, u32[]{:S(2)}, u32[]{:S(2)}) %collective-permute-start.28) | collective-permute-done | bytes 131104 | tf_op jit(solution)/shard_map/ppermute | solution.py:15
  137.7 4.9 %fusion.8 = f32[32,2048]{1,0:T(8,128)S(1)} fusion(bf16[3,2048,2048]{2,1,0:T(8,128)(2,1)} %param.5, f32[32,1024]{1,0:T(8,128)S(1)} %get-tuple-element.21, f32[32,1024]{1,0:T(8,128)S(1)} %get-tuple-element.20, f32[32,1024]{1,0:T(8,128)S(1)} %get-tuple-element.31, f32[32,1024]{1,0:T(8,128)S(1)} %get-tuple-element.30), kind=kOutput, calls=%fused_computation.8 | convolution fusion | flops 268697600 | bytes 9175040 | tf_op jit(solution)/shard_map/li,ij->lj/dot_general | solution.py:62
  144.8 2.4 %collective-permute-start.32 = (f32[32,512]{1,0:T(8,128)S(1)}, f32[32,512]{1,0:T(8,128)S(1)}, u32[]{:S(2)}, u32[]{:S(2)}) collective-permute-start(f32[32,512]{1,0:T(8,128)S(1)} %get-tuple-element.18), channel_id=1, source_target_pairs={{0,12},{4,8},{8,4},{12,0},{1,13},{5,9},{9,5},{13,1},{2,14},{6,10},... | collective-permute-start | bytes 196616 | tf_op jit(solution)/shard_map/ppermute | solution.py:15
  147.2 4.8 %collective-permute-done.31 = f32[32,512]{1,0:T(8,128)S(1)} collective-permute-done((f32[32,512]{1,0:T(8,128)S(1)}, f32[32,512]{1,0:T(8,128)S(1)}, u32[]{:S(2)}, u32[]{:S(2)}) %collective-permute-start.31) | collective-permute-done | bytes 65568 | tf_op jit(solution)/shard_map/ppermute | solution.py:15
  154.4 2.1 %collective-permute-start.35 = (f32[32,512]{1,0:T(8,128)S(1)}, f32[32,512]{1,0:T(8,128)S(1)}, u32[]{:S(2)}, u32[]{:S(2)}) collective-permute-start(f32[32,512]{1,0:T(8,128)S(1)} %get-tuple-element.5), channel_id=1, source_target_pairs={{0,12},{4,8},{8,4},{12,0},{1,13},{5,9},{9,5},{13,1},{2,14},{6,10},... | collective-permute-start | bytes 196616 | tf_op jit(solution)/shard_map/ppermute | solution.py:15
  156.5 4.8 %collective-permute-done.34 = f32[32,512]{1,0:T(8,128)S(1)} collective-permute-done((f32[32,512]{1,0:T(8,128)S(1)}, f32[32,512]{1,0:T(8,128)S(1)}, u32[]{:S(2)}, u32[]{:S(2)}) %collective-permute-start.34) | collective-permute-done | bytes 65568 | tf_op jit(solution)/shard_map/ppermute | solution.py:15
  167.5 4.1 %collective-permute-done.37 = f32[32,1024]{1,0:T(8,128)S(1)} collective-permute-done((f32[32,1024]{1,0:T(8,128)S(1)}, f32[32,1024]{1,0:T(8,128)S(1)}, u32[]{:S(2)}, u32[]{:S(2)}) %collective-permute-start.37) | collective-permute-done | bytes 131104 | tf_op jit(solution)/shard_map/ppermute | solution.py:15
  173.0 4.9 %fusion.20 = f32[32,2048]{1,0:T(8,128)S(1)} fusion(bf16[3,2048,2048]{2,1,0:T(8,128)(2,1)} %param.5, f32[32,1024]{1,0:T(8,128)S(1)} %get-tuple-element.16, f32[32,1024]{1,0:T(8,128)S(1)} %get-tuple-element.15, f32[32,1024]{1,0:T(8,128)S(1)} %get-tuple-element.36, f32[32,1024]{1,0:T(8,128)S(1)} %get-tuple-element.35), kind=kOutput, calls=%fused_computation.20 | convolution fusion | flops 268697600 | bytes 9175040 | tf_op jit(solution)/shard_map/li,ij->lj/dot_general | solution.py:62
  180.1 2.4 %collective-permute-start.41 = (f32[32,512]{1,0:T(8,128)S(1)}, f32[32,512]{1,0:T(8,128)S(1)}, u32[]{:S(2)}, u32[]{:S(2)}) collective-permute-start(f32[32,512]{1,0:T(8,128)S(1)} %get-tuple-element.13), channel_id=1, source_target_pairs={{0,12},{4,8},{8,4},{12,0},{1,13},{5,9},{9,5},{13,1},{2,14},{6,10},... | collective-permute-start | bytes 196616 | tf_op jit(solution)/shard_map/ppermute | solution.py:15
  182.5 4.8 %collective-permute-done.40 = f32[32,512]{1,0:T(8,128)S(1)} collective-permute-done((f32[32,512]{1,0:T(8,128)S(1)}, f32[32,512]{1,0:T(8,128)S(1)}, u32[]{:S(2)}, u32[]{:S(2)}) %collective-permute-start.40) | collective-permute-done | bytes 65568 | tf_op jit(solution)/shard_map/ppermute | solution.py:15
  192.7 4.5 %collective-permute-done.43 = f32[32,512]{1,0:T(8,128)S(1)} collective-permute-done((f32[32,512]{1,0:T(8,128)S(1)}, f32[32,512]{1,0:T(8,128)S(1)}, u32[]{:S(2)}, u32[]{:S(2)}) %collective-permute-start.43) | collective-permute-done | bytes 65568 | tf_op jit(solution)/shard_map/ppermute | solution.py:15
  (142 shorter events, 63.1 us)
Async XLA Ops:
  10.6 6.7 %collective-permute-start.1 = (f32[32,1024]{1,0:T(8,128)S(1)}, f32[32,1024]{1,0:T(8,128)S(1)}, u32[]{:S(2)}, u32[]{:S(2)}) collective-permute-start(f32[32,1024]{1,0:T(8,128)S(1)} %select_add_fusion.4), channel_id=1, source_target_pairs={{0,2},{1,3},{2,0},{3,1},{4,6},{5,7},{6,4},{7,5},{8,10},{9,11},{10,... | collective-permute-start | bytes 393224 | tf_op jit(solution)/shard_map/ppermute | solution.py:15
  24.8 4.5 %collective-permute-start.3 = (f32[32,512]{1,0:T(8,128)S(1)}, f32[32,512]{1,0:T(8,128)S(1)}, u32[]{:S(2)}, u32[]{:S(2)}) collective-permute-start(f32[32,512]{1,0:T(8,128)S(1)} %get-tuple-element.32), channel_id=1, source_target_pairs={{0,4},{4,0},{8,12},{12,8},{1,5},{5,1},{9,13},{13,9},{2,6},{6,2},{1... | collective-permute-start | bytes 196616 | tf_op jit(solution)/shard_map/ppermute | solution.py:15
  26.7 7.5 %collective-permute-start.4 = (f32[32,512]{1,0:T(8,128)S(1)}, f32[32,512]{1,0:T(8,128)S(1)}, u32[]{:S(2)}, u32[]{:S(2)}) collective-permute-start(f32[32,512]{1,0:T(8,128)S(1)} %get-tuple-element.34), channel_id=1, source_target_pairs={{0,8},{4,12},{8,0},{12,4},{1,9},{5,13},{9,1},{13,5},{2,10},{6,14},... | collective-permute-start | bytes 196616 | tf_op jit(solution)/shard_map/ppermute | solution.py:15
  29.3 6.2 %collective-permute-start.5 = (f32[32,512]{1,0:T(8,128)S(1)}, f32[32,512]{1,0:T(8,128)S(1)}, u32[]{:S(2)}, u32[]{:S(2)}) collective-permute-start(f32[32,512]{1,0:T(8,128)S(1)} %get-tuple-element.33), channel_id=1, source_target_pairs={{0,12},{4,8},{8,4},{12,0},{1,13},{5,9},{9,5},{13,1},{2,14},{6,10},... | collective-permute-start | bytes 196616 | tf_op jit(solution)/shard_map/ppermute | solution.py:15
  35.5 4.6 %collective-permute-start.6 = (f32[32,512]{1,0:T(8,128)S(1)}, f32[32,512]{1,0:T(8,128)S(1)}, u32[]{:S(2)}, u32[]{:S(2)}) collective-permute-start(f32[32,512]{1,0:T(8,128)S(1)} %get-tuple-element.11), channel_id=1, source_target_pairs={{0,4},{4,0},{8,12},{12,8},{1,5},{5,1},{9,13},{13,9},{2,6},{6,2},{1... | collective-permute-start | bytes 196616 | tf_op jit(solution)/shard_map/ppermute | solution.py:15
  36.4 6.2 %collective-permute-start.7 = (f32[32,512]{1,0:T(8,128)S(1)}, f32[32,512]{1,0:T(8,128)S(1)}, u32[]{:S(2)}, u32[]{:S(2)}) collective-permute-start(f32[32,512]{1,0:T(8,128)S(1)} %get-tuple-element.11), channel_id=1, source_target_pairs={{0,8},{4,12},{8,0},{12,4},{1,9},{5,13},{9,1},{13,5},{2,10},{6,14},... | collective-permute-start | bytes 196616 | tf_op jit(solution)/shard_map/ppermute | solution.py:15
  38.1 6.1 %collective-permute-start.8 = (f32[32,512]{1,0:T(8,128)S(1)}, f32[32,512]{1,0:T(8,128)S(1)}, u32[]{:S(2)}, u32[]{:S(2)}) collective-permute-start(f32[32,512]{1,0:T(8,128)S(1)} %get-tuple-element.11), channel_id=1, source_target_pairs={{0,12},{4,8},{8,4},{12,0},{1,13},{5,9},{9,5},{13,1},{2,14},{6,10},... | collective-permute-start | bytes 196616 | tf_op jit(solution)/shard_map/ppermute | solution.py:15
  51.8 5.6 %collective-permute-start.10 = (f32[32,1024]{1,0:T(8,128)S(1)}, f32[32,1024]{1,0:T(8,128)S(1)}, u32[]{:S(2)}, u32[]{:S(2)}) collective-permute-start(f32[32,1024]{1,0:T(8,128)S(1)} %select_add_fusion.3), channel_id=1, source_target_pairs={{0,2},{1,3},{2,0},{3,1},{4,6},{5,7},{6,4},{7,5},{8,10},{9,11},{10,... | collective-permute-start | bytes 393224 | tf_op jit(solution)/shard_map/ppermute | solution.py:15
  71.2 5.3 %collective-permute-start.12 = (f32[32,512]{1,0:T(8,128)S(1)}, f32[32,512]{1,0:T(8,128)S(1)}, u32[]{:S(2)}, u32[]{:S(2)}) collective-permute-start(f32[32,512]{1,0:T(8,128)S(1)} %get-tuple-element.27), channel_id=1, source_target_pairs={{0,4},{4,0},{8,12},{12,8},{1,5},{5,1},{9,13},{13,9},{2,6},{6,2},{1... | collective-permute-start | bytes 196616 | tf_op jit(solution)/shard_map/ppermute | solution.py:15
  71.3 7.9 %collective-permute-start.13 = (f32[32,512]{1,0:T(8,128)S(1)}, f32[32,512]{1,0:T(8,128)S(1)}, u32[]{:S(2)}, u32[]{:S(2)}) collective-permute-start(f32[32,512]{1,0:T(8,128)S(1)} %get-tuple-element.29), channel_id=1, source_target_pairs={{0,8},{4,12},{8,0},{12,4},{1,9},{5,13},{9,1},{13,5},{2,10},{6,14},... | collective-permute-start | bytes 196616 | tf_op jit(solution)/shard_map/ppermute | solution.py:15
  73.8 6.2 %collective-permute-start.14 = (f32[32,512]{1,0:T(8,128)S(1)}, f32[32,512]{1,0:T(8,128)S(1)}, u32[]{:S(2)}, u32[]{:S(2)}) collective-permute-start(f32[32,512]{1,0:T(8,128)S(1)} %get-tuple-element.28), channel_id=1, source_target_pairs={{0,12},{4,8},{8,4},{12,0},{1,13},{5,9},{9,5},{13,1},{2,14},{6,10},... | collective-permute-start | bytes 196616 | tf_op jit(solution)/shard_map/ppermute | solution.py:15
  80.0 4.5 %collective-permute-start.15 = (f32[32,512]{1,0:T(8,128)S(1)}, f32[32,512]{1,0:T(8,128)S(1)}, u32[]{:S(2)}, u32[]{:S(2)}) collective-permute-start(f32[32,512]{1,0:T(8,128)S(1)} %get-tuple-element.9), channel_id=1, source_target_pairs={{0,4},{4,0},{8,12},{12,8},{1,5},{5,1},{9,13},{13,9},{2,6},{6,2},{1... | collective-permute-start | bytes 196616 | tf_op jit(solution)/shard_map/ppermute | solution.py:15
  81.4 7.7 %collective-permute-start.16 = (f32[32,512]{1,0:T(8,128)S(1)}, f32[32,512]{1,0:T(8,128)S(1)}, u32[]{:S(2)}, u32[]{:S(2)}) collective-permute-start(f32[32,512]{1,0:T(8,128)S(1)} %get-tuple-element.9), channel_id=1, source_target_pairs={{0,8},{4,12},{8,0},{12,4},{1,9},{5,13},{9,1},{13,5},{2,10},{6,14},... | collective-permute-start | bytes 196616 | tf_op jit(solution)/shard_map/ppermute | solution.py:15
  82.8 6.3 %collective-permute-start.17 = (f32[32,512]{1,0:T(8,128)S(1)}, f32[32,512]{1,0:T(8,128)S(1)}, u32[]{:S(2)}, u32[]{:S(2)}) collective-permute-start(f32[32,512]{1,0:T(8,128)S(1)} %get-tuple-element.9), channel_id=1, source_target_pairs={{0,12},{4,8},{8,4},{12,0},{1,13},{5,9},{9,5},{13,1},{2,14},{6,10},... | collective-permute-start | bytes 196616 | tf_op jit(solution)/shard_map/ppermute | solution.py:15
  96.7 5.6 %collective-permute-start.19 = (f32[32,1024]{1,0:T(8,128)S(1)}, f32[32,1024]{1,0:T(8,128)S(1)}, u32[]{:S(2)}, u32[]{:S(2)}) collective-permute-start(f32[32,1024]{1,0:T(8,128)S(1)} %select_add_fusion.2), channel_id=1, source_target_pairs={{0,2},{1,3},{2,0},{3,1},{4,6},{5,7},{6,4},{7,5},{8,10},{9,11},{10,... | collective-permute-start | bytes 393224 | tf_op jit(solution)/shard_map/ppermute | solution.py:15
  110.2 8.0 %collective-permute-start.22 = (f32[32,512]{1,0:T(8,128)S(1)}, f32[32,512]{1,0:T(8,128)S(1)}, u32[]{:S(2)}, u32[]{:S(2)}) collective-permute-start(f32[32,512]{1,0:T(8,128)S(1)} %get-tuple-element.24), channel_id=1, source_target_pairs={{0,8},{4,12},{8,0},{12,4},{1,9},{5,13},{9,1},{13,5},{2,10},{6,14},... | collective-permute-start | bytes 196616 | tf_op jit(solution)/shard_map/ppermute | solution.py:15
  111.1 7.2 %collective-permute-start.23 = (f32[32,512]{1,0:T(8,128)S(1)}, f32[32,512]{1,0:T(8,128)S(1)}, u32[]{:S(2)}, u32[]{:S(2)}) collective-permute-start(f32[32,512]{1,0:T(8,128)S(1)} %get-tuple-element.23), channel_id=1, source_target_pairs={{0,12},{4,8},{8,4},{12,0},{1,13},{5,9},{9,5},{13,1},{2,14},{6,10},... | collective-permute-start | bytes 196616 | tf_op jit(solution)/shard_map/ppermute | solution.py:15
  119.9 7.6 %collective-permute-start.25 = (f32[32,512]{1,0:T(8,128)S(1)}, f32[32,512]{1,0:T(8,128)S(1)}, u32[]{:S(2)}, u32[]{:S(2)}) collective-permute-start(f32[32,512]{1,0:T(8,128)S(1)} %get-tuple-element.7), channel_id=1, source_target_pairs={{0,8},{4,12},{8,0},{12,4},{1,9},{5,13},{9,1},{13,5},{2,10},{6,14},... | collective-permute-start | bytes 196616 | tf_op jit(solution)/shard_map/ppermute | solution.py:15
  120.6 6.9 %collective-permute-start.26 = (f32[32,512]{1,0:T(8,128)S(1)}, f32[32,512]{1,0:T(8,128)S(1)}, u32[]{:S(2)}, u32[]{:S(2)}) collective-permute-start(f32[32,512]{1,0:T(8,128)S(1)} %get-tuple-element.7), channel_id=1, source_target_pairs={{0,12},{4,8},{8,4},{12,0},{1,13},{5,9},{9,5},{13,1},{2,14},{6,10},... | collective-permute-start | bytes 196616 | tf_op jit(solution)/shard_map/ppermute | solution.py:15
  130.7 5.6 %collective-permute-start.28 = (f32[32,1024]{1,0:T(8,128)S(1)}, f32[32,1024]{1,0:T(8,128)S(1)}, u32[]{:S(2)}, u32[]{:S(2)}) collective-permute-start(f32[32,1024]{1,0:T(8,128)S(1)} %select_add_fusion.1), channel_id=1, source_target_pairs={{0,2},{1,3},{2,0},{3,1},{4,6},{5,7},{6,4},{7,5},{8,10},{9,11},{10,... | collective-permute-start | bytes 393224 | tf_op jit(solution)/shard_map/ppermute | solution.py:15
  142.7 4.5 %collective-permute-start.30 = (f32[32,512]{1,0:T(8,128)S(1)}, f32[32,512]{1,0:T(8,128)S(1)}, u32[]{:S(2)}, u32[]{:S(2)}) collective-permute-start(f32[32,512]{1,0:T(8,128)S(1)} %get-tuple-element.17), channel_id=1, source_target_pairs={{0,4},{4,0},{8,12},{12,8},{1,5},{5,1},{9,13},{13,9},{2,6},{6,2},{1... | collective-permute-start | bytes 196616 | tf_op jit(solution)/shard_map/ppermute | solution.py:15
  144.0 8.0 %collective-permute-start.31 = (f32[32,512]{1,0:T(8,128)S(1)}, f32[32,512]{1,0:T(8,128)S(1)}, u32[]{:S(2)}, u32[]{:S(2)}) collective-permute-start(f32[32,512]{1,0:T(8,128)S(1)} %get-tuple-element.19), channel_id=1, source_target_pairs={{0,8},{4,12},{8,0},{12,4},{1,9},{5,13},{9,1},{13,5},{2,10},{6,14},... | collective-permute-start | bytes 196616 | tf_op jit(solution)/shard_map/ppermute | solution.py:15
  144.8 7.2 %collective-permute-start.32 = (f32[32,512]{1,0:T(8,128)S(1)}, f32[32,512]{1,0:T(8,128)S(1)}, u32[]{:S(2)}, u32[]{:S(2)}) collective-permute-start(f32[32,512]{1,0:T(8,128)S(1)} %get-tuple-element.18), channel_id=1, source_target_pairs={{0,12},{4,8},{8,4},{12,0},{1,13},{5,9},{9,5},{13,1},{2,14},{6,10},... | collective-permute-start | bytes 196616 | tf_op jit(solution)/shard_map/ppermute | solution.py:15
  153.7 7.6 %collective-permute-start.34 = (f32[32,512]{1,0:T(8,128)S(1)}, f32[32,512]{1,0:T(8,128)S(1)}, u32[]{:S(2)}, u32[]{:S(2)}) collective-permute-start(f32[32,512]{1,0:T(8,128)S(1)} %get-tuple-element.5), channel_id=1, source_target_pairs={{0,8},{4,12},{8,0},{12,4},{1,9},{5,13},{9,1},{13,5},{2,10},{6,14},... | collective-permute-start | bytes 196616 | tf_op jit(solution)/shard_map/ppermute | solution.py:15
  154.4 6.9 %collective-permute-start.35 = (f32[32,512]{1,0:T(8,128)S(1)}, f32[32,512]{1,0:T(8,128)S(1)}, u32[]{:S(2)}, u32[]{:S(2)}) collective-permute-start(f32[32,512]{1,0:T(8,128)S(1)} %get-tuple-element.5), channel_id=1, source_target_pairs={{0,12},{4,8},{8,4},{12,0},{1,13},{5,9},{9,5},{13,1},{2,14},{6,10},... | collective-permute-start | bytes 196616 | tf_op jit(solution)/shard_map/ppermute | solution.py:15
  165.9 5.6 %collective-permute-start.37 = (f32[32,1024]{1,0:T(8,128)S(1)}, f32[32,1024]{1,0:T(8,128)S(1)}, u32[]{:S(2)}, u32[]{:S(2)}) collective-permute-start(f32[32,1024]{1,0:T(8,128)S(1)} %select_add_fusion), channel_id=1, source_target_pairs={{0,2},{1,3},{2,0},{3,1},{4,6},{5,7},{6,4},{7,5},{8,10},{9,11},{10,... | collective-permute-start | bytes 393224 | tf_op jit(solution)/shard_map/ppermute | solution.py:15
  178.0 4.5 %collective-permute-start.39 = (f32[32,512]{1,0:T(8,128)S(1)}, f32[32,512]{1,0:T(8,128)S(1)}, u32[]{:S(2)}, u32[]{:S(2)}) collective-permute-start(f32[32,512]{1,0:T(8,128)S(1)} %get-tuple-element.12), channel_id=1, source_target_pairs={{0,4},{4,0},{8,12},{12,8},{1,5},{5,1},{9,13},{13,9},{2,6},{6,2},{1... | collective-permute-start | bytes 196616 | tf_op jit(solution)/shard_map/ppermute | solution.py:15
  179.3 8.0 %collective-permute-start.40 = (f32[32,512]{1,0:T(8,128)S(1)}, f32[32,512]{1,0:T(8,128)S(1)}, u32[]{:S(2)}, u32[]{:S(2)}) collective-permute-start(f32[32,512]{1,0:T(8,128)S(1)} %get-tuple-element.14), channel_id=1, source_target_pairs={{0,8},{4,12},{8,0},{12,4},{1,9},{5,13},{9,1},{13,5},{2,10},{6,14},... | collective-permute-start | bytes 196616 | tf_op jit(solution)/shard_map/ppermute | solution.py:15
  180.1 7.2 %collective-permute-start.41 = (f32[32,512]{1,0:T(8,128)S(1)}, f32[32,512]{1,0:T(8,128)S(1)}, u32[]{:S(2)}, u32[]{:S(2)}) collective-permute-start(f32[32,512]{1,0:T(8,128)S(1)} %get-tuple-element.13), channel_id=1, source_target_pairs={{0,12},{4,8},{8,4},{12,0},{1,13},{5,9},{9,5},{13,1},{2,14},{6,10},... | collective-permute-start | bytes 196616 | tf_op jit(solution)/shard_map/ppermute | solution.py:15
  187.3 5.4 %collective-permute-start.42 = (f32[32,512]{1,0:T(8,128)S(1)}, f32[32,512]{1,0:T(8,128)S(1)}, u32[]{:S(2)}, u32[]{:S(2)}) collective-permute-start(f32[32,512]{1,0:T(8,128)S(1)} %get-tuple-element.3), channel_id=1, source_target_pairs={{0,4},{4,0},{8,12},{12,8},{1,5},{5,1},{9,13},{13,9},{2,6},{6,2},{1... | collective-permute-start | bytes 196616 | tf_op jit(solution)/shard_map/ppermute | solution.py:15
  189.9 7.4 %collective-permute-start.43 = (f32[32,512]{1,0:T(8,128)S(1)}, f32[32,512]{1,0:T(8,128)S(1)}, u32[]{:S(2)}, u32[]{:S(2)}) collective-permute-start(f32[32,512]{1,0:T(8,128)S(1)} %get-tuple-element.3), channel_id=1, source_target_pairs={{0,8},{4,12},{8,0},{12,4},{1,9},{5,13},{9,1},{13,5},{2,10},{6,14},... | collective-permute-start | bytes 196616 | tf_op jit(solution)/shard_map/ppermute | solution.py:15
  190.6 6.7 %collective-permute-start.44 = (f32[32,512]{1,0:T(8,128)S(1)}, f32[32,512]{1,0:T(8,128)S(1)}, u32[]{:S(2)}, u32[]{:S(2)}) collective-permute-start(f32[32,512]{1,0:T(8,128)S(1)} %get-tuple-element.3), channel_id=1, source_target_pairs={{0,12},{4,8},{8,4},{12,0},{1,13},{5,9},{9,5},{13,1},{2,14},{6,10},... | collective-permute-start | bytes 196616 | tf_op jit(solution)/shard_map/ppermute | solution.py:15
  (21 other events, 423.2 us)

commit v2 on v0

v2 whole, which is shorter than its diff:
```python
import functools
import jax
import jax.numpy as jnp
from jax import lax
from jax.experimental import pallas as pl
from jax.experimental.pallas import tpu as pltpu
from jax.sharding import PartitionSpec as P

LEVELS = 3
STREAMS = 2
COPIES = 8
IN_VMEM = pl.BlockSpec(memory_space=pltpu.VMEM)
IN_PLACE = pl.BlockSpec(memory_space=pltpu.HBM)
LOWER = (((1,), (1,)), ((), ()))
UPPER = (((1,), (0,)), ((), ()))


def pair_index(high, low):
    return high * (high - 1) // 2 + low


def params():
    return pltpu.CompilerParams(vmem_limit_bytes=2 << 20)


def block_copies(blocks_ref, out_ref, sems, index):
    height = out_ref.shape[0] // COPIES
    return [
        pltpu.make_async_copy(
            blocks_ref.at[index, pl.ds(i * height, height), :],
            out_ref.at[pl.ds(i * height, height), :],
            sems.at[i],
        )
        for i in range(COPIES)
    ]


def fetch(blocks, index):
    def kernel(blocks_ref, out_ref, sems):
        copies = block_copies(blocks_ref, out_ref, sems, index)
        for copy in copies:
            copy.start()
        for copy in copies:
            copy.wait()

    return pl.pallas_call(
        kernel,
        out_shape=jax.ShapeDtypeStruct(blocks.shape[1:], blocks.dtype),
        in_specs=[IN_PLACE],
        out_specs=IN_VMEM,
        scratch_shapes=[pltpu.SemaphoreType.DMA((COPIES,))],
        compiler_params=params(),
        name="fetch",
    )(pltpu.with_memory_space_constraint(blocks, pltpu.HBM))


def fetch_and_apply(vector, blocks, index):
    rows, cols = blocks.shape[1:]
    height = rows // COPIES

    def kernel(vector_ref, blocks_ref, block_ref, out_ref, sems):
        copies = block_copies(blocks_ref, block_ref, sems, index)
        for copy in copies:
            copy.start()
        vector_bf = vector_ref[...].astype(jnp.bfloat16)
        for i, copy in enumerate(copies):
            copy.wait()
            span = pl.ds(i * height, height)
            out_ref[:, span] = lax.dot_general(
                vector_bf, block_ref[span, :], LOWER, preferred_element_type=jnp.float32
            )

    return pl.pallas_call(
        kernel,
        out_shape=(
            jax.ShapeDtypeStruct((rows, cols), blocks.dtype),
            jax.ShapeDtypeStruct((vector.shape[0], rows), jnp.float32),
        ),
        in_specs=[IN_VMEM, IN_PLACE],
        out_specs=(IN_VMEM, IN_VMEM),
        scratch_shapes=[pltpu.SemaphoreType.DMA((COPIES,))],
        compiler_params=params(),
        name="fetch_and_apply",
    )(vector, pltpu.with_memory_space_constraint(blocks, pltpu.HBM))


def apply(vector, block, dims):
    width = block.shape[0] if dims is LOWER else block.shape[1]

    def kernel(vector_ref, block_ref, out_ref):
        out_ref[...] = lax.dot_general(
            vector_ref[...].astype(jnp.bfloat16),
            block_ref[...],
            dims,
            preferred_element_type=jnp.float32,
        )

    return pl.pallas_call(
        kernel,
        out_shape=jax.ShapeDtypeStruct((vector.shape[0], width), jnp.float32),
        in_specs=[IN_VMEM, IN_VMEM],
        out_specs=IN_VMEM,
        compiler_params=params(),
        name="apply_lower" if dims is LOWER else "apply_upper",
    )(vector, block)


class Order:
    def __init__(self, first):
        self.last = first

    def after(self, *values):
        *values, self.last = lax.optimization_barrier((*values, self.last))
        return values

    def run(self, function, *values):
        result = function(*self.after(*values))
        self.last = result
        return result


def body(coupling, diag_inverse, loads, axle_index, *, sizes):
    positions = loads.shape[1]
    selector = (axle_index[:, None] == jnp.arange(positions, dtype=jnp.int32)[None, :]).astype(
        jnp.bfloat16
    )
    rhs = jnp.einsum("lp,kpc->klc", selector, loads, preferred_element_type=jnp.float32)
    count = rhs.shape[1] // STREAMS
    order = Order(rhs)
    blocks = {}
    solved = {}
    answers = {}
    early = {}

    def bring(kind, index):
        if (kind, index) not in blocks:
            source = diag_inverse if kind == "diag" else coupling
            blocks[kind, index] = order.run(lambda a: fetch(a, index), source)

    def all_sum(value, axis):
        size = sizes[axis]
        step = 1
        while step < size:
            (value,) = order.after(value)
            other = lax.ppermute(value, axis, [(i, i ^ step) for i in range(size)])
            yield
            value = order.run(jnp.add, value, other)
            step *= 2
        return value

    def times(vector, kind, index, dims):
        bring(kind, index)
        return order.run(lambda a, b: apply(a, b, dims), vector, blocks[kind, index])

    def far_term(high, low, me, found, dims):
        if (high, low, me, dims) not in early:
            source = low if dims is LOWER else high
            early[high, low, me, dims] = times(
                found[source, me], "coupling", pair_index(high, low), dims
            )
        return early[high, low, me, dims]

    def stream(me, first):
        part = first
        for level in range(LEVELS):
            if level > 0:
                part = times(solved[level - 1, me], "coupling", pair_index(level, level - 1), LOWER)
                for lower in range(level - 1):
                    part = part + far_term(level, lower, me, solved, LOWER)
                total = yield from all_sum(part, "rows")
                resid = rhs[level, me * count : (me + 1) * count] - total
                part = times(resid, "diag", level, LOWER)
            yield
            solved[level, me] = yield from all_sum(part, "cols")
        for level in range(LEVELS - 1, -1, -1):
            resid = solved[level, me]
            if level < LEVELS - 1:
                part = times(answers[level + 1, me], "coupling", pair_index(level + 1, level), UPPER)
                for upper in range(level + 2, LEVELS):
                    part = part + far_term(upper, level, me, answers, UPPER)
                resid = resid - (yield from all_sum(part, "cols"))
            part = times(resid, "diag", level, UPPER)
            answers[level, me] = yield from all_sum(part, "rows")

    block, first = fetch_and_apply(rhs[0], diag_inverse, 0)
    blocks["diag", 0] = block
    order.last = first
    lanes = [stream(me, first[me * count : (me + 1) * count]) for me in range(STREAMS)]

    def advance(me):
        try:
            next(lanes[me])
            return True
        except StopIteration:
            return False

    fetches = [("coupling", 0), ("diag", 1), ("coupling", 1), ("coupling", 2), ("diag", 2)]
    step = 0
    alive = True
    while alive:
        alive = False
        for me in range(STREAMS):
            alive = advance(me) or alive
            if fetches and step % 2 == 0:
                bring(*fetches.pop(0))
            for high in range(2, LEVELS):
                for low in range(high - 1):
                    if (low, me) in solved and ("coupling", pair_index(high, low)) in blocks:
                        far_term(high, low, me, solved, LOWER)
                    if (high, me) in answers:
                        far_term(high, low, me, answers, UPPER)
            step += 1
    stack = lambda found: jnp.stack(
        [jnp.concatenate([found[level, me] for me in range(STREAMS)]) for level in range(LEVELS)]
    )
    return stack(answers), stack(solved)


def solution(mesh):
    placed = (
        P("groups", "cols", "rows"),
        P("groups", "rows", "cols"),
        P("groups", None, "cols"),
        P("groups"),
    )
    return jax.shard_map(
        functools.partial(body, sizes=dict(mesh.shape)),
        mesh=mesh,
        in_specs=placed,
        out_specs=(P("groups", None, "cols"), P("groups", None, "rows")),
        check_vma=False,
    )
```

time: 432 us -> 176 us (0.41)
  waiting for transfers between devices: 338 us -> 72.9 us
  matrix products: 74.4 us -> 1.04 us
  Pallas kernels: 0 us -> 61.2 us
  starting transfers between devices: 0.6 us -> 35.5 us
  between operations: 14.2 us -> 1.03 us
    psum x10 -> x0, waiting for transfers between devices: 338 us -> none  [the longest x3 105 us: backward_diag(): return lax.psum(partial_value, 'rows')]
    dot_general x12 -> x0, matrix products: 73.4 us -> none  [the longest x3 20.2 us: forward_diag(): jnp.einsum('lm,im->li', resid.astype(jnp.bfloat16), tile, preferred_eleme...]
    ppermute x0 -> x40, waiting for transfers between devices: none -> 72.9 us  [all_sum(): other = lax.ppermute(value, axis, [(i, i ^ step) for i in range(size)])]
    pallas_call x0 -> x28, Pallas kernels: none -> 61.2 us  [the longest x22 37.3 us: apply(): pl.pallas_call(kernel, out_shape=jax.ShapeDtypeStruct((vector.shape[0], w...]
    ppermute x0 -> x40, starting transfers between devices: none -> 35.5 us  [all_sum(): other = lax.ppermute(value, axis, [(i, i ^ step) for i in range(size)])]
  transfers between devices with their start and end apart: 10 -> 40, of which waited for: 10 -> 25; matrix products, arithmetic and copies ran while one was open for 0% -> 1% of each run, Pallas kernels for 0% -> 27%
where the time goes in v2:
time: 176 us
  waiting for transfers between devices  72.9 us (41%)
  Pallas kernels  61.2 us (35%)
  starting transfers between devices  35.5 us (20%)
  other arithmetic  2.84 us (2%)
    ppermute x40, waiting for transfers between devices, all_sum(): other = lax.ppermute(value, axis, [(i, i ^ step) for i in range(size)])  72.9 us
    pallas_call x22, Pallas kernels, apply(): pl.pallas_call(kernel, out_shape=jax.ShapeDtypeStruct((vector.shape[0], w...  37.3 us
    ppermute x40, starting transfers between devices, all_sum(): other = lax.ppermute(value, axis, [(i, i ^ step) for i in range(size)])  35.5 us
    pallas_call x5, Pallas kernels, fetch(): pl.pallas_call(kernel, out_shape=jax.ShapeDtypeStruct(blocks.shape[1:], b...  17.4 us
    pallas_call x1, Pallas kernels, fetch_and_apply(): pl.pallas_call(kernel, out_shape=(jax.ShapeDtypeStruct((rows, cols), bloc...  6.59 us
  transfers between devices with their start and end apart: 40, of which 25 were waited for; matrix products, arithmetic and copies ran while one was open for 1% of the time, Pallas kernels for 27%

profile of v2, /device:TPU:0, one launch (start us, length us, event | category | flops | bytes accessed | tf_op | source)
XLA Modules:
  0.0 176.0 jit_solution(12921005406550312511)
XLA Ops:
  3.1 6.6 %fetch_and_apply.1 = (bf16[2048,2048]{1,0:T(8,128)(2,1)S(1)}, f32[32,2048]{1,0:T(8,128)S(1)}) custom-call(f32[32,2048]{1,0:T(8,128)S(1)} %slice_bitcast_fusion.vector_ref, bf16[3,2048,2048]{2,1,0:T(8,128)(2,1)} %blocks_ref.6), custom_call_target="tpu_custom_call" | custom-call | tf_op jit(solution)/shard_map/fetch_and_apply/pallas_call | solution.py:73
  9.7 3.5 %fetch.5.block_ref = bf16[2048,2048]{1,0:T(8,128)(2,1)S(1)} custom-call(bf16[3,2048,2048]{2,1,0:T(8,128)(2,1)} %blocks_ref.5), custom_call_target="tpu_custom_call" | custom-call | tf_op jit(solution)/shard_map/fetch/pallas_call | solution.py:46
  13.7 3.5 %fetch.6.block_ref = bf16[2048,2048]{1,0:T(8,128)(2,1)S(1)} custom-call(bf16[3,2048,2048]{2,1,0:T(8,128)(2,1)} %blocks_ref.6), custom_call_target="tpu_custom_call" | custom-call | tf_op jit(solution)/shard_map/fetch/pallas_call | solution.py:46
  17.4 3.0 %collective-permute-start.1 = (f32[16,2048]{1,0:T(8,128)S(1)}, f32[16,2048]{1,0:T(8,128)S(1)}, u32[]{:S(2)}, u32[]{:S(2)}) collective-permute-start(f32[16,2048]{1,0:T(8,128)S(1)} %add.132), channel_id=1, source_target_pairs={{0,2},{1,3},{2,0},{3,1},{4,6},{5,7},{6,4},{7,5},{8,10},{9,11},{10,... | collective-permute-start | bytes 393224 | tf_op jit(solution)/shard_map/ppermute | solution.py:145
  20.4 3.5 %fetch.7.block_ref = bf16[2048,2048]{1,0:T(8,128)(2,1)S(1)} custom-call(bf16[3,2048,2048]{2,1,0:T(8,128)(2,1)} %blocks_ref.5), custom_call_target="tpu_custom_call" | custom-call | tf_op jit(solution)/shard_map/fetch/pallas_call | solution.py:46
  24.1 2.3 %apply_lower.10 = f32[16,2048]{1,0:T(8,128)S(1)} custom-call(f32[16,2048]{1,0:T(8,128)S(1)} %add.133.vector_ref, bf16[2048,2048]{1,0:T(8,128)(2,1)S(1)} %fetch.5.block_ref), custom_call_target="tpu_custom_call" | custom-call | tf_op jit(solution)/shard_map/apply_lower/pallas_call | solution.py:98
  28.4 3.5 %fetch.8.block_ref = bf16[2048,2048]{1,0:T(8,128)(2,1)S(1)} custom-call(bf16[3,2048,2048]{2,1,0:T(8,128)(2,1)} %blocks_ref.5), custom_call_target="tpu_custom_call" | custom-call | tf_op jit(solution)/shard_map/fetch/pallas_call | solution.py:46
  31.8 2.3 %apply_lower.11 = f32[16,2048]{1,0:T(8,128)S(1)} custom-call(f32[16,2048]{1,0:T(8,128)S(1)} %add.133.vector_ref, bf16[2048,2048]{1,0:T(8,128)(2,1)S(1)} %fetch.7.block_ref), custom_call_target="tpu_custom_call" | custom-call | tf_op jit(solution)/shard_map/apply_lower/pallas_call | solution.py:98
  34.2 2.3 %apply_lower.14 = f32[16,2048]{1,0:T(8,128)S(1)} custom-call(f32[16,2048]{1,0:T(8,128)S(1)} %add.135.vector_ref, bf16[2048,2048]{1,0:T(8,128)(2,1)S(1)} %fetch.5.block_ref), custom_call_target="tpu_custom_call" | custom-call | tf_op jit(solution)/shard_map/apply_lower/pallas_call | solution.py:98
  36.5 2.3 %apply_lower.12 = f32[16,2048]{1,0:T(8,128)S(1)} custom-call(f32[16,2048]{1,0:T(8,128)S(1)} %add.135.vector_ref, bf16[2048,2048]{1,0:T(8,128)(2,1)S(1)} %fetch.7.block_ref), custom_call_target="tpu_custom_call" | custom-call | tf_op jit(solution)/shard_map/apply_lower/pallas_call | solution.py:98
  38.8 3.1 %collective-permute-start.5 = (f32[16,2048]{1,0:T(8,128)S(1)}, f32[16,2048]{1,0:T(8,128)S(1)}, u32[]{:S(2)}, u32[]{:S(2)}) collective-permute-start(f32[16,2048]{1,0:T(8,128)S(1)} %add.136), channel_id=1, source_target_pairs={{0,8},{4,12},{8,0},{12,4},{1,9},{5,13},{9,1},{13,5},{2,10},{6,14},... | collective-permute-start | bytes 393224 | tf_op jit(solution)/shard_map/ppermute | solution.py:145
  41.8 3.5 %fetch.9.block_ref = bf16[2048,2048]{1,0:T(8,128)(2,1)S(1)} custom-call(bf16[3,2048,2048]{2,1,0:T(8,128)(2,1)} %blocks_ref.6), custom_call_target="tpu_custom_call" | custom-call | tf_op jit(solution)/shard_map/fetch/pallas_call | solution.py:46
  47.2 2.3 %apply_lower.13 = f32[16,2048]{1,0:T(8,128)S(1)} custom-call(f32[16,2048]{1,0:T(8,128)S(1)} %fusion.3, bf16[2048,2048]{1,0:T(8,128)(2,1)S(1)} %fetch.6.block_ref), custom_call_target="tpu_custom_call" | custom-call | tf_op jit(solution)/shard_map/apply_lower/pallas_call | solution.py:98
  49.5 3.6 %collective-permute-done.7 = f32[16,2048]{1,0:T(8,128)S(1)} collective-permute-done((f32[16,2048]{1,0:T(8,128)S(1)}, f32[16,2048]{1,0:T(8,128)S(1)}, u32[]{:S(2)}, u32[]{:S(2)}) %collective-permute-start.7) | collective-permute-done | bytes 131104 | tf_op jit(solution)/shard_map/ppermute | solution.py:145
  53.2 2.3 %apply_lower.15 = f32[16,2048]{1,0:T(8,128)S(1)} custom-call(f32[16,2048]{1,0:T(8,128)S(1)} %fusion.2, bf16[2048,2048]{1,0:T(8,128)(2,1)S(1)} %fetch.6.block_ref), custom_call_target="tpu_custom_call" | custom-call | tf_op jit(solution)/shard_map/apply_lower/pallas_call | solution.py:98
  59.0 4.2 %collective-permute-done.9 = f32[16,2048]{1,0:T(8,128)S(1)} collective-permute-done((f32[16,2048]{1,0:T(8,128)S(1)}, f32[16,2048]{1,0:T(8,128)S(1)}, u32[]{:S(2)}, u32[]{:S(2)}) %collective-permute-start.9) | collective-permute-done | bytes 131104 | tf_op jit(solution)/shard_map/ppermute | solution.py:145
  63.3 2.4 %apply_lower.16 = f32[16,2048]{1,0:T(8,128)S(1)} custom-call(f32[16,2048]{1,0:T(8,128)S(1)} %add.141.vector_ref, bf16[2048,2048]{1,0:T(8,128)(2,1)S(1)} %fetch.8.block_ref), custom_call_target="tpu_custom_call" | custom-call | tf_op jit(solution)/shard_map/apply_lower/pallas_call | solution.py:98
  66.5 2.3 %apply_lower.18 = f32[16,2048]{1,0:T(8,128)S(1)} custom-call(f32[16,2048]{1,0:T(8,128)S(1)} %add.146.vector_ref, bf16[2048,2048]{1,0:T(8,128)(2,1)S(1)} %fetch.8.block_ref), custom_call_target="tpu_custom_call" | custom-call | tf_op jit(solution)/shard_map/apply_lower/pallas_call | solution.py:98
  75.0 2.4 %collective-permute-start.15 = (f32[16,2048]{1,0:T(8,128)S(1)}, f32[16,2048]{1,0:T(8,128)S(1)}, u32[]{:S(2)}, u32[]{:S(2)}) collective-permute-start(f32[16,2048]{1,0:T(8,128)S(1)} %add.148), channel_id=1, source_target_pairs={{0,8},{4,12},{8,0},{12,4},{1,9},{5,13},{9,1},{13,5},{2,10},{6,14},... | collective-permute-start | bytes 393224 | tf_op jit(solution)/shard_map/ppermute | solution.py:145
  77.4 5.1 %collective-permute-done.11 = f32[16,2048]{1,0:T(8,128)S(1)} collective-permute-done((f32[16,2048]{1,0:T(8,128)S(1)}, f32[16,2048]{1,0:T(8,128)S(1)}, u32[]{:S(2)}, u32[]{:S(2)}) %collective-permute-start.11) | collective-permute-done | bytes 131104 | tf_op jit(solution)/shard_map/ppermute | solution.py:145
  82.6 2.3 %apply_lower.17 = f32[16,2048]{1,0:T(8,128)S(1)} custom-call(f32[16,2048]{1,0:T(8,128)S(1)} %fusion.1, bf16[2048,2048]{1,0:T(8,128)(2,1)S(1)} %fetch.9.block_ref), custom_call_target="tpu_custom_call" | custom-call | tf_op jit(solution)/shard_map/apply_lower/pallas_call | solution.py:98
  84.9 2.3 %apply_lower.19 = f32[16,2048]{1,0:T(8,128)S(1)} custom-call(f32[16,2048]{1,0:T(8,128)S(1)} %fusion, bf16[2048,2048]{1,0:T(8,128)(2,1)S(1)} %fetch.9.block_ref), custom_call_target="tpu_custom_call" | custom-call | tf_op jit(solution)/shard_map/apply_lower/pallas_call | solution.py:98
  90.8 4.2 %collective-permute-done.17 = f32[16,2048]{1,0:T(8,128)S(1)} collective-permute-done((f32[16,2048]{1,0:T(8,128)S(1)}, f32[16,2048]{1,0:T(8,128)S(1)}, u32[]{:S(2)}, u32[]{:S(2)}) %collective-permute-start.17) | collective-permute-done | bytes 131104 | tf_op jit(solution)/shard_map/ppermute | solution.py:145
  99.5 4.2 %collective-permute-done.18 = f32[16,2048]{1,0:T(8,128)S(1)} collective-permute-done((f32[16,2048]{1,0:T(8,128)S(1)}, f32[16,2048]{1,0:T(8,128)S(1)}, u32[]{:S(2)}, u32[]{:S(2)}) %collective-permute-start.18) | collective-permute-done | bytes 131104 | tf_op jit(solution)/shard_map/ppermute | solution.py:145
  107.3 7.2 %collective-permute-done.19 = f32[16,2048]{1,0:T(8,128)S(1)} collective-permute-done((f32[16,2048]{1,0:T(8,128)S(1)}, f32[16,2048]{1,0:T(8,128)S(1)}, u32[]{:S(2)}, u32[]{:S(2)}) %collective-permute-start.19) | collective-permute-done | bytes 131104 | tf_op jit(solution)/shard_map/ppermute | solution.py:145
  122.1 4.3 %collective-permute-done.25 = f32[16,2048]{1,0:T(8,128)S(1)} collective-permute-done((f32[16,2048]{1,0:T(8,128)S(1)}, f32[16,2048]{1,0:T(8,128)S(1)}, u32[]{:S(2)}, u32[]{:S(2)}) %collective-permute-start.25) | collective-permute-done | bytes 131104 | tf_op jit(solution)/shard_map/ppermute | solution.py:145
  131.0 3.2 %collective-permute-done.26 = f32[16,2048]{1,0:T(8,128)S(1)} collective-permute-done((f32[16,2048]{1,0:T(8,128)S(1)}, f32[16,2048]{1,0:T(8,128)S(1)}, u32[]{:S(2)}, u32[]{:S(2)}) %collective-permute-start.26) | collective-permute-done | bytes 131104 | tf_op jit(solution)/shard_map/ppermute | solution.py:145
  134.4 2.3 %collective-permute-done.34 = f32[16,2048]{1,0:T(8,128)S(1)} collective-permute-done((f32[16,2048]{1,0:T(8,128)S(1)}, f32[16,2048]{1,0:T(8,128)S(1)}, u32[]{:S(2)}, u32[]{:S(2)}) %collective-permute-start.34) | collective-permute-done | bytes 131104 | tf_op jit(solution)/shard_map/ppermute | solution.py:145
  137.3 7.7 %collective-permute-done.27 = f32[16,2048]{1,0:T(8,128)S(1)} collective-permute-done((f32[16,2048]{1,0:T(8,128)S(1)}, f32[16,2048]{1,0:T(8,128)S(1)}, u32[]{:S(2)}, u32[]{:S(2)}) %collective-permute-start.27) | collective-permute-done | bytes 131104 | tf_op jit(solution)/shard_map/ppermute | solution.py:145
  150.8 3.9 %collective-permute-done.29 = f32[16,2048]{1,0:T(8,128)S(1)} collective-permute-done((f32[16,2048]{1,0:T(8,128)S(1)}, f32[16,2048]{1,0:T(8,128)S(1)}, u32[]{:S(2)}, u32[]{:S(2)}) %collective-permute-start.29) | collective-permute-done | bytes 131104 | tf_op jit(solution)/shard_map/ppermute | solution.py:145
  160.1 3.5 %collective-permute-done.30 = f32[16,2048]{1,0:T(8,128)S(1)} collective-permute-done((f32[16,2048]{1,0:T(8,128)S(1)}, f32[16,2048]{1,0:T(8,128)S(1)}, u32[]{:S(2)}, u32[]{:S(2)}) %collective-permute-start.30) | collective-permute-done | bytes 131104 | tf_op jit(solution)/shard_map/ppermute | solution.py:145
  166.7 6.9 %collective-permute-done.31 = f32[16,2048]{1,0:T(8,128)S(1)} collective-permute-done((f32[16,2048]{1,0:T(8,128)S(1)}, f32[16,2048]{1,0:T(8,128)S(1)}, u32[]{:S(2)}, u32[]{:S(2)}) %collective-permute-start.31) | collective-permute-done | bytes 131104 | tf_op jit(solution)/shard_map/ppermute | solution.py:145
  (133 shorter events, 59.2 us)
Async XLA Ops:
  17.2 6.6 %collective-permute-start.3 = (f32[16,2048]{1,0:T(8,128)S(1)}, f32[16,2048]{1,0:T(8,128)S(1)}, u32[]{:S(2)}, u32[]{:S(2)}) collective-permute-start(f32[16,2048]{1,0:T(8,128)S(1)} %get-tuple-element.147), channel_id=1, source_target_pairs={{0,1},{1,0},{2,3},{3,2},{4,5},{5,4},{6,7},{7,6},{8,9},{9,8},{10,11... | collective-permute-start | bytes 393224 | tf_op jit(solution)/shard_map/ppermute | solution.py:145
  17.4 6.7 %collective-permute-start.1 = (f32[16,2048]{1,0:T(8,128)S(1)}, f32[16,2048]{1,0:T(8,128)S(1)}, u32[]{:S(2)}, u32[]{:S(2)}) collective-permute-start(f32[16,2048]{1,0:T(8,128)S(1)} %add.132), channel_id=1, source_target_pairs={{0,2},{1,3},{2,0},{3,1},{4,6},{5,7},{6,4},{7,5},{8,10},{9,11},{10,... | collective-permute-start | bytes 393224 | tf_op jit(solution)/shard_map/ppermute | solution.py:145
  23.9 10.2 %collective-permute-start.4 = (f32[16,2048]{1,0:T(8,128)S(1)}, f32[16,2048]{1,0:T(8,128)S(1)}, u32[]{:S(2)}, u32[]{:S(2)}) collective-permute-start(f32[16,2048]{1,0:T(8,128)S(1)} %add.134), channel_id=1, source_target_pairs={{0,2},{1,3},{2,0},{3,1},{4,6},{5,7},{6,4},{7,5},{8,10},{9,11},{10,... | collective-permute-start | bytes 393224 | tf_op jit(solution)/shard_map/ppermute | solution.py:145
  26.3 12.4 %collective-permute-start.2 = (f32[16,2048]{1,0:T(8,128)S(1)}, f32[16,2048]{1,0:T(8,128)S(1)}, u32[]{:S(2)}, u32[]{:S(2)}) collective-permute-start(f32[16,2048]{1,0:T(8,128)S(1)} %apply_lower.10), channel_id=1, source_target_pairs={{0,4},{4,0},{8,12},{12,8},{1,5},{5,1},{9,13},{13,9},{2,6},{6,2},{1... | collective-permute-start | bytes 393224 | tf_op jit(solution)/shard_map/ppermute | solution.py:145
  36.4 8.9 %collective-permute-start.6 = (f32[16,2048]{1,0:T(8,128)S(1)}, f32[16,2048]{1,0:T(8,128)S(1)}, u32[]{:S(2)}, u32[]{:S(2)}) collective-permute-start(f32[16,2048]{1,0:T(8,128)S(1)} %apply_lower.14), channel_id=1, source_target_pairs={{0,4},{4,0},{8,12},{12,8},{1,5},{5,1},{9,13},{13,9},{2,6},{6,2},{1... | collective-permute-start | bytes 393224 | tf_op jit(solution)/shard_map/ppermute | solution.py:145
  38.8 8.5 %collective-permute-start.5 = (f32[16,2048]{1,0:T(8,128)S(1)}, f32[16,2048]{1,0:T(8,128)S(1)}, u32[]{:S(2)}, u32[]{:S(2)}) collective-permute-start(f32[16,2048]{1,0:T(8,128)S(1)} %add.136), channel_id=1, source_target_pairs={{0,8},{4,12},{8,0},{12,4},{1,9},{5,13},{9,1},{13,5},{2,10},{6,14},... | collective-permute-start | bytes 393224 | tf_op jit(solution)/shard_map/ppermute | solution.py:145
  45.4 7.8 %collective-permute-start.7 = (f32[16,2048]{1,0:T(8,128)S(1)}, f32[16,2048]{1,0:T(8,128)S(1)}, u32[]{:S(2)}, u32[]{:S(2)}) collective-permute-start(f32[16,2048]{1,0:T(8,128)S(1)} %add.138), channel_id=1, source_target_pairs={{0,8},{4,12},{8,0},{12,4},{1,9},{5,13},{9,1},{13,5},{2,10},{6,14},... | collective-permute-start | bytes 393224 | tf_op jit(solution)/shard_map/ppermute | solution.py:145
  56.8 6.4 %collective-permute-start.9 = (f32[16,2048]{1,0:T(8,128)S(1)}, f32[16,2048]{1,0:T(8,128)S(1)}, u32[]{:S(2)}, u32[]{:S(2)}) collective-permute-start(f32[16,2048]{1,0:T(8,128)S(1)} %add.140), channel_id=1, source_target_pairs={{0,2},{1,3},{2,0},{3,1},{4,6},{5,7},{6,4},{7,5},{8,10},{9,11},{10,... | collective-permute-start | bytes 393224 | tf_op jit(solution)/shard_map/ppermute | solution.py:145
  58.4 8.1 %collective-permute-start.13 = (f32[16,2048]{1,0:T(8,128)S(1)}, f32[16,2048]{1,0:T(8,128)S(1)}, u32[]{:S(2)}, u32[]{:S(2)}) collective-permute-start(f32[16,2048]{1,0:T(8,128)S(1)} %add.145), channel_id=1, source_target_pairs={{0,2},{1,3},{2,0},{3,1},{4,6},{5,7},{6,4},{7,5},{8,10},{9,11},{10,... | collective-permute-start | bytes 393224 | tf_op jit(solution)/shard_map/ppermute | solution.py:145
  65.7 6.1 %collective-permute-start.10 = (f32[16,2048]{1,0:T(8,128)S(1)}, f32[16,2048]{1,0:T(8,128)S(1)}, u32[]{:S(2)}, u32[]{:S(2)}) collective-permute-start(f32[16,2048]{1,0:T(8,128)S(1)} %add.142), channel_id=1, source_target_pairs={{0,4},{4,0},{8,12},{12,8},{1,5},{5,1},{9,13},{13,9},{2,6},{6,2},{1... | collective-permute-start | bytes 393224 | tf_op jit(solution)/shard_map/ppermute | solution.py:145
  68.8 6.1 %collective-permute-start.14 = (f32[16,2048]{1,0:T(8,128)S(1)}, f32[16,2048]{1,0:T(8,128)S(1)}, u32[]{:S(2)}, u32[]{:S(2)}) collective-permute-start(f32[16,2048]{1,0:T(8,128)S(1)} %add.147), channel_id=1, source_target_pairs={{0,4},{4,0},{8,12},{12,8},{1,5},{5,1},{9,13},{13,9},{2,6},{6,2},{1... | collective-permute-start | bytes 393224 | tf_op jit(solution)/shard_map/ppermute | solution.py:145
  71.9 10.7 %collective-permute-start.11 = (f32[16,2048]{1,0:T(8,128)S(1)}, f32[16,2048]{1,0:T(8,128)S(1)}, u32[]{:S(2)}, u32[]{:S(2)}) collective-permute-start(f32[16,2048]{1,0:T(8,128)S(1)} %add.143), channel_id=1, source_target_pairs={{0,8},{4,12},{8,0},{12,4},{1,9},{5,13},{9,1},{13,5},{2,10},{6,14},... | collective-permute-start | bytes 393224 | tf_op jit(solution)/shard_map/ppermute | solution.py:145
  75.0 9.9 %collective-permute-start.15 = (f32[16,2048]{1,0:T(8,128)S(1)}, f32[16,2048]{1,0:T(8,128)S(1)}, u32[]{:S(2)}, u32[]{:S(2)}) collective-permute-start(f32[16,2048]{1,0:T(8,128)S(1)} %add.148), channel_id=1, source_target_pairs={{0,8},{4,12},{8,0},{12,4},{1,9},{5,13},{9,1},{13,5},{2,10},{6,14},... | collective-permute-start | bytes 393224 | tf_op jit(solution)/shard_map/ppermute | solution.py:145
  88.6 6.4 %collective-permute-start.17 = (f32[16,2048]{1,0:T(8,128)S(1)}, f32[16,2048]{1,0:T(8,128)S(1)}, u32[]{:S(2)}, u32[]{:S(2)}) collective-permute-start(f32[16,2048]{1,0:T(8,128)S(1)} %add.150), channel_id=1, source_target_pairs={{0,2},{1,3},{2,0},{3,1},{4,6},{5,7},{6,4},{7,5},{8,10},{9,11},{10,... | collective-permute-start | bytes 393224 | tf_op jit(solution)/shard_map/ppermute | solution.py:145
  90.2 6.8 %collective-permute-start.22 = (f32[16,2048]{1,0:T(8,128)S(1)}, f32[16,2048]{1,0:T(8,128)S(1)}, u32[]{:S(2)}, u32[]{:S(2)}) collective-permute-start(f32[16,2048]{1,0:T(8,128)S(1)} %add.154), channel_id=1, source_target_pairs={{0,2},{1,3},{2,0},{3,1},{4,6},{5,7},{6,4},{7,5},{8,10},{9,11},{10,... | collective-permute-start | bytes 393224 | tf_op jit(solution)/shard_map/ppermute | solution.py:145
  96.2 7.5 %collective-permute-start.18 = (f32[16,2048]{1,0:T(8,128)S(1)}, f32[16,2048]{1,0:T(8,128)S(1)}, u32[]{:S(2)}, u32[]{:S(2)}) collective-permute-start(f32[16,2048]{1,0:T(8,128)S(1)} %apply_upper.12), channel_id=1, source_target_pairs={{0,4},{4,0},{8,12},{12,8},{1,5},{5,1},{9,13},{13,9},{2,6},{6,2},{1... | collective-permute-start | bytes 393224 | tf_op jit(solution)/shard_map/ppermute | solution.py:145
  98.2 7.2 %collective-permute-start.23 = (f32[16,2048]{1,0:T(8,128)S(1)}, f32[16,2048]{1,0:T(8,128)S(1)}, u32[]{:S(2)}, u32[]{:S(2)}) collective-permute-start(f32[16,2048]{1,0:T(8,128)S(1)} %apply_upper.14), channel_id=1, source_target_pairs={{0,4},{4,0},{8,12},{12,8},{1,5},{5,1},{9,13},{13,9},{2,6},{6,2},{1... | collective-permute-start | bytes 393224 | tf_op jit(solution)/shard_map/ppermute | solution.py:145
  103.7 10.8 %collective-permute-start.19 = (f32[16,2048]{1,0:T(8,128)S(1)}, f32[16,2048]{1,0:T(8,128)S(1)}, u32[]{:S(2)}, u32[]{:S(2)}) collective-permute-start(f32[16,2048]{1,0:T(8,128)S(1)} %add.152), channel_id=1, source_target_pairs={{0,8},{4,12},{8,0},{12,4},{1,9},{5,13},{9,1},{13,5},{2,10},{6,14},... | collective-permute-start | bytes 393224 | tf_op jit(solution)/shard_map/ppermute | solution.py:145
  105.4 11.5 %collective-permute-start.24 = (f32[16,2048]{1,0:T(8,128)S(1)}, f32[16,2048]{1,0:T(8,128)S(1)}, u32[]{:S(2)}, u32[]{:S(2)}) collective-permute-start(f32[16,2048]{1,0:T(8,128)S(1)} %add.156), channel_id=1, source_target_pairs={{0,8},{4,12},{8,0},{12,4},{1,9},{5,13},{9,1},{13,5},{2,10},{6,14},... | collective-permute-start | bytes 393224 | tf_op jit(solution)/shard_map/ppermute | solution.py:145
  115.7 4.1 %collective-permute-start.20 = (f32[16,2048]{1,0:T(8,128)S(1)}, f32[16,2048]{1,0:T(8,128)S(1)}, u32[]{:S(2)}, u32[]{:S(2)}) collective-permute-start(f32[16,2048]{1,0:T(8,128)S(1)} %apply_upper.13), channel_id=1, source_target_pairs={{0,1},{1,0},{2,3},{3,2},{4,5},{5,4},{6,7},{7,6},{8,9},{9,8},{10,11... | collective-permute-start | bytes 393224 | tf_op jit(solution)/shard_map/ppermute | solution.py:145
  119.9 6.4 %collective-permute-start.25 = (f32[16,2048]{1,0:T(8,128)S(1)}, f32[16,2048]{1,0:T(8,128)S(1)}, u32[]{:S(2)}, u32[]{:S(2)}) collective-permute-start(f32[16,2048]{1,0:T(8,128)S(1)} %add.158), channel_id=1, source_target_pairs={{0,2},{1,3},{2,0},{3,1},{4,6},{5,7},{6,4},{7,5},{8,10},{9,11},{10,... | collective-permute-start | bytes 393224 | tf_op jit(solution)/shard_map/ppermute | solution.py:145
  121.5 6.7 %collective-permute-start.33 = (f32[16,2048]{1,0:T(8,128)S(1)}, f32[16,2048]{1,0:T(8,128)S(1)}, u32[]{:S(2)}, u32[]{:S(2)}) collective-permute-start(f32[16,2048]{1,0:T(8,128)S(1)} %add.167), channel_id=1, source_target_pairs={{0,2},{1,3},{2,0},{3,1},{4,6},{5,7},{6,4},{7,5},{8,10},{9,11},{10,... | collective-permute-start | bytes 393224 | tf_op jit(solution)/shard_map/ppermute | solution.py:145
  127.6 6.7 %collective-permute-start.26 = (f32[16,2048]{1,0:T(8,128)S(1)}, f32[16,2048]{1,0:T(8,128)S(1)}, u32[]{:S(2)}, u32[]{:S(2)}) collective-permute-start(f32[16,2048]{1,0:T(8,128)S(1)} %apply_upper.17), channel_id=1, source_target_pairs={{0,4},{4,0},{8,12},{12,8},{1,5},{5,1},{9,13},{13,9},{2,6},{6,2},{1... | collective-permute-start | bytes 393224 | tf_op jit(solution)/shard_map/ppermute | solution.py:145
  129.6 7.1 %collective-permute-start.34 = (f32[16,2048]{1,0:T(8,128)S(1)}, f32[16,2048]{1,0:T(8,128)S(1)}, u32[]{:S(2)}, u32[]{:S(2)}) collective-permute-start(f32[16,2048]{1,0:T(8,128)S(1)} %apply_upper.21), channel_id=1, source_target_pairs={{0,4},{4,0},{8,12},{12,8},{1,5},{5,1},{9,13},{13,9},{2,6},{6,2},{1... | collective-permute-start | bytes 393224 | tf_op jit(solution)/shard_map/ppermute | solution.py:145
  134.2 10.8 %collective-permute-start.27 = (f32[16,2048]{1,0:T(8,128)S(1)}, f32[16,2048]{1,0:T(8,128)S(1)}, u32[]{:S(2)}, u32[]{:S(2)}) collective-permute-start(f32[16,2048]{1,0:T(8,128)S(1)} %add.160), channel_id=1, source_target_pairs={{0,8},{4,12},{8,0},{12,4},{1,9},{5,13},{9,1},{13,5},{2,10},{6,14},... | collective-permute-start | bytes 393224 | tf_op jit(solution)/shard_map/ppermute | solution.py:145
  136.8 9.7 %collective-permute-start.35 = (f32[16,2048]{1,0:T(8,128)S(1)}, f32[16,2048]{1,0:T(8,128)S(1)}, u32[]{:S(2)}, u32[]{:S(2)}) collective-permute-start(f32[16,2048]{1,0:T(8,128)S(1)} %add.169), channel_id=1, source_target_pairs={{0,8},{4,12},{8,0},{12,4},{1,9},{5,13},{9,1},{13,5},{2,10},{6,14},... | collective-permute-start | bytes 393224 | tf_op jit(solution)/shard_map/ppermute | solution.py:145
  148.2 6.4 %collective-permute-start.29 = (f32[16,2048]{1,0:T(8,128)S(1)}, f32[16,2048]{1,0:T(8,128)S(1)}, u32[]{:S(2)}, u32[]{:S(2)}) collective-permute-start(f32[16,2048]{1,0:T(8,128)S(1)} %add.163), channel_id=1, source_target_pairs={{0,2},{1,3},{2,0},{3,1},{4,6},{5,7},{6,4},{7,5},{8,10},{9,11},{10,... | collective-permute-start | bytes 393224 | tf_op jit(solution)/shard_map/ppermute | solution.py:145
  149.9 6.7 %collective-permute-start.37 = (f32[16,2048]{1,0:T(8,128)S(1)}, f32[16,2048]{1,0:T(8,128)S(1)}, u32[]{:S(2)}, u32[]{:S(2)}) collective-permute-start(f32[16,2048]{1,0:T(8,128)S(1)} %add.172), channel_id=1, source_target_pairs={{0,2},{1,3},{2,0},{3,1},{4,6},{5,7},{6,4},{7,5},{8,10},{9,11},{10,... | collective-permute-start | bytes 393224 | tf_op jit(solution)/shard_map/ppermute | solution.py:145
  155.9 7.7 %collective-permute-start.30 = (f32[16,2048]{1,0:T(8,128)S(1)}, f32[16,2048]{1,0:T(8,128)S(1)}, u32[]{:S(2)}, u32[]{:S(2)}) collective-permute-start(f32[16,2048]{1,0:T(8,128)S(1)} %apply_upper.19), channel_id=1, source_target_pairs={{0,4},{4,0},{8,12},{12,8},{1,5},{5,1},{9,13},{13,9},{2,6},{6,2},{1... | collective-permute-start | bytes 393224 | tf_op jit(solution)/shard_map/ppermute | solution.py:145
  157.8 7.3 %collective-permute-start.38 = (f32[16,2048]{1,0:T(8,128)S(1)}, f32[16,2048]{1,0:T(8,128)S(1)}, u32[]{:S(2)}, u32[]{:S(2)}) collective-permute-start(f32[16,2048]{1,0:T(8,128)S(1)} %apply_upper.23), channel_id=1, source_target_pairs={{0,4},{4,0},{8,12},{12,8},{1,5},{5,1},{9,13},{13,9},{2,6},{6,2},{1... | collective-permute-start | bytes 393224 | tf_op jit(solution)/shard_map/ppermute | solution.py:145
  163.6 10.0 %collective-permute-start.31 = (f32[16,2048]{1,0:T(8,128)S(1)}, f32[16,2048]{1,0:T(8,128)S(1)}, u32[]{:S(2)}, u32[]{:S(2)}) collective-permute-start(f32[16,2048]{1,0:T(8,128)S(1)} %add.165), channel_id=1, source_target_pairs={{0,8},{4,12},{8,0},{12,4},{1,9},{5,13},{9,1},{13,5},{2,10},{6,14},... | collective-permute-start | bytes 393224 | tf_op jit(solution)/shard_map/ppermute | solution.py:145
  165.1 9.9 %collective-permute-start.39 = (f32[16,2048]{1,0:T(8,128)S(1)}, f32[16,2048]{1,0:T(8,128)S(1)}, u32[]{:S(2)}, u32[]{:S(2)}) collective-permute-start(f32[16,2048]{1,0:T(8,128)S(1)} %add.174), channel_id=1, source_target_pairs={{0,8},{4,12},{8,0},{12,4},{1,9},{5,13},{9,1},{13,5},{2,10},{6,14},... | collective-permute-start | bytes 393224 | tf_op jit(solution)/shard_map/ppermute | solution.py:145
  (10 other events, 42.8 us)

commit v3 on v0

v3 whole, which is shorter than its diff:
```python
import functools
from typing import NamedTuple

import jax
import jax.numpy as jnp
from jax import lax
from jax.experimental import pallas as pl
from jax.experimental.pallas import tpu as pltpu
from jax.sharding import PartitionSpec as P

LEVELS = 3
COPIES = 8
AHEAD = 2
LANES = 128
DIRECT_MAX = 8
IN_VMEM = pl.BlockSpec(memory_space=pltpu.VMEM)
IN_HBM = pl.BlockSpec(memory_space=pltpu.HBM)
SHORT = pl.CostEstimate(flops=0, transcendentals=0, bytes_accessed=0)
LOWER = (((1,), (1,)), ((), ()))
UPPER = (((1,), (0,)), ((), ()))


def pair_index(high, low):
    return high * (high - 1) // 2 + low


def power_of_two(size):
    return size & (size - 1) == 0


class Piece(NamedTuple):
    axis: str
    away: int
    parts: int

    def span(self, extent):
        width = extent // self.parts
        own = lax.axis_index(self.axis) % self.parts
        return pl.ds(pl.multiple_of((own ^ self.away) * width, LANES), width)


class Job(NamedTuple):
    vectors: list
    places: list
    block: jax.Array
    dims: tuple
    given: list
    outs: list


def in_hbm(blocks):
    return pltpu.with_memory_space_constraint(blocks, pltpu.HBM)


def block_copies(blocks_ref, out_ref, sems, index):
    height = out_ref.shape[0] // COPIES
    return [
        pltpu.make_async_copy(
            blocks_ref.at[index, pl.ds(i * height, height), :],
            out_ref.at[pl.ds(i * height, height), :],
            sems.at[i],
        )
        for i in range(COPIES)
    ]


def work(job, bring):
    operands, in_specs, out_shape, scratch = [], [], [], []
    if job:
        operands += [*job.vectors, *(job.given or ()), job.block]
        in_specs += [IN_VMEM] * len(operands)
        extent = job.block.shape[0 if job.dims is LOWER else 1]
        depth = job.block.shape[1 if job.dims is LOWER else 0]
        rows = job.vectors[0].shape[0]
        out_shape += [
            jax.ShapeDtypeStruct((rows, extent // out.parts), jnp.float32) for out in job.outs
        ]
    if bring:
        operands.append(in_hbm(bring[0]))
        in_specs.append(IN_HBM)
        out_shape.append(jax.ShapeDtypeStruct(bring[0].shape[1:], bring[0].dtype))
        scratch.append(pltpu.SemaphoreType.DMA((COPIES,)))

    def kernel(*refs):
        ins, refs = refs[: len(operands)], refs[len(operands) :]
        outs, refs = refs[: len(out_shape)], refs[len(out_shape) :]
        copies = block_copies(ins[-1], outs[-1], refs[0], bring[1]) if bring else []
        for copy in copies:
            copy.start()
        if job:
            count = len(job.vectors)
            vectors = [ref[...].astype(jnp.bfloat16) for ref in ins[:count]]
            block_ref = ins[count + len(job.given or ())]
            for j, out in enumerate(job.outs):
                total = ins[count + j][...] if job.given else None
                for vector, place in zip(vectors, job.places):
                    inner, outer = place.span(depth), out.span(extent)
                    part = block_ref[outer, inner] if job.dims is LOWER else block_ref[inner, outer]
                    term = lax.dot_general(
                        vector, part, job.dims, preferred_element_type=jnp.float32
                    )
                    total = term if total is None else total + term
                outs[j][...] = total
        for copy in copies:
            copy.wait()

    return pl.pallas_call(
        kernel,
        out_shape=out_shape,
        in_specs=in_specs,
        out_specs=[IN_VMEM] * len(out_shape),
        scratch_shapes=scratch,
        compiler_params=pltpu.CompilerParams(vmem_limit_bytes=2 << 20),
        cost_estimate=SHORT,
        name=("products" if job else "fetch") + ("_fetch" if job and bring else ""),
    )(*operands)


def begin(selector, loads, blocks, out):
    rows, cols = blocks.shape[1:]
    height = rows // out.parts
    copies_of = COPIES // out.parts
    piece = height // copies_of

    def kernel(selector_ref, loads_ref, blocks_ref, out_ref, block_ref, sems):
        start = out.span(rows).start
        copies = [
            pltpu.make_async_copy(
                blocks_ref.at[0, pl.ds(pl.multiple_of(start + i * piece, LANES), piece), :],
                block_ref.at[pl.ds(i * piece, piece), :],
                sems.at[i],
            )
            for i in range(copies_of)
        ]
        for copy in copies[:AHEAD]:
            copy.start()
        vector = jnp.dot(selector_ref[...], loads_ref[0], preferred_element_type=jnp.float32)
        vector_bf = vector.astype(jnp.bfloat16)
        for i, copy in enumerate(copies):
            copy.wait()
            if i + AHEAD < copies_of:
                copies[i + AHEAD].start()
            span = slice(i * piece, (i + 1) * piece)
            out_ref[:, span] = lax.dot_general(
                vector_bf, block_ref[span, :], LOWER, preferred_element_type=jnp.float32
            )

    return pl.pallas_call(
        kernel,
        out_shape=jax.ShapeDtypeStruct((selector.shape[0], height), jnp.float32),
        in_specs=[IN_VMEM, IN_VMEM, IN_HBM],
        out_specs=IN_VMEM,
        scratch_shapes=[
            pltpu.VMEM((height, cols), blocks.dtype),
            pltpu.SemaphoreType.DMA((copies_of,)),
        ],
        compiler_params=pltpu.CompilerParams(vmem_limit_bytes=6 << 20),
        cost_estimate=SHORT,
        name="begin",
    )(selector, loads, in_hbm(blocks))


def select(selector, loads, out):
    def kernel(selector_ref, loads_ref, *out_refs):
        for level, out_ref in enumerate(out_refs, 1):
            out_ref[...] = jnp.dot(
                selector_ref[...],
                loads_ref[level, :, out.span(loads.shape[2])],
                preferred_element_type=jnp.float32,
            )

    shape = jax.ShapeDtypeStruct((selector.shape[0], loads.shape[2] // out.parts), jnp.float32)
    return pl.pallas_call(
        kernel,
        out_shape=[shape] * (LEVELS - 1),
        in_specs=[IN_VMEM, IN_VMEM],
        out_specs=[IN_VMEM] * (LEVELS - 1),
        compiler_params=pltpu.CompilerParams(vmem_limit_bytes=2 << 20),
        cost_estimate=SHORT,
        name="select",
    )(selector, loads)


def place(levels, pieces, places, width, held):
    rows = pieces[0].shape[0]

    def kernel(*refs):
        out_ref, sems = refs[-2:]
        copies = []
        for i, ref in enumerate(refs[: len(pieces)]):
            which, j = divmod(i, len(places))
            target = out_ref.at[levels[which], :, places[j].span(width)]
            copies.append(pltpu.make_async_copy(ref, target, sems.at[i]))
        for copy in copies:
            copy.start()
        for copy in copies:
            copy.wait()

    return pl.pallas_call(
        kernel,
        out_shape=jax.ShapeDtypeStruct((LEVELS, rows, width), jnp.float32),
        in_specs=[IN_VMEM] * len(pieces) + [IN_HBM] * len(held),
        out_specs=IN_HBM,
        scratch_shapes=[pltpu.SemaphoreType.DMA((len(pieces),))],
        input_output_aliases={len(pieces): 0} if held else {},
        compiler_params=pltpu.CompilerParams(vmem_limit_bytes=2 << 20),
        cost_estimate=SHORT,
        name="place",
    )(*pieces, *held)


class Order:
    def __init__(self):
        self.last = ()

    def after(self, *values):
        *values, self.last = lax.optimization_barrier((*values, self.last))
        return values

    def run(self, function, *values):
        self.last = function(*self.after(*values))
        return self.last


def staged(coupling, diag_inverse, loads, selector, n_rows, n_cols):
    order = Order()
    far = list(range(n_rows - 1, n_rows // 2 - 1, -1))
    near = list(range(n_rows // 2 - 1, 0, -1))
    chunk = {k: Piece("rows", k, n_rows) for k in range(n_rows)}
    keep_half, send_half = Piece("cols", 0, 2), Piece("cols", 1, 2)
    blocks = {}

    def products(vectors, places, name, dims, given, outs, bring=None):
        def call(*values):
            job = Job(
                values[: len(vectors)], places, values[len(vectors)], dims, values[len(vectors) + 1 :], outs
            )
            return work(job, source(bring))

        result = list(order.run(call, *vectors, blocks[name], *(given or ())))
        if bring:
            blocks[bring] = result.pop()
        return result

    def source(name):
        return name and (diag_inverse if name[0] == "diag" else coupling, name[1])

    def fetch(name):
        def call():
            if name not in blocks:
                (blocks[name],) = order.run(lambda: work(None, source(name)))

        return call

    def permute(value, axis, step):
        size = n_rows if axis == "rows" else n_cols
        (value,) = order.after(value)
        return lax.ppermute(value, axis, [(i, i ^ step) for i in range(size)])

    def add(*values):
        return order.run(lambda *found: functools.reduce(jnp.add, found), *values)

    def nothing():
        pass

    def cols_sum(keep, got, filler):
        kept = add(keep, got)
        step = 2
        while step < n_cols:
            got = permute(kept, "cols", step)
            filler()
            filler = nothing
            kept = add(kept, got)
            step *= 2
        return kept

    def through_rows(kept, name, dims, given=None, filler=nothing):
        other = permute(kept, "cols", 1)
        ks = far + near + [0]
        parts = products([kept], [keep_half], name, dims, given, [chunk[k] for k in ks])
        parts = dict(zip(ks, parts))

        def finish(ks):
            return products(
                [other], [send_half], name, dims, [parts[k] for k in ks], [chunk[k] for k in ks]
            )

        (other,) = order.after(other)
        got = [permute(part, "rows", k) for k, part in zip(far, finish(far))]
        *rest, own = finish(near + [0])
        got += [permute(part, "rows", k) for k, part in zip(near, rest)]
        filler()
        return other, add(own, *got[::-1])

    def gather(own):
        return {0: own} | {k: permute(own, "rows", k) for k in far + near}

    def through_cols(pieces, name, dims, given=None, bring=None, filler=nothing):
        halves = [send_half, keep_half]
        given = products([pieces[0]], [chunk[0]], name, dims, given, halves, bring)
        for k in near:
            given = products([pieces[k]], [chunk[k]], name, dims, given, halves)
        last = [pieces[k] for k in far], [chunk[k] for k in far]
        (send,) = products(*last, name, dims, given[:1], halves[:1])
        got = permute(send, "cols", 1)
        (keep,) = products(*last, name, dims, given[1:], halves[1:])
        return cols_sum(keep, got, filler)

    assert LEVELS == 3
    pair = lambda high, low: ("coupling", pair_index(high, low))
    send = order.run(lambda a, b: begin(a, b, diag_inverse, send_half), selector, loads)
    got = permute(send, "cols", 1)
    keep = order.run(lambda a, b: begin(a, b, diag_inverse, keep_half), selector, loads)
    rhs_chunks = {}
    skipped = {}

    def skip_forward():
        ks = far + near + [0]
        skipped["forward"] = products(
            solved[0], [keep_half, send_half], pair(2, 0), LOWER, None, [chunk[k] for k in ks], pair(2, 1)
        )

    def skip_backward():
        ks = list(answers[2])
        skipped["backward"] = products(
            [answers[2][k] for k in ks], [chunk[k] for k in ks], pair(2, 0), UPPER, None,
            [send_half, keep_half],
        )

    solved, answers = {}, {}


    def prepare():
        found = order.run(lambda a, b: select(a, b, chunk[0]), selector, loads)
        rhs_chunks.update(enumerate(found, 1))
        fetch(pair(1, 0))()

    kept = cols_sum(keep, got, prepare)
    other, total = through_rows(kept, pair(1, 0), LOWER, None, fetch(("diag", 1)))
    solved[0] = [kept, other]
    pieces = gather(order.run(jnp.subtract, rhs_chunks[1], total))
    kept = through_cols(pieces, ("diag", 1), LOWER, None, pair(2, 0), skip_forward)
    other, total = through_rows(kept, pair(2, 1), LOWER, skipped["forward"], fetch(("diag", 2)))
    solved[1] = [kept, other]
    pieces = gather(order.run(jnp.subtract, rhs_chunks[2], total))
    kept = through_cols(pieces, ("diag", 2), LOWER)
    other, total = through_rows(kept, ("diag", 2), UPPER)
    solved[2] = [kept, other]
    answers[2] = gather(total)
    kept = through_cols(answers[2], pair(2, 1), UPPER, None, None, skip_backward)
    kept = order.run(jnp.subtract, solved[1][0], kept)
    forward = []

    def put_forward():
        pieces = [piece for level in range(LEVELS) for piece in solved[level]]
        width = diag_inverse.shape[1]
        halves = [keep_half, send_half]
        forward.append(
            order.run(lambda *found: place(range(LEVELS), found, halves, width, ()), *pieces)
        )

    def put_influence(levels, held):
        width = diag_inverse.shape[2]
        pieces = [answers[level][k] for level in levels for k in chunk]
        count = len(pieces)
        return order.run(
            lambda *found: place(
                levels, found[:count], list(chunk.values()), width, found[count:]
            ),
            *pieces,
            *held,
        )

    held = []
    _, total = through_rows(kept, ("diag", 1), UPPER, None, fetch(("diag", 0)))
    answers[1] = gather(total)
    kept = through_cols(answers[1], pair(1, 0), UPPER, skipped["backward"], None, put_forward)
    kept = order.run(jnp.subtract, solved[0][0], kept)
    _, total = through_rows(
        kept, ("diag", 0), UPPER, None, lambda: held.append(put_influence([2, 1], ()))
    )
    answers[0] = gather(total)
    influence = put_influence([0], held)
    forward = forward[0]
    return influence, forward


def plain(coupling, diag_inverse, rhs):
    def lower(vector, block):
        return lax.dot_general(
            vector.astype(jnp.bfloat16), block, LOWER, preferred_element_type=jnp.float32
        )

    def upper(vector, block):
        return lax.dot_general(
            vector.astype(jnp.bfloat16), block, UPPER, preferred_element_type=jnp.float32
        )

    solved, answers = {}, {}
    for level in range(LEVELS):
        resid = rhs[level]
        if level:
            terms = [lower(solved[j], coupling[pair_index(level, j)]) for j in range(level)]
            resid = resid - lax.psum(functools.reduce(jnp.add, terms), "rows")
        solved[level] = lax.psum(lower(resid, diag_inverse[level]), "cols")
    for level in range(LEVELS - 1, -1, -1):
        resid = solved[level]
        if level < LEVELS - 1:
            terms = [
                upper(answers[j], coupling[pair_index(j, level)]) for j in range(level + 1, LEVELS)
            ]
            resid = resid - lax.psum(functools.reduce(jnp.add, terms), "cols")
        answers[level] = lax.psum(upper(resid, diag_inverse[level]), "rows")
    stack = lambda found: jnp.stack([found[level] for level in range(LEVELS)])
    return stack(answers), stack(solved)


def body(coupling, diag_inverse, loads, axle_index, *, n_rows, n_cols):
    positions = loads.shape[1]
    selector = (axle_index[:, None] == jnp.arange(positions, dtype=jnp.int32)[None, :]).astype(
        jnp.bfloat16
    )
    over_rows, over_cols = diag_inverse.shape[1:]
    if (
        power_of_two(n_rows)
        and power_of_two(n_cols)
        and 1 < n_rows <= DIRECT_MAX
        and n_cols > 1
        and over_cols % (n_rows * LANES) == 0
        and over_rows % (COPIES * LANES) == 0
    ):
        return staged(coupling, diag_inverse, loads, selector, n_rows, n_cols)
    rhs = jnp.einsum("lp,kpc->klc", selector, loads, preferred_element_type=jnp.float32)
    return plain(coupling, diag_inverse, rhs)


def solution(mesh):
    placed = (
        P("groups", "cols", "rows"),
        P("groups", "rows", "cols"),
        P("groups", None, "cols"),
        P("groups"),
    )
    return jax.shard_map(
        functools.partial(body, n_rows=mesh.shape["rows"], n_cols=mesh.shape["cols"]),
        mesh=mesh,
        in_specs=placed,
        out_specs=(P("groups", None, "cols"), P("groups", None, "rows")),
        check_vma=False,
    )
```

time: 432 us -> 155 us (0.36)
  waiting for transfers between devices: 338 us -> 51.8 us
  matrix products: 74.4 us -> 0 us
  Pallas kernels: 0 us -> 54.5 us
  starting transfers between devices: 0.6 us -> 44.4 us
  between operations: 14.2 us -> 1.16 us
    psum x10 -> x0, waiting for transfers between devices: 338 us -> none  [the longest x3 105 us: backward_diag(): return lax.psum(partial_value, 'rows')]
    dot_general x13 -> x0, matrix products: 74.4 us -> none  [the longest x3 20.2 us: forward_diag(): jnp.einsum('lm,im->li', resid.astype(jnp.bfloat16), tile, preferred_eleme...]
    pallas_call x0 -> x43, Pallas kernels: none -> 54.5 us  [the longest x37 43.9 us: work(): pl.pallas_call(kernel, out_shape=out_shape, in_specs=in_specs, out_specs=...]
    ppermute x0 -> x45, waiting for transfers between devices: none -> 51.8 us  [permute(): return lax.ppermute(value, axis, [(i, i ^ step) for i in range(size)])]
    ppermute x0 -> x45, starting transfers between devices: none -> 44.4 us  [permute(): return lax.ppermute(value, axis, [(i, i ^ step) for i in range(size)])]
  transfers between devices with their start and end apart: 10 -> 45, of which waited for: 10 -> 33; matrix products, arithmetic and copies ran while one was open for 0% -> 0% of each run, Pallas kernels for 0% -> 29%
where the time goes in v3:
time: 155 us; the launch traced here: 154 us
  Pallas kernels  54.5 us (35%)
  waiting for transfers between devices  51.8 us (33%)
  starting transfers between devices  44.4 us (29%)
    ppermute x45, waiting for transfers between devices, permute(): return lax.ppermute(value, axis, [(i, i ^ step) for i in range(size)])  51.8 us
    ppermute x45, starting transfers between devices, permute(): return lax.ppermute(value, axis, [(i, i ^ step) for i in range(size)])  44.4 us
    pallas_call x37, Pallas kernels, work(): pl.pallas_call(kernel, out_shape=out_shape, in_specs=in_specs, out_specs=...  43.9 us
    pallas_call x2, Pallas kernels, begin(): pl.pallas_call(kernel, out_shape=jax.ShapeDtypeStruct((selector.shape[0],...  7.97 us
  transfers between devices with their start and end apart: 45, of which 33 were waited for; matrix products, arithmetic and copies ran while one was open for 0% of the time, Pallas kernels for 29%

profile of v3, /device:TPU:0, one launch (start us, length us, event | category | flops | bytes accessed | tf_op | source)
XLA Modules:
  0.0 154.4 jit_solution(1523282340920249976)
XLA Ops:
  2.8 4.0 %begin.3 = f32[32,1024]{1,0:T(8,128)S(1)} custom-call(bf16[32,128]{1,0:T(8,128)(2,1)S(1)} %fusion.selector_ref, bf16[3,128,2048]{2,1,0:T(8,128)(2,1)S(1)} %copy-done, bf16[3,2048,2048]{2,1,0:T(8,128)(2,1)} %refs_0_.7), custom_call_target="tpu_custom_call" | custom-call | tf_op jit(solution)/shard_map/begin/pallas_call | solution.py:148
  7.3 4.0 %begin.2 = f32[32,1024]{1,0:T(8,128)S(1)} custom-call(bf16[32,128]{1,0:T(8,128)(2,1)S(1)} %fusion.selector_ref, bf16[3,128,2048]{2,1,0:T(8,128)(2,1)S(1)} %copy-done, bf16[3,2048,2048]{2,1,0:T(8,128)(2,1)} %refs_0_.7), custom_call_target="tpu_custom_call" | custom-call | tf_op jit(solution)/shard_map/begin/pallas_call | solution.py:148
  11.3 2.6 %collective-permute-start.1 = (f32[32,1024]{1,0:T(8,128)S(1)}, f32[32,1024]{1,0:T(8,128)S(1)}, u32[]{:S(2)}, u32[]{:S(2)}) collective-permute-start(f32[32,1024]{1,0:T(8,128)S(1)} %add.75), channel_id=1, source_target_pairs={{0,2},{1,3},{2,0},{3,1},{4,6},{5,7},{6,4},{7,5},{8,10},{9,11},{10,... | collective-permute-start | bytes 393224 | tf_op jit(solution)/shard_map/ppermute | solution.py:258
  13.9 3.5 %fetch.4.refs_1_.refs_3_ = bf16[2048,2048]{1,0:T(8,128)(2,1)S(1)} custom-call(bf16[3,2048,2048]{2,1,0:T(8,128)(2,1)} %refs_3_.1), custom_call_target="tpu_custom_call" | custom-call | tf_op jit(solution)/shard_map/fetch/pallas_call | solution.py:107
  20.2 2.9 %collective-permute-start.4 = (f32[32,512]{1,0:T(8,128)S(1)}, f32[32,512]{1,0:T(8,128)S(1)}, u32[]{:S(2)}, u32[]{:S(2)}) collective-permute-start(f32[32,512]{1,0:T(8,128)S(1)} %get-tuple-element.313), channel_id=1, source_target_pairs={{0,8},{4,12},{8,0},{12,4},{1,9},{5,13},{9,1},{13,5},{2,10},{6,14},... | collective-permute-start | bytes 196616 | tf_op jit(solution)/shard_map/ppermute | solution.py:258
  25.5 3.6 %fetch.5.refs_1_.refs_3_ = bf16[2048,2048]{1,0:T(8,128)(2,1)S(1)} custom-call(bf16[3,2048,2048]{2,1,0:T(8,128)(2,1)} %refs_0_.7), custom_call_target="tpu_custom_call" | custom-call | tf_op jit(solution)/shard_map/fetch/pallas_call | solution.py:107
  31.1 3.2 %collective-permute-start.6 = (f32[32,512]{1,0:T(8,128)S(1)}, f32[32,512]{1,0:T(8,128)S(1)}, u32[]{:S(2)}, u32[]{:S(2)}) collective-permute-start(f32[32,512]{1,0:T(8,128)S(1)} %sub.12.refs_0_), channel_id=1, source_target_pairs={{0,12},{4,8},{8,4},{12,0},{1,13},{5,9},{9,5},{13,1},{2,14},{6,10},... | collective-permute-start | bytes 196616 | tf_op jit(solution)/shard_map/ppermute | solution.py:258
  34.3 3.5 %products_fetch.2 = (f32[32,1024]{1,0:T(8,128)S(1)}, f32[32,1024]{1,0:T(8,128)S(1)}, bf16[2048,2048]{1,0:T(8,128)(2,1)S(1)}) custom-call(f32[32,512]{1,0:T(8,128)S(1)} %sub.12.refs_0_, bf16[2048,2048]{1,0:T(8,128)(2,1)S(1)} %fetch.5.refs_1_.refs_3_, bf16[3,2048,2048]{2,1,0:T(8,128)(2,1)} %refs_3_.1), custom_call_target="tpu_custom_call" | custom-call | tf_op jit(solution)/shard_map/products_fetch/pallas_call | solution.py:107
  38.6 2.0 %collective-permute-done.7.refs_1_ = f32[32,512]{1,0:T(8,128)S(1)} collective-permute-done((f32[32,512]{1,0:T(8,128)S(1)}, f32[32,512]{1,0:T(8,128)S(1)}, u32[]{:S(2)}, u32[]{:S(2)}) %collective-permute-start.7) | collective-permute-done | bytes 65568 | tf_op jit(solution)/shard_map/ppermute | solution.py:258
  44.3 5.1 %products_fetch.3 = (f32[32,512]{1,0:T(8,128)S(1)}, f32[32,512]{1,0:T(8,128)S(1)}, f32[32,512]{1,0:T(8,128)S(1)}, f32[32,512]{1,0:T(8,128)S(1)}, bf16[2048,2048]{1,0:T(8,128)(2,1)S(1)}) custom-call(f32[32,1024]{1,0:T(8,128)S(1)} %add.76.refs_0_, f32[32,1024]{1,0:T(8,128)S(1)} %collective-permute-done.2.refs_0_.refs_1_, ...), custom_call_target="tpu_custom_call" | custom-call | tf_op jit(solution)/shard_map/products_fetch/pallas_call | solution.py:107
  55.9 3.5 %fetch.6.refs_1_.refs_3_ = bf16[2048,2048]{1,0:T(8,128)(2,1)S(1)} custom-call(bf16[3,2048,2048]{2,1,0:T(8,128)(2,1)} %refs_0_.7), custom_call_target="tpu_custom_call" | custom-call | tf_op jit(solution)/shard_map/fetch/pallas_call | solution.py:107
  61.8 1.9 %collective-permute-start.15 = (f32[32,512]{1,0:T(8,128)S(1)}, f32[32,512]{1,0:T(8,128)S(1)}, u32[]{:S(2)}, u32[]{:S(2)}) collective-permute-start(f32[32,512]{1,0:T(8,128)S(1)} %sub.13.refs_0_), channel_id=1, source_target_pairs={{0,12},{4,8},{8,4},{12,0},{1,13},{5,9},{9,5},{13,1},{2,14},{6,10},... | collective-permute-start | bytes 196616 | tf_op jit(solution)/shard_map/ppermute | solution.py:258
  66.2 2.0 %collective-permute-done.15.refs_0_ = f32[32,512]{1,0:T(8,128)S(1)} collective-permute-done((f32[32,512]{1,0:T(8,128)S(1)}, f32[32,512]{1,0:T(8,128)S(1)}, u32[]{:S(2)}, u32[]{:S(2)}) %collective-permute-start.15) | collective-permute-done | bytes 65568 | tf_op jit(solution)/shard_map/ppermute | solution.py:258
  68.2 2.7 %collective-permute-done.16.refs_1_ = f32[32,512]{1,0:T(8,128)S(1)} collective-permute-done((f32[32,512]{1,0:T(8,128)S(1)}, f32[32,512]{1,0:T(8,128)S(1)}, u32[]{:S(2)}, u32[]{:S(2)}) %collective-permute-start.16) | collective-permute-done | bytes 65568 | tf_op jit(solution)/shard_map/ppermute | solution.py:258
  73.7 5.0 %collective-permute-done.19 = f32[32,1024]{1,0:T(8,128)S(1)} collective-permute-done((f32[32,1024]{1,0:T(8,128)S(1)}, f32[32,1024]{1,0:T(8,128)S(1)}, u32[]{:S(2)}, u32[]{:S(2)}) %collective-permute-start.19) | collective-permute-done | bytes 131104 | tf_op jit(solution)/shard_map/ppermute | solution.py:258
  81.1 1.9 %collective-permute-start.23 = (f32[32,512]{1,0:T(8,128)S(1)}, f32[32,512]{1,0:T(8,128)S(1)}, u32[]{:S(2)}, u32[]{:S(2)}) collective-permute-start(f32[32,512]{1,0:T(8,128)S(1)} %get-tuple-element.428), channel_id=1, source_target_pairs={{0,12},{4,8},{8,4},{12,0},{1,13},{5,9},{9,5},{13,1},{2,14},{6,10},... | collective-permute-start | bytes 196616 | tf_op jit(solution)/shard_map/ppermute | solution.py:258
  84.7 3.4 %collective-permute-done.22 = f32[32,512]{1,0:T(8,128)S(1)} collective-permute-done((f32[32,512]{1,0:T(8,128)S(1)}, f32[32,512]{1,0:T(8,128)S(1)}, u32[]{:S(2)}, u32[]{:S(2)}) %collective-permute-start.22) | collective-permute-done | bytes 65568 | tf_op jit(solution)/shard_map/ppermute | solution.py:258
  90.0 1.9 %collective-permute-start.24 = (f32[32,512]{1,0:T(8,128)S(1)}, f32[32,512]{1,0:T(8,128)S(1)}, u32[]{:S(2)}, u32[]{:S(2)}) collective-permute-start(f32[32,512]{1,0:T(8,128)S(1)} %add_add_fusion.2.refs_0_), channel_id=1, source_target_pairs={{0,12},{4,8},{8,4},{12,0},{1,13},{5,9},{9,5},{13,1},{2,14},{6,10},... | collective-permute-start | bytes 196616 | tf_op jit(solution)/shard_map/ppermute | solution.py:258
  94.2 2.3 %collective-permute-done.24.refs_0_.refs_1_.refs_3_ = f32[32,512]{1,0:T(8,128)S(1)} collective-permute-done((f32[32,512]{1,0:T(8,128)S(1)}, f32[32,512]{1,0:T(8,128)S(1)}, u32[]{:S(2)}, u32[]{:S(2)}) %collective-permute-start.24) | collective-permute-done | bytes 65568 | tf_op jit(solution)/shard_map/ppermute | solution.py:258
  96.4 2.7 %collective-permute-done.25.refs_1_.refs_2_ = f32[32,512]{1,0:T(8,128)S(1)} collective-permute-done((f32[32,512]{1,0:T(8,128)S(1)}, f32[32,512]{1,0:T(8,128)S(1)}, u32[]{:S(2)}, u32[]{:S(2)}) %collective-permute-start.25) | collective-permute-done | bytes 65568 | tf_op jit(solution)/shard_map/ppermute | solution.py:258
  103.1 3.5 %collective-permute-done.28 = f32[32,1024]{1,0:T(8,128)S(1)} collective-permute-done((f32[32,1024]{1,0:T(8,128)S(1)}, f32[32,1024]{1,0:T(8,128)S(1)}, u32[]{:S(2)}, u32[]{:S(2)}) %collective-permute-start.28) | collective-permute-done | bytes 131104 | tf_op jit(solution)/shard_map/ppermute | solution.py:258
  108.8 1.9 %collective-permute-start.32 = (f32[32,512]{1,0:T(8,128)S(1)}, f32[32,512]{1,0:T(8,128)S(1)}, u32[]{:S(2)}, u32[]{:S(2)}) collective-permute-start(f32[32,512]{1,0:T(8,128)S(1)} %get-tuple-element.485), channel_id=1, source_target_pairs={{0,12},{4,8},{8,4},{12,0},{1,13},{5,9},{9,5},{13,1},{2,14},{6,10},... | collective-permute-start | bytes 196616 | tf_op jit(solution)/shard_map/ppermute | solution.py:258
  112.5 3.5 %fetch.7.refs_1_.refs_3_ = bf16[2048,2048]{1,0:T(8,128)(2,1)S(1)} custom-call(bf16[3,2048,2048]{2,1,0:T(8,128)(2,1)} %refs_0_.7), custom_call_target="tpu_custom_call" | custom-call | tf_op jit(solution)/shard_map/fetch/pallas_call | solution.py:107
  117.8 1.9 %collective-permute-start.33 = (f32[32,512]{1,0:T(8,128)S(1)}, f32[32,512]{1,0:T(8,128)S(1)}, u32[]{:S(2)}, u32[]{:S(2)}) collective-permute-start(f32[32,512]{1,0:T(8,128)S(1)} %add_add_fusion.1.refs_0_.refs_4_), channel_id=1, source_target_pairs={{0,12},{4,8},{8,4},{12,0},{1,13},{5,9},{9,5},{13,1},{2,14},{6,10},... | collective-permute-start | bytes 196616 | tf_op jit(solution)/shard_map/ppermute | solution.py:258
  121.9 2.2 %collective-permute-done.33.refs_0_.refs_7_ = f32[32,512]{1,0:T(8,128)S(1)} collective-permute-done((f32[32,512]{1,0:T(8,128)S(1)}, f32[32,512]{1,0:T(8,128)S(1)}, u32[]{:S(2)}, u32[]{:S(2)}) %collective-permute-start.33) | collective-permute-done | bytes 65568 | tf_op jit(solution)/shard_map/ppermute | solution.py:258
  124.1 2.7 %collective-permute-done.34.refs_1_.refs_6_ = f32[32,512]{1,0:T(8,128)S(1)} collective-permute-done((f32[32,512]{1,0:T(8,128)S(1)}, f32[32,512]{1,0:T(8,128)S(1)}, u32[]{:S(2)}, u32[]{:S(2)}) %collective-permute-start.34) | collective-permute-done | bytes 65568 | tf_op jit(solution)/shard_map/ppermute | solution.py:258
  130.2 4.1 %collective-permute-done.37 = f32[32,1024]{1,0:T(8,128)S(1)} collective-permute-done((f32[32,1024]{1,0:T(8,128)S(1)}, f32[32,1024]{1,0:T(8,128)S(1)}, u32[]{:S(2)}, u32[]{:S(2)}) %collective-permute-start.37) | collective-permute-done | bytes 131104 | tf_op jit(solution)/shard_map/ppermute | solution.py:258
  136.5 1.9 %collective-permute-start.41 = (f32[32,512]{1,0:T(8,128)S(1)}, f32[32,512]{1,0:T(8,128)S(1)}, u32[]{:S(2)}, u32[]{:S(2)}) collective-permute-start(f32[32,512]{1,0:T(8,128)S(1)} %get-tuple-element.543), channel_id=1, source_target_pairs={{0,12},{4,8},{8,4},{12,0},{1,13},{5,9},{9,5},{13,1},{2,14},{6,10},... | collective-permute-start | bytes 196616 | tf_op jit(solution)/shard_map/ppermute | solution.py:258
  141.0 2.6 %collective-permute-done.40 = f32[32,512]{1,0:T(8,128)S(1)} collective-permute-done((f32[32,512]{1,0:T(8,128)S(1)}, f32[32,512]{1,0:T(8,128)S(1)}, u32[]{:S(2)}, u32[]{:S(2)}) %collective-permute-start.40) | collective-permute-done | bytes 65568 | tf_op jit(solution)/shard_map/ppermute | solution.py:258
  144.8 2.0 %collective-permute-start.44 = (f32[32,512]{1,0:T(8,128)S(1)}, f32[32,512]{1,0:T(8,128)S(1)}, u32[]{:S(2)}, u32[]{:S(2)}) collective-permute-start(f32[32,512]{1,0:T(8,128)S(1)} %add_add_fusion.refs_0_), channel_id=1, source_target_pairs={{0,12},{4,8},{8,4},{12,0},{1,13},{5,9},{9,5},{13,1},{2,14},{6,10},... | collective-permute-start | bytes 196616 | tf_op jit(solution)/shard_map/ppermute | solution.py:258
  146.8 2.4 %collective-permute-start.43 = (f32[32,512]{1,0:T(8,128)S(1)}, f32[32,512]{1,0:T(8,128)S(1)}, u32[]{:S(2)}, u32[]{:S(2)}) collective-permute-start(f32[32,512]{1,0:T(8,128)S(1)} %add_add_fusion.refs_0_), channel_id=1, source_target_pairs={{0,8},{4,12},{8,0},{12,4},{1,9},{5,13},{9,1},{13,5},{2,10},{6,14},... | collective-permute-start | bytes 196616 | tf_op jit(solution)/shard_map/ppermute | solution.py:258
  149.3 2.3 %collective-permute-done.44.refs_3_ = f32[32,512]{1,0:T(8,128)S(1)} collective-permute-done((f32[32,512]{1,0:T(8,128)S(1)}, f32[32,512]{1,0:T(8,128)S(1)}, u32[]{:S(2)}, u32[]{:S(2)}) %collective-permute-start.44) | collective-permute-done | bytes 65568 | tf_op jit(solution)/shard_map/ppermute | solution.py:258
  (125 shorter events, 60.6 us)
Async XLA Ops:
  11.3 6.7 %collective-permute-start.1 = (f32[32,1024]{1,0:T(8,128)S(1)}, f32[32,1024]{1,0:T(8,128)S(1)}, u32[]{:S(2)}, u32[]{:S(2)}) collective-permute-start(f32[32,1024]{1,0:T(8,128)S(1)} %add.75), channel_id=1, source_target_pairs={{0,2},{1,3},{2,0},{3,1},{4,6},{5,7},{6,4},{7,5},{8,10},{9,11},{10,... | collective-permute-start | bytes 393224 | tf_op jit(solution)/shard_map/ppermute | solution.py:258
  20.2 9.1 %collective-permute-start.4 = (f32[32,512]{1,0:T(8,128)S(1)}, f32[32,512]{1,0:T(8,128)S(1)}, u32[]{:S(2)}, u32[]{:S(2)}) collective-permute-start(f32[32,512]{1,0:T(8,128)S(1)} %get-tuple-element.313), channel_id=1, source_target_pairs={{0,8},{4,12},{8,0},{12,4},{1,9},{5,13},{9,1},{13,5},{2,10},{6,14},... | collective-permute-start | bytes 196616 | tf_op jit(solution)/shard_map/ppermute | solution.py:258
  23.1 6.4 %collective-permute-start.5 = (f32[32,512]{1,0:T(8,128)S(1)}, f32[32,512]{1,0:T(8,128)S(1)}, u32[]{:S(2)}, u32[]{:S(2)}) collective-permute-start(f32[32,512]{1,0:T(8,128)S(1)} %get-tuple-element.314), channel_id=1, source_target_pairs={{0,12},{4,8},{8,4},{12,0},{1,13},{5,9},{9,5},{13,1},{2,14},{6,10},... | collective-permute-start | bytes 196616 | tf_op jit(solution)/shard_map/ppermute | solution.py:258
  25.2 5.4 %collective-permute-start.3 = (f32[32,512]{1,0:T(8,128)S(1)}, f32[32,512]{1,0:T(8,128)S(1)}, u32[]{:S(2)}, u32[]{:S(2)}) collective-permute-start(f32[32,512]{1,0:T(8,128)S(1)} %get-tuple-element.308), channel_id=1, source_target_pairs={{0,4},{4,0},{8,12},{12,8},{1,5},{5,1},{9,13},{13,9},{2,6},{6,2},{1... | collective-permute-start | bytes 196616 | tf_op jit(solution)/shard_map/ppermute | solution.py:258
  30.6 7.2 %collective-permute-start.8 = (f32[32,512]{1,0:T(8,128)S(1)}, f32[32,512]{1,0:T(8,128)S(1)}, u32[]{:S(2)}, u32[]{:S(2)}) collective-permute-start(f32[32,512]{1,0:T(8,128)S(1)} %sub.12.refs_0_), channel_id=1, source_target_pairs={{0,4},{4,0},{8,12},{12,8},{1,5},{5,1},{9,13},{13,9},{2,6},{6,2},{1... | collective-permute-start | bytes 196616 | tf_op jit(solution)/shard_map/ppermute | solution.py:258
  31.1 7.5 %collective-permute-start.6 = (f32[32,512]{1,0:T(8,128)S(1)}, f32[32,512]{1,0:T(8,128)S(1)}, u32[]{:S(2)}, u32[]{:S(2)}) collective-permute-start(f32[32,512]{1,0:T(8,128)S(1)} %sub.12.refs_0_), channel_id=1, source_target_pairs={{0,12},{4,8},{8,4},{12,0},{1,13},{5,9},{9,5},{13,1},{2,14},{6,10},... | collective-permute-start | bytes 196616 | tf_op jit(solution)/shard_map/ppermute | solution.py:258
  34.3 6.3 %collective-permute-start.7 = (f32[32,512]{1,0:T(8,128)S(1)}, f32[32,512]{1,0:T(8,128)S(1)}, u32[]{:S(2)}, u32[]{:S(2)}) collective-permute-start(f32[32,512]{1,0:T(8,128)S(1)} %sub.12.refs_0_), channel_id=1, source_target_pairs={{0,8},{4,12},{8,0},{12,4},{1,9},{5,13},{9,1},{13,5},{2,10},{6,14},... | collective-permute-start | bytes 196616 | tf_op jit(solution)/shard_map/ppermute | solution.py:258
  42.7 6.7 %collective-permute-start.10 = (f32[32,1024]{1,0:T(8,128)S(1)}, f32[32,1024]{1,0:T(8,128)S(1)}, u32[]{:S(2)}, u32[]{:S(2)}) collective-permute-start(f32[32,1024]{1,0:T(8,128)S(1)} %add.80), channel_id=1, source_target_pairs={{0,2},{1,3},{2,0},{3,1},{4,6},{5,7},{6,4},{7,5},{8,10},{9,11},{10,... | collective-permute-start | bytes 393224 | tf_op jit(solution)/shard_map/ppermute | solution.py:258
  51.6 8.2 %collective-permute-start.13 = (f32[32,512]{1,0:T(8,128)S(1)}, f32[32,512]{1,0:T(8,128)S(1)}, u32[]{:S(2)}, u32[]{:S(2)}) collective-permute-start(f32[32,512]{1,0:T(8,128)S(1)} %get-tuple-element.377), channel_id=1, source_target_pairs={{0,8},{4,12},{8,0},{12,4},{1,9},{5,13},{9,1},{13,5},{2,10},{6,14},... | collective-permute-start | bytes 196616 | tf_op jit(solution)/shard_map/ppermute | solution.py:258
  52.6 7.2 %collective-permute-start.14 = (f32[32,512]{1,0:T(8,128)S(1)}, f32[32,512]{1,0:T(8,128)S(1)}, u32[]{:S(2)}, u32[]{:S(2)}) collective-permute-start(f32[32,512]{1,0:T(8,128)S(1)} %get-tuple-element.378), channel_id=1, source_target_pairs={{0,12},{4,8},{8,4},{12,0},{1,13},{5,9},{9,5},{13,1},{2,14},{6,10},... | collective-permute-start | bytes 196616 | tf_op jit(solution)/shard_map/ppermute | solution.py:258
  55.0 6.2 %collective-permute-start.12 = (f32[32,512]{1,0:T(8,128)S(1)}, f32[32,512]{1,0:T(8,128)S(1)}, u32[]{:S(2)}, u32[]{:S(2)}) collective-permute-start(f32[32,512]{1,0:T(8,128)S(1)} %get-tuple-element.372), channel_id=1, source_target_pairs={{0,4},{4,0},{8,12},{12,8},{1,5},{5,1},{9,13},{13,9},{2,6},{6,2},{1... | collective-permute-start | bytes 196616 | tf_op jit(solution)/shard_map/ppermute | solution.py:258
  61.8 6.4 %collective-permute-start.15 = (f32[32,512]{1,0:T(8,128)S(1)}, f32[32,512]{1,0:T(8,128)S(1)}, u32[]{:S(2)}, u32[]{:S(2)}) collective-permute-start(f32[32,512]{1,0:T(8,128)S(1)} %sub.13.refs_0_), channel_id=1, source_target_pairs={{0,12},{4,8},{8,4},{12,0},{1,13},{5,9},{9,5},{13,1},{2,14},{6,10},... | collective-permute-start | bytes 196616 | tf_op jit(solution)/shard_map/ppermute | solution.py:258
  63.8 7.2 %collective-permute-start.16 = (f32[32,512]{1,0:T(8,128)S(1)}, f32[32,512]{1,0:T(8,128)S(1)}, u32[]{:S(2)}, u32[]{:S(2)}) collective-permute-start(f32[32,512]{1,0:T(8,128)S(1)} %sub.13.refs_0_), channel_id=1, source_target_pairs={{0,8},{4,12},{8,0},{12,4},{1,9},{5,13},{9,1},{13,5},{2,10},{6,14},... | collective-permute-start | bytes 196616 | tf_op jit(solution)/shard_map/ppermute | solution.py:258
  73.1 5.6 %collective-permute-start.19 = (f32[32,1024]{1,0:T(8,128)S(1)}, f32[32,1024]{1,0:T(8,128)S(1)}, u32[]{:S(2)}, u32[]{:S(2)}) collective-permute-start(f32[32,1024]{1,0:T(8,128)S(1)} %add.85), channel_id=1, source_target_pairs={{0,2},{1,3},{2,0},{3,1},{4,6},{5,7},{6,4},{7,5},{8,10},{9,11},{10,... | collective-permute-start | bytes 393224 | tf_op jit(solution)/shard_map/ppermute | solution.py:258
  80.8 7.4 %collective-permute-start.22 = (f32[32,512]{1,0:T(8,128)S(1)}, f32[32,512]{1,0:T(8,128)S(1)}, u32[]{:S(2)}, u32[]{:S(2)}) collective-permute-start(f32[32,512]{1,0:T(8,128)S(1)} %get-tuple-element.427), channel_id=1, source_target_pairs={{0,8},{4,12},{8,0},{12,4},{1,9},{5,13},{9,1},{13,5},{2,10},{6,14},... | collective-permute-start | bytes 196616 | tf_op jit(solution)/shard_map/ppermute | solution.py:258
  81.1 7.1 %collective-permute-start.23 = (f32[32,512]{1,0:T(8,128)S(1)}, f32[32,512]{1,0:T(8,128)S(1)}, u32[]{:S(2)}, u32[]{:S(2)}) collective-permute-start(f32[32,512]{1,0:T(8,128)S(1)} %get-tuple-element.428), channel_id=1, source_target_pairs={{0,12},{4,8},{8,4},{12,0},{1,13},{5,9},{9,5},{13,1},{2,14},{6,10},... | collective-permute-start | bytes 196616 | tf_op jit(solution)/shard_map/ppermute | solution.py:258
  83.4 5.9 %collective-permute-start.21 = (f32[32,512]{1,0:T(8,128)S(1)}, f32[32,512]{1,0:T(8,128)S(1)}, u32[]{:S(2)}, u32[]{:S(2)}) collective-permute-start(f32[32,512]{1,0:T(8,128)S(1)} %get-tuple-element.422), channel_id=1, source_target_pairs={{0,4},{4,0},{8,12},{12,8},{1,5},{5,1},{9,13},{13,9},{2,6},{6,2},{1... | collective-permute-start | bytes 196616 | tf_op jit(solution)/shard_map/ppermute | solution.py:258
  90.0 6.4 %collective-permute-start.24 = (f32[32,512]{1,0:T(8,128)S(1)}, f32[32,512]{1,0:T(8,128)S(1)}, u32[]{:S(2)}, u32[]{:S(2)}) collective-permute-start(f32[32,512]{1,0:T(8,128)S(1)} %add_add_fusion.2.refs_0_), channel_id=1, source_target_pairs={{0,12},{4,8},{8,4},{12,0},{1,13},{5,9},{9,5},{13,1},{2,14},{6,10},... | collective-permute-start | bytes 196616 | tf_op jit(solution)/shard_map/ppermute | solution.py:258
  92.0 7.2 %collective-permute-start.25 = (f32[32,512]{1,0:T(8,128)S(1)}, f32[32,512]{1,0:T(8,128)S(1)}, u32[]{:S(2)}, u32[]{:S(2)}) collective-permute-start(f32[32,512]{1,0:T(8,128)S(1)} %add_add_fusion.2.refs_0_), channel_id=1, source_target_pairs={{0,8},{4,12},{8,0},{12,4},{1,9},{5,13},{9,1},{13,5},{2,10},{6,14},... | collective-permute-start | bytes 196616 | tf_op jit(solution)/shard_map/ppermute | solution.py:258
  101.0 5.6 %collective-permute-start.28 = (f32[32,1024]{1,0:T(8,128)S(1)}, f32[32,1024]{1,0:T(8,128)S(1)}, u32[]{:S(2)}, u32[]{:S(2)}) collective-permute-start(f32[32,1024]{1,0:T(8,128)S(1)} %add.90), channel_id=1, source_target_pairs={{0,2},{1,3},{2,0},{3,1},{4,6},{5,7},{6,4},{7,5},{8,10},{9,11},{10,... | collective-permute-start | bytes 393224 | tf_op jit(solution)/shard_map/ppermute | solution.py:258
  108.5 7.5 %collective-permute-start.31 = (f32[32,512]{1,0:T(8,128)S(1)}, f32[32,512]{1,0:T(8,128)S(1)}, u32[]{:S(2)}, u32[]{:S(2)}) collective-permute-start(f32[32,512]{1,0:T(8,128)S(1)} %get-tuple-element.484), channel_id=1, source_target_pairs={{0,8},{4,12},{8,0},{12,4},{1,9},{5,13},{9,1},{13,5},{2,10},{6,14},... | collective-permute-start | bytes 196616 | tf_op jit(solution)/shard_map/ppermute | solution.py:258
  108.8 7.2 %collective-permute-start.32 = (f32[32,512]{1,0:T(8,128)S(1)}, f32[32,512]{1,0:T(8,128)S(1)}, u32[]{:S(2)}, u32[]{:S(2)}) collective-permute-start(f32[32,512]{1,0:T(8,128)S(1)} %get-tuple-element.485), channel_id=1, source_target_pairs={{0,12},{4,8},{8,4},{12,0},{1,13},{5,9},{9,5},{13,1},{2,14},{6,10},... | collective-permute-start | bytes 196616 | tf_op jit(solution)/shard_map/ppermute | solution.py:258
  111.2 5.9 %collective-permute-start.30 = (f32[32,512]{1,0:T(8,128)S(1)}, f32[32,512]{1,0:T(8,128)S(1)}, u32[]{:S(2)}, u32[]{:S(2)}) collective-permute-start(f32[32,512]{1,0:T(8,128)S(1)} %get-tuple-element.479), channel_id=1, source_target_pairs={{0,4},{4,0},{8,12},{12,8},{1,5},{5,1},{9,13},{13,9},{2,6},{6,2},{1... | collective-permute-start | bytes 196616 | tf_op jit(solution)/shard_map/ppermute | solution.py:258
  117.8 6.3 %collective-permute-start.33 = (f32[32,512]{1,0:T(8,128)S(1)}, f32[32,512]{1,0:T(8,128)S(1)}, u32[]{:S(2)}, u32[]{:S(2)}) collective-permute-start(f32[32,512]{1,0:T(8,128)S(1)} %add_add_fusion.1.refs_0_.refs_4_), channel_id=1, source_target_pairs={{0,12},{4,8},{8,4},{12,0},{1,13},{5,9},{9,5},{13,1},{2,14},{6,10},... | collective-permute-start | bytes 196616 | tf_op jit(solution)/shard_map/ppermute | solution.py:258
  119.7 7.2 %collective-permute-start.34 = (f32[32,512]{1,0:T(8,128)S(1)}, f32[32,512]{1,0:T(8,128)S(1)}, u32[]{:S(2)}, u32[]{:S(2)}) collective-permute-start(f32[32,512]{1,0:T(8,128)S(1)} %add_add_fusion.1.refs_0_.refs_4_), channel_id=1, source_target_pairs={{0,8},{4,12},{8,0},{12,4},{1,9},{5,13},{9,1},{13,5},{2,10},{6,14},... | collective-permute-start | bytes 196616 | tf_op jit(solution)/shard_map/ppermute | solution.py:258
  128.7 5.6 %collective-permute-start.37 = (f32[32,1024]{1,0:T(8,128)S(1)}, f32[32,1024]{1,0:T(8,128)S(1)}, u32[]{:S(2)}, u32[]{:S(2)}) collective-permute-start(f32[32,1024]{1,0:T(8,128)S(1)} %add.95), channel_id=1, source_target_pairs={{0,2},{1,3},{2,0},{3,1},{4,6},{5,7},{6,4},{7,5},{8,10},{9,11},{10,... | collective-permute-start | bytes 393224 | tf_op jit(solution)/shard_map/ppermute | solution.py:258
  136.2 7.4 %collective-permute-start.40 = (f32[32,512]{1,0:T(8,128)S(1)}, f32[32,512]{1,0:T(8,128)S(1)}, u32[]{:S(2)}, u32[]{:S(2)}) collective-permute-start(f32[32,512]{1,0:T(8,128)S(1)} %get-tuple-element.542), channel_id=1, source_target_pairs={{0,8},{4,12},{8,0},{12,4},{1,9},{5,13},{9,1},{13,5},{2,10},{6,14},... | collective-permute-start | bytes 196616 | tf_op jit(solution)/shard_map/ppermute | solution.py:258
  136.5 7.1 %collective-permute-start.41 = (f32[32,512]{1,0:T(8,128)S(1)}, f32[32,512]{1,0:T(8,128)S(1)}, u32[]{:S(2)}, u32[]{:S(2)}) collective-permute-start(f32[32,512]{1,0:T(8,128)S(1)} %get-tuple-element.543), channel_id=1, source_target_pairs={{0,12},{4,8},{8,4},{12,0},{1,13},{5,9},{9,5},{13,1},{2,14},{6,10},... | collective-permute-start | bytes 196616 | tf_op jit(solution)/shard_map/ppermute | solution.py:258
  138.9 5.9 %collective-permute-start.39 = (f32[32,512]{1,0:T(8,128)S(1)}, f32[32,512]{1,0:T(8,128)S(1)}, u32[]{:S(2)}, u32[]{:S(2)}) collective-permute-start(f32[32,512]{1,0:T(8,128)S(1)} %get-tuple-element.537), channel_id=1, source_target_pairs={{0,4},{4,0},{8,12},{12,8},{1,5},{5,1},{9,13},{13,9},{2,6},{6,2},{1... | collective-permute-start | bytes 196616 | tf_op jit(solution)/shard_map/ppermute | solution.py:258
  144.8 6.7 %collective-permute-start.44 = (f32[32,512]{1,0:T(8,128)S(1)}, f32[32,512]{1,0:T(8,128)S(1)}, u32[]{:S(2)}, u32[]{:S(2)}) collective-permute-start(f32[32,512]{1,0:T(8,128)S(1)} %add_add_fusion.refs_0_), channel_id=1, source_target_pairs={{0,12},{4,8},{8,4},{12,0},{1,13},{5,9},{9,5},{13,1},{2,14},{6,10},... | collective-permute-start | bytes 196616 | tf_op jit(solution)/shard_map/ppermute | solution.py:258
  146.8 6.5 %collective-permute-start.42 = (f32[32,512]{1,0:T(8,128)S(1)}, f32[32,512]{1,0:T(8,128)S(1)}, u32[]{:S(2)}, u32[]{:S(2)}) collective-permute-start(f32[32,512]{1,0:T(8,128)S(1)} %add_add_fusion.refs_0_), channel_id=1, source_target_pairs={{0,4},{4,0},{8,12},{12,8},{1,5},{5,1},{9,13},{13,9},{2,6},{6,2},{1... | collective-permute-start | bytes 196616 | tf_op jit(solution)/shard_map/ppermute | solution.py:258
  146.8 6.7 %collective-permute-start.43 = (f32[32,512]{1,0:T(8,128)S(1)}, f32[32,512]{1,0:T(8,128)S(1)}, u32[]{:S(2)}, u32[]{:S(2)}) collective-permute-start(f32[32,512]{1,0:T(8,128)S(1)} %add_add_fusion.refs_0_), channel_id=1, source_target_pairs={{0,8},{4,12},{8,0},{12,4},{1,9},{5,13},{9,1},{13,5},{2,10},{6,14},... | collective-permute-start | bytes 196616 | tf_op jit(solution)/shard_map/ppermute | solution.py:258
  (15 other events, 35.5 us)

commit v4 on v3

v4 whole, which is shorter than its diff:
```python
import functools
from typing import NamedTuple

import jax
import jax.numpy as jnp
from jax import lax
from jax.experimental import pallas as pl
from jax.experimental.pallas import tpu as pltpu
from jax.sharding import PartitionSpec as P

LEVELS = 3
COPIES = 8
LANES = 128
CHUNKS = 2
IN_VMEM = pl.BlockSpec(memory_space=pltpu.VMEM)
IN_HBM = pl.BlockSpec(memory_space=pltpu.HBM)
SHORT = pl.CostEstimate(flops=0, transcendentals=0, bytes_accessed=0)
LOWER = (((1,), (1,)), ((), ()))
UPPER = (((1,), (0,)), ((), ()))


def pair_index(high, low):
    return high * (high - 1) // 2 + low


def power_of_two(size):
    return size & (size - 1) == 0


class Part(NamedTuple):
    axis: str
    away: int
    chunk: int = 0
    chunks: int = 1

    def span(self, extent):
        width = extent // 2
        at = lax.axis_index(self.axis)
        if self.axis == "rows":
            at = at ^ (at >> 1)
        inner = width // self.chunks
        start = ((at & 1) ^ self.away) * width + self.chunk * inner
        return pl.ds(pl.multiple_of(start, LANES), inner)

    def width(self, extent):
        return extent // (2 * self.chunks)


class Whole(NamedTuple):
    def span(self, extent):
        return pl.ds(0, extent)


class Job(NamedTuple):
    vectors: list
    places: list
    block: jax.Array
    dims: tuple
    given: list
    outs: list


def in_hbm(blocks):
    return pltpu.with_memory_space_constraint(blocks, pltpu.HBM)


def block_copies(blocks_ref, out_ref, sems, index):
    height = out_ref.shape[0] // COPIES
    return [
        pltpu.make_async_copy(
            blocks_ref.at[index, pl.ds(i * height, height), :],
            out_ref.at[pl.ds(i * height, height), :],
            sems.at[i],
        )
        for i in range(COPIES)
    ]


def work(job, bring):
    operands, in_specs, out_shape, scratch = [], [], [], []
    if job:
        operands += [*job.vectors, *(job.given or ()), job.block]
        in_specs += [IN_VMEM] * len(operands)
        extent = job.block.shape[0 if job.dims is LOWER else 1]
        depth = job.block.shape[1 if job.dims is LOWER else 0]
        rows = job.vectors[0].shape[0]
        out_shape += [
            jax.ShapeDtypeStruct((rows, out.width(extent)), jnp.float32) for out in job.outs
        ]
    if bring:
        operands.append(in_hbm(bring[0]))
        in_specs.append(IN_HBM)
        out_shape.append(jax.ShapeDtypeStruct(bring[0].shape[1:], bring[0].dtype))
        scratch.append(pltpu.SemaphoreType.DMA((COPIES,)))

    def kernel(*refs):
        ins, refs = refs[: len(operands)], refs[len(operands) :]
        outs, refs = refs[: len(out_shape)], refs[len(out_shape) :]
        copies = block_copies(ins[-1], outs[-1], refs[0], bring[1]) if bring else []
        for copy in copies:
            copy.start()
        if job:
            count = len(job.vectors)
            vectors = [ref[...].astype(jnp.bfloat16) for ref in ins[:count]]
            block_ref = ins[count + len(job.given or ())]
            for j, out in enumerate(job.outs):
                total = ins[count + j][...] if job.given else None
                for vector, place in zip(vectors, job.places):
                    inner, outer = place.span(depth), out.span(extent)
                    part = block_ref[outer, inner] if job.dims is LOWER else block_ref[inner, outer]
                    term = lax.dot_general(
                        vector, part, job.dims, preferred_element_type=jnp.float32
                    )
                    total = term if total is None else total + term
                outs[j][...] = total
        for copy in copies:
            copy.wait()

    return pl.pallas_call(
        kernel,
        out_shape=out_shape,
        in_specs=in_specs,
        out_specs=[IN_VMEM] * len(out_shape),
        scratch_shapes=scratch,
        compiler_params=pltpu.CompilerParams(vmem_limit_bytes=2 << 20),
        cost_estimate=SHORT,
        name=("products" if job else "fetch") + ("_fetch" if job and bring else ""),
    )(*operands)


def begin(axle_index, loads, blocks, out):
    rows, cols = blocks.shape[1:]
    height = rows // 2
    count, positions = axle_index.shape[0], loads.shape[1]
    piece = rows // COPIES
    first = height // piece

    def kernel(index_ref, loads_ref, blocks_ref, *refs):
        selector_ref, vector_ref, part_ref, block_ref, index, table, small_sems, sems = refs
        start = out.span(rows).start
        spans = [
            pl.ds(pl.multiple_of((start + i * piece) % rows, piece), piece) for i in range(COPIES)
        ]
        copies = [
            pltpu.make_async_copy(blocks_ref.at[0, span, :], block_ref.at[span, :], sems.at[i])
            for i, span in enumerate(spans)
        ]
        small = [
            pltpu.make_async_copy(index_ref, index, small_sems.at[0]),
            pltpu.make_async_copy(loads_ref.at[0], table, small_sems.at[1]),
        ]
        for copy in small + copies[:first]:
            copy.start()
        for copy in small:
            copy.wait()
        line = lax.broadcasted_iota(jnp.int32, (count, positions), 0)
        wanted = jnp.zeros((count, positions), jnp.int32)
        for i in range(count):
            wanted = jnp.where(line == i, index[i], wanted)
        here = lax.broadcasted_iota(jnp.int32, (count, positions), 1)
        selector = jnp.where(wanted == here, 1.0, 0.0)
        selector_ref[...] = selector
        vector = jnp.dot(
            selector.astype(loads.dtype), table[...], preferred_element_type=jnp.float32
        )
        vector_ref[...] = vector
        for copy in copies[:first]:
            copy.wait()
        for copy in copies[first:]:
            copy.start()
        part_ref[...] = lax.dot_general(
            vector.astype(blocks.dtype),
            block_ref[pl.ds(pl.multiple_of(start, LANES), height), :],
            LOWER,
            preferred_element_type=jnp.float32,
        )
        for copy in copies[first:]:
            copy.wait()

    return pl.pallas_call(
        kernel,
        out_shape=(
            jax.ShapeDtypeStruct((count, positions), jnp.float32),
            jax.ShapeDtypeStruct((count, cols), jnp.float32),
            jax.ShapeDtypeStruct((count, height), jnp.float32),
            jax.ShapeDtypeStruct((rows, cols), blocks.dtype),
        ),
        in_specs=[IN_HBM] * 3,
        out_specs=[IN_VMEM] * 4,
        scratch_shapes=[
            pltpu.SMEM((count,), jnp.int32),
            pltpu.VMEM((positions, cols), loads.dtype),
            pltpu.SemaphoreType.DMA((2,)),
            pltpu.SemaphoreType.DMA((COPIES,)),
        ],
        compiler_params=pltpu.CompilerParams(vmem_limit_bytes=3 << 20),
        cost_estimate=SHORT,
        name="begin",
    )(in_hbm(axle_index), in_hbm(loads), in_hbm(blocks))


def select(selector, loads, outs):
    found = [(level, out) for level, parts in outs.items() for out in parts]

    def kernel(selector_ref, loads_ref, *out_refs):
        for (level, out), out_ref in zip(found, out_refs):
            out_ref[...] = jnp.dot(
                selector_ref[...].astype(loads.dtype),
                loads_ref[level, :, out.span(loads.shape[2])],
                preferred_element_type=jnp.float32,
            )

    result = pl.pallas_call(
        kernel,
        out_shape=[
            jax.ShapeDtypeStruct((selector.shape[0], out.width(loads.shape[2])), jnp.float32)
            for _, out in found
        ],
        in_specs=[IN_VMEM, IN_VMEM],
        out_specs=[IN_VMEM] * len(found),
        compiler_params=pltpu.CompilerParams(vmem_limit_bytes=2 << 20),
        cost_estimate=SHORT,
        name="select",
    )(selector, loads)
    return {key: [r for (level, _), r in zip(found, result) if level == key] for key in outs}


def place(pieces, targets, width, held):
    rows = pieces[0].shape[0]

    def kernel(*refs):
        out_ref, sems = refs[-2:]
        copies = [
            pltpu.make_async_copy(ref, out_ref.at[level, :, part.span(width)], sems.at[i])
            for i, (ref, (level, part)) in enumerate(zip(refs, targets))
        ]
        for copy in copies:
            copy.start()
        for copy in copies:
            copy.wait()

    return pl.pallas_call(
        kernel,
        out_shape=jax.ShapeDtypeStruct((LEVELS, rows, width), jnp.float32),
        in_specs=[IN_VMEM] * len(pieces) + [IN_HBM] * len(held),
        out_specs=IN_HBM,
        scratch_shapes=[pltpu.SemaphoreType.DMA((len(pieces),))],
        input_output_aliases={len(pieces): 0} if held else {},
        compiler_params=pltpu.CompilerParams(vmem_limit_bytes=2 << 20),
        cost_estimate=SHORT,
        name="place",
    )(*pieces, *held)


class Order:
    def __init__(self):
        self.last = ()

    def after(self, *values):
        *values, self.last = lax.optimization_barrier((*values, self.last))
        return values

    def run(self, function, *values):
        self.last = function(*self.after(*values))
        return self.last


def staged(coupling, diag_inverse, loads, axle_index, sizes):
    order = Order()
    blocks = {}
    steps = {axis: [1 << i for i in range(1, size.bit_length() - 1)] for axis, size in sizes.items()}
    steps["rows"] = [3 if step == 2 else step for step in steps["rows"]]

    def parts(axis, away, chunks):
        return [Part(axis, away, chunk, chunks) for chunk in range(chunks)]

    def source(name):
        return name and (diag_inverse if name[0] == "diag" else coupling, name[1])

    def products(vectors, places, name, dims, given, outs):
        count = len(vectors)

        def call(*values):
            job = Job(values[:count], places, values[count], dims, values[count + 1 :], outs)
            return work(job, None)

        return list(order.run(call, *vectors, blocks[name], *(given or ())))

    def fetch(name):
        def call():
            (blocks[name],) = order.run(lambda: work(None, source(name)))

        return call

    def permute(value, axis, step):
        (value,) = order.after(value)
        return lax.ppermute(value, axis, [(i, i ^ step) for i in range(sizes[axis])])

    def nothing():
        pass

    def phase(axis, chunks, finish, onward, early=nothing, middle=nothing, late=nothing, post=None):
        every = range(chunks)
        got = [permute(finish([i])[0], axis, 1) for i in every]
        kept = finish([chunks + i for i in every])
        early()
        for step in [*steps[axis], None]:
            sent = []
            for i in every:
                kept[i] = order.run(jnp.add, kept[i], got[i])
                if step is None and post is not None:
                    kept[i] = order.run(jnp.subtract, post()[i], kept[i])
                sent.append(permute(kept[i], axis, step or 1))
            got = sent
            if step is not None:
                middle()
                middle = nothing
        own, others = parts(axis, 0, chunks), parts(axis, 1, chunks)
        if onward is None:
            late(kept)
            return kept, got, None
        name, dims, next_chunks, given = onward
        away = "cols" if axis == "rows" else "rows"
        outs = parts(away, 1, next_chunks) + parts(away, 0, next_chunks)
        given = products(kept, own, name, dims, given and given(), outs)
        late()
        for i in every[:-1]:
            (got[i],) = order.after(got[i])
            given = products(got[i : i + 1], others[i : i + 1], name, dims, given, outs)
        (got[-1],) = order.after(got[-1])

        def rest(which):
            return products(
                got[-1:], others[-1:], name, dims, [given[i] for i in which], [outs[i] for i in which]
            )

        return kept, got, rest

    def pair(high, low):
        return "coupling", pair_index(high, low)

    chunks = {level: 1 if level == 1 else CHUNKS for level in range(1, LEVELS)}
    selector, vector, first, blocks["diag", 0] = order.run(
        lambda: begin(axle_index, loads, diag_inverse, Part("cols", 1))
    )
    rhs, solved, answers, skipped, done = {}, {}, {}, {}, {}

    def first_finish(which):
        if which == [0]:
            return [first]
        return products([vector], [Whole()], ("diag", 0), LOWER, None, [Part("cols", 0)])

    def prepare():
        del blocks["diag", 0]
        wanted = {level: parts("rows", 0, count) for level, count in chunks.items()}
        rhs.update(order.run(lambda a, b: select(a, b, wanted), selector, loads))
        fetch(pair(1, 0))()

    def skip_forward():
        outs = parts("rows", 1, CHUNKS) + parts("rows", 0, CHUNKS)
        skipped[LOWER] = products(
            sum(solved[0], []), parts("cols", 0, 1) + parts("cols", 1, 1), pair(2, 0), LOWER, None, outs
        )

    def skip_backward():
        outs = parts("cols", 1, 1) + parts("cols", 0, 1)
        places = parts("rows", 0, CHUNKS) + parts("rows", 1, CHUNKS)
        skipped[UPPER] = products(sum(answers[2], []), places, pair(2, 0), UPPER, None, outs)

    def put(found, levels, axis, count, halves=(0, 1), held=()):
        width = diag_inverse.shape[2 if axis == "rows" else 1]
        pieces = [piece for level in levels for half in halves for piece in found[level][half]]
        targets = [
            (level, part) for level in levels for half in halves for part in parts(axis, half, count)
        ]
        number = len(pieces)
        return order.run(
            lambda *values: place(values[:number], targets, width, values[number:]), *pieces, *held
        )

    def put_forward():
        done["forward"] = put(solved, range(LEVELS), "cols", 1)

    def put_early():
        done["early"] = put(answers, [2, 1], "rows", CHUNKS)

    def put_own(kept):
        done["own"] = put({0: [kept]}, [0], "rows", CHUNKS, [0], [done["early"]])

    *solved[0], finish = phase(
        "cols", 1, first_finish, (pair(1, 0), LOWER, chunks[1], None), middle=prepare
    )
    *_, finish = phase(
        "rows", chunks[1], finish, (("diag", 1), LOWER, 1, None),
        fetch(("diag", 1)), fetch(pair(2, 0)), skip_forward, lambda: rhs[1],
    )
    *solved[1], finish = phase(
        "cols", 1, finish, (pair(2, 1), LOWER, chunks[2], lambda: skipped[LOWER]),
        middle=fetch(pair(2, 1)),
    )
    *_, finish = phase(
        "rows", chunks[2], finish, (("diag", 2), LOWER, 1, None),
        middle=fetch(("diag", 2)), post=lambda: rhs[2],
    )
    *solved[2], finish = phase("cols", 1, finish, (("diag", 2), UPPER, CHUNKS, None))
    *answers[2], finish = phase("rows", CHUNKS, finish, (pair(2, 1), UPPER, 1, None))
    *_, finish = phase(
        "cols", 1, finish, (("diag", 1), UPPER, CHUNKS, None),
        middle=skip_backward, post=lambda: solved[1][0],
    )
    *answers[1], finish = phase(
        "rows", CHUNKS, finish, (pair(1, 0), UPPER, 1, lambda: skipped[UPPER]),
        middle=fetch(("diag", 0)),
    )
    *_, finish = phase(
        "cols", 1, finish, (("diag", 0), UPPER, CHUNKS, None),
        middle=put_forward, post=lambda: solved[0][0],
    )
    *answers[0], _ = phase("rows", CHUNKS, finish, None, middle=put_early, late=put_own)
    influence = put(answers, [0], "rows", CHUNKS, [1], [done["own"]])
    return influence, done["forward"]


def plain(coupling, diag_inverse, rhs):
    def lower(vector, block):
        return lax.dot_general(
            vector.astype(jnp.bfloat16), block, LOWER, preferred_element_type=jnp.float32
        )

    def upper(vector, block):
        return lax.dot_general(
            vector.astype(jnp.bfloat16), block, UPPER, preferred_element_type=jnp.float32
        )

    solved, answers = {}, {}
    for level in range(LEVELS):
        resid = rhs[level]
        if level:
            terms = [lower(solved[j], coupling[pair_index(level, j)]) for j in range(level)]
            resid = resid - lax.psum(functools.reduce(jnp.add, terms), "rows")
        solved[level] = lax.psum(lower(resid, diag_inverse[level]), "cols")
    for level in range(LEVELS - 1, -1, -1):
        resid = solved[level]
        if level < LEVELS - 1:
            terms = [
                upper(answers[j], coupling[pair_index(j, level)]) for j in range(level + 1, LEVELS)
            ]
            resid = resid - lax.psum(functools.reduce(jnp.add, terms), "cols")
        answers[level] = lax.psum(upper(resid, diag_inverse[level]), "rows")
    stack = lambda found: jnp.stack([found[level] for level in range(LEVELS)])
    return stack(answers), stack(solved)


def body(coupling, diag_inverse, loads, axle_index, *, n_rows, n_cols):
    over_rows, over_cols = diag_inverse.shape[1:]
    if (
        power_of_two(n_rows)
        and power_of_two(n_cols)
        and min(n_rows, n_cols) > 1
        and over_cols % (2 * CHUNKS * LANES) == 0
        and over_rows % (2 * LANES) == 0
    ):
        sizes = {"rows": n_rows, "cols": n_cols}
        return staged(coupling, diag_inverse, loads, axle_index, sizes)
    positions = loads.shape[1]
    selector = (axle_index[:, None] == jnp.arange(positions, dtype=jnp.int32)[None, :]).astype(
        jnp.bfloat16
    )
    rhs = jnp.einsum("lp,kpc->klc", selector, loads, preferred_element_type=jnp.float32)
    return plain(coupling, diag_inverse, rhs)


def solution(mesh):
    placed = (
        P("groups", "cols", "rows"),
        P("groups", "rows", "cols"),
        P("groups", None, "cols"),
        P("groups"),
    )
    return jax.shard_map(
        functools.partial(body, n_rows=mesh.shape["rows"], n_cols=mesh.shape["cols"]),
        mesh=mesh,
        in_specs=placed,
        out_specs=(P("groups", None, "cols"), P("groups", None, "rows")),
        check_vma=False,
    )
```

time: 155 us -> 145 us (0.935)
  waiting for transfers between devices: 51.8 us -> 39.9 us
  starting transfers between devices: 44.4 us -> 48.8 us
    ppermute x45 -> x42, waiting for transfers between devices: 51.8 us -> 39.9 us  [permute(): lax.ppermute(value, axis, [(i, i ^ step) for i in range(sizes[axis])])]
    ppermute x45 -> x42, starting transfers between devices: 44.4 us -> 48.8 us  [permute(): lax.ppermute(value, axis, [(i, i ^ step) for i in range(sizes[axis])])]
    pallas_call x3 -> x2, Pallas kernels: 8.14 us -> 4.81 us  [the longest x1 4.61 us: begin(): pl.pallas_call(kernel, out_shape=(jax.ShapeDtypeStruct((count, positions)...]
    pallas_call x37 -> x43, Pallas kernels: 43.9 us -> 47 us  [work(): pl.pallas_call(kernel, out_shape=out_shape, in_specs=in_specs, out_specs=...]
  transfers between devices with their start and end apart: 45 -> 42, of which waited for: 33 -> 29; matrix products, arithmetic and copies ran while one was open for 0% -> 0% of each run, Pallas kernels for 29% -> 32%
where the time goes in v4:
time: 145 us
  Pallas kernels  54.9 us (38%)
  starting transfers between devices  48.8 us (34%)
  waiting for transfers between devices  39.9 us (28%)
    ppermute x42, starting transfers between devices, permute(): lax.ppermute(value, axis, [(i, i ^ step) for i in range(sizes[axis])])  48.8 us
    pallas_call x43, Pallas kernels, work(): pl.pallas_call(kernel, out_shape=out_shape, in_specs=in_specs, out_specs=...  47 us
    ppermute x42, waiting for transfers between devices, permute(): lax.ppermute(value, axis, [(i, i ^ step) for i in range(sizes[axis])])  39.9 us
    pallas_call x1, Pallas kernels, begin(): pl.pallas_call(kernel, out_shape=(jax.ShapeDtypeStruct((count, positions)...  4.61 us
    pallas_call x4, Pallas kernels, place(): pl.pallas_call(kernel, out_shape=jax.ShapeDtypeStruct((LEVELS, rows, widt...  3.1 us
  transfers between devices with their start and end apart: 42, of which 29 were waited for; matrix products, arithmetic and copies ran while one was open for 0% of the time, Pallas kernels for 32%

profile of v4, /device:TPU:0, one launch (start us, length us, event | category | flops | bytes accessed | tf_op | source)
XLA Modules:
  0.0 145.3 jit_solution(7342134949651631748)
XLA Ops:
  0.6 4.6 %begin.1 = (f32[32,128]{1,0:T(8,128)S(1)}, f32[32,2048]{1,0:T(8,128)S(1)}, f32[32,1024]{1,0:T(8,128)S(1)}, bf16[2048,2048]{1,0:T(8,128)(2,1)S(1)}) custom-call(s32[32]{0:T(128)} %index_ref.1, bf16[3,128,2048]{2,1,0:T(8,128)(2,1)} %loads_ref.2, bf16[3,2048,2048]{2,1,0:T(8,128)(2,1)} %refs_0_.11), custom_call_target="tpu_custom_call" | custom-call | tf_op jit(solution)/shard_map/begin/pallas_call | solution.py:180
  7.1 2.6 %collective-permute-start.1 = (f32[32,1024]{1,0:T(8,128)S(1)}, f32[32,1024]{1,0:T(8,128)S(1)}, u32[]{:S(2)}, u32[]{:S(2)}) collective-permute-start(f32[32,1024]{1,0:T(8,128)S(1)} %add.84), channel_id=1, source_target_pairs={{0,2},{1,3},{2,0},{3,1},{4,6},{5,7},{6,4},{7,5},{8,10},{9,11},{10,... | collective-permute-start | bytes 393224 | tf_op jit(solution)/shard_map/ppermute | solution.py:297
  9.7 3.5 %fetch.6.refs_1_.refs_2_.refs_4_.refs_3_ = bf16[2048,2048]{1,0:T(8,128)(2,1)S(1)} custom-call(bf16[3,2048,2048]{2,1,0:T(8,128)(2,1)} %refs_0_.9), custom_call_target="tpu_custom_call" | custom-call | tf_op jit(solution)/shard_map/fetch/pallas_call | solution.py:119
  16.0 1.9 %collective-permute-start.3 = (f32[32,1024]{1,0:T(8,128)S(1)}, f32[32,1024]{1,0:T(8,128)S(1)}, u32[]{:S(2)}, u32[]{:S(2)}) collective-permute-start(f32[32,1024]{1,0:T(8,128)S(1)} %products.40), channel_id=1, source_target_pairs={{0,4},{4,0},{8,12},{12,8},{1,5},{5,1},{9,13},{13,9},{2,6},{6,2},{1... | collective-permute-start | bytes 393224 | tf_op jit(solution)/shard_map/ppermute | solution.py:297
  17.9 3.5 %fetch.7.refs_1_.refs_2_.refs_3_ = bf16[2048,2048]{1,0:T(8,128)(2,1)S(1)} custom-call(bf16[3,2048,2048]{2,1,0:T(8,128)(2,1)} %refs_0_.11), custom_call_target="tpu_custom_call" | custom-call | tf_op jit(solution)/shard_map/fetch/pallas_call | solution.py:119
  22.2 3.7 %collective-permute-start.4 = (f32[32,1024]{1,0:T(8,128)S(1)}, f32[32,1024]{1,0:T(8,128)S(1)}, u32[]{:S(2)}, u32[]{:S(2)}) collective-permute-start(f32[32,1024]{1,0:T(8,128)S(1)} %add.86), channel_id=1, source_target_pairs={{0,12},{4,8},{8,4},{12,0},{1,13},{5,9},{9,5},{13,1},{2,14},{6,10},... | collective-permute-start | bytes 393224 | tf_op jit(solution)/shard_map/ppermute | solution.py:297
  25.9 3.5 %fetch.8.refs_2_.refs_4_ = bf16[2048,2048]{1,0:T(8,128)(2,1)S(1)} custom-call(bf16[3,2048,2048]{2,1,0:T(8,128)(2,1)} %refs_0_.9), custom_call_target="tpu_custom_call" | custom-call | tf_op jit(solution)/shard_map/fetch/pallas_call | solution.py:119
  29.8 2.4 %collective-permute-start.5 = (f32[32,1024]{1,0:T(8,128)S(1)}, f32[32,1024]{1,0:T(8,128)S(1)}, u32[]{:S(2)}, u32[]{:S(2)}) collective-permute-start(f32[32,1024]{1,0:T(8,128)S(1)} %sub.15.refs_0_), channel_id=1, source_target_pairs={{0,4},{4,0},{8,12},{12,8},{1,5},{5,1},{9,13},{13,9},{2,6},{6,2},{1... | collective-permute-start | bytes 393224 | tf_op jit(solution)/shard_map/ppermute | solution.py:297
  33.5 2.6 %products.42 = (f32[32,512]{1,0:T(8,128)S(1)}, f32[32,512]{1,0:T(8,128)S(1)}, f32[32,512]{1,0:T(8,128)S(1)}, f32[32,512]{1,0:T(8,128)S(1)}) custom-call(f32[32,1024]{1,0:T(8,128)S(1)} %add.85.refs_0_, f32[32,1024]{1,0:T(8,128)S(1)} %collective-permute-done.2.refs_0_.refs_1_, bf16[2048,2048]{1,0:T(8,128)(2,1)S(1)} %fetch.8.refs_2_.refs_4_), custom_call_target="tpu_custom_call" | custom-call | tf_op jit(solution)/shard_map/products/pallas_call | solution.py:119
  39.8 3.5 %fetch.9.refs_5_.refs_3_.refs_2_ = bf16[2048,2048]{1,0:T(8,128)(2,1)S(1)} custom-call(bf16[3,2048,2048]{2,1,0:T(8,128)(2,1)} %refs_0_.9), custom_call_target="tpu_custom_call" | custom-call | tf_op jit(solution)/shard_map/fetch/pallas_call | solution.py:119
  50.5 2.7 %collective-permute-start.10 = (f32[32,512]{1,0:T(8,128)S(1)}, f32[32,512]{1,0:T(8,128)S(1)}, u32[]{:S(2)}, u32[]{:S(2)}) collective-permute-start(f32[32,512]{1,0:T(8,128)S(1)} %add.90), channel_id=1, source_target_pairs={{0,12},{4,8},{8,4},{12,0},{1,13},{5,9},{9,5},{13,1},{2,14},{6,10},... | collective-permute-start | bytes 196616 | tf_op jit(solution)/shard_map/ppermute | solution.py:297
  54.4 3.5 %fetch.10.refs_2_.refs_3_.refs_1_ = bf16[2048,2048]{1,0:T(8,128)(2,1)S(1)} custom-call(bf16[3,2048,2048]{2,1,0:T(8,128)(2,1)} %refs_0_.11), custom_call_target="tpu_custom_call" | custom-call | tf_op jit(solution)/shard_map/fetch/pallas_call | solution.py:119
  59.5 2.1 %collective-permute-start.11 = (f32[32,512]{1,0:T(8,128)S(1)}, f32[32,512]{1,0:T(8,128)S(1)}, u32[]{:S(2)}, u32[]{:S(2)}) collective-permute-start(f32[32,512]{1,0:T(8,128)S(1)} %sub.16.refs_1_), channel_id=1, source_target_pairs={{0,4},{4,0},{8,12},{12,8},{1,5},{5,1},{9,13},{13,9},{2,6},{6,2},{1... | collective-permute-start | bytes 196616 | tf_op jit(solution)/shard_map/ppermute | solution.py:297
  66.3 1.6 %collective-permute-start.16 = (f32[32,1024]{1,0:T(8,128)S(1)}, f32[32,1024]{1,0:T(8,128)S(1)}, u32[]{:S(2)}, u32[]{:S(2)}) collective-permute-start(f32[32,1024]{1,0:T(8,128)S(1)} %add.94), channel_id=1, source_target_pairs={{0,2},{1,3},{2,0},{3,1},{4,6},{5,7},{6,4},{7,5},{8,10},{9,11},{10,... | collective-permute-start | bytes 393224 | tf_op jit(solution)/shard_map/ppermute | solution.py:297
  67.8 4.1 %collective-permute-done.16 = f32[32,1024]{1,0:T(8,128)S(1)} collective-permute-done((f32[32,1024]{1,0:T(8,128)S(1)}, f32[32,1024]{1,0:T(8,128)S(1)}, u32[]{:S(2)}, u32[]{:S(2)}) %collective-permute-start.16) | collective-permute-done | bytes 131104 | tf_op jit(solution)/shard_map/ppermute | solution.py:297
  77.9 3.3 %collective-permute-start.22 = (f32[32,512]{1,0:T(8,128)S(1)}, f32[32,512]{1,0:T(8,128)S(1)}, u32[]{:S(2)}, u32[]{:S(2)}) collective-permute-start(f32[32,512]{1,0:T(8,128)S(1)} %add.98), channel_id=1, source_target_pairs={{0,12},{4,8},{8,4},{12,0},{1,13},{5,9},{9,5},{13,1},{2,14},{6,10},... | collective-permute-start | bytes 196616 | tf_op jit(solution)/shard_map/ppermute | solution.py:297
  81.9 2.6 %collective-permute-done.22 = f32[32,512]{1,0:T(8,128)S(1)} collective-permute-done((f32[32,512]{1,0:T(8,128)S(1)}, f32[32,512]{1,0:T(8,128)S(1)}, u32[]{:S(2)}, u32[]{:S(2)}) %collective-permute-start.22) | collective-permute-done | bytes 65568 | tf_op jit(solution)/shard_map/ppermute | solution.py:297
  85.8 1.7 %collective-permute-done.19 = f32[32,512]{1,0:T(8,128)S(1)} collective-permute-done((f32[32,512]{1,0:T(8,128)S(1)}, f32[32,512]{1,0:T(8,128)S(1)}, u32[]{:S(2)}, u32[]{:S(2)}) %collective-permute-start.19) | collective-permute-done | bytes 65568 | tf_op jit(solution)/shard_map/ppermute | solution.py:297
  89.3 2.4 %collective-permute-done.20.refs_0_.refs_3_ = f32[32,512]{1,0:T(8,128)S(1)} collective-permute-done((f32[32,512]{1,0:T(8,128)S(1)}, f32[32,512]{1,0:T(8,128)S(1)}, u32[]{:S(2)}, u32[]{:S(2)}) %collective-permute-start.20) | collective-permute-done | bytes 65568 | tf_op jit(solution)/shard_map/ppermute | solution.py:297
  96.5 2.5 %collective-permute-done.25 = f32[32,1024]{1,0:T(8,128)S(1)} collective-permute-done((f32[32,1024]{1,0:T(8,128)S(1)}, f32[32,1024]{1,0:T(8,128)S(1)}, u32[]{:S(2)}, u32[]{:S(2)}) %collective-permute-start.25) | collective-permute-done | bytes 131104 | tf_op jit(solution)/shard_map/ppermute | solution.py:297
  101.1 2.0 %collective-permute-start.27 = (f32[32,512]{1,0:T(8,128)S(1)}, f32[32,512]{1,0:T(8,128)S(1)}, u32[]{:S(2)}, u32[]{:S(2)}) collective-permute-start(f32[32,512]{1,0:T(8,128)S(1)} %products.64), channel_id=1, source_target_pairs={{0,4},{4,0},{8,12},{12,8},{1,5},{5,1},{9,13},{13,9},{2,6},{6,2},{1... | collective-permute-start | bytes 196616 | tf_op jit(solution)/shard_map/ppermute | solution.py:297
  103.6 2.1 %collective-permute-done.30 = f32[32,512]{1,0:T(8,128)S(1)} collective-permute-done((f32[32,512]{1,0:T(8,128)S(1)}, f32[32,512]{1,0:T(8,128)S(1)}, u32[]{:S(2)}, u32[]{:S(2)}) %collective-permute-start.30) | collective-permute-done | bytes 65568 | tf_op jit(solution)/shard_map/ppermute | solution.py:297
  106.9 2.8 %collective-permute-start.28 = (f32[32,512]{1,0:T(8,128)S(1)}, f32[32,512]{1,0:T(8,128)S(1)}, u32[]{:S(2)}, u32[]{:S(2)}) collective-permute-start(f32[32,512]{1,0:T(8,128)S(1)} %add.102), channel_id=1, source_target_pairs={{0,12},{4,8},{8,4},{12,0},{1,13},{5,9},{9,5},{13,1},{2,14},{6,10},... | collective-permute-start | bytes 196616 | tf_op jit(solution)/shard_map/ppermute | solution.py:297
  109.6 3.5 %fetch.11.refs_1_.refs_3_.refs_2_ = bf16[2048,2048]{1,0:T(8,128)(2,1)S(1)} custom-call(bf16[3,2048,2048]{2,1,0:T(8,128)(2,1)} %refs_0_.11), custom_call_target="tpu_custom_call" | custom-call | tf_op jit(solution)/shard_map/fetch/pallas_call | solution.py:119
  113.2 2.1 %collective-permute-start.29 = (f32[32,512]{1,0:T(8,128)S(1)}, f32[32,512]{1,0:T(8,128)S(1)}, u32[]{:S(2)}, u32[]{:S(2)}) collective-permute-start(f32[32,512]{1,0:T(8,128)S(1)} %add.103.refs_1_.refs_5_), channel_id=1, source_target_pairs={{0,4},{4,0},{8,12},{12,8},{1,5},{5,1},{9,13},{13,9},{2,6},{6,2},{1... | collective-permute-start | bytes 196616 | tf_op jit(solution)/shard_map/ppermute | solution.py:297
  119.8 1.6 %collective-permute-start.34 = (f32[32,1024]{1,0:T(8,128)S(1)}, f32[32,1024]{1,0:T(8,128)S(1)}, u32[]{:S(2)}, u32[]{:S(2)}) collective-permute-start(f32[32,1024]{1,0:T(8,128)S(1)} %add.106), channel_id=1, source_target_pairs={{0,2},{1,3},{2,0},{3,1},{4,6},{5,7},{6,4},{7,5},{8,10},{9,11},{10,... | collective-permute-start | bytes 393224 | tf_op jit(solution)/shard_map/ppermute | solution.py:297
  122.3 3.1 %collective-permute-done.34 = f32[32,1024]{1,0:T(8,128)S(1)} collective-permute-done((f32[32,1024]{1,0:T(8,128)S(1)}, f32[32,1024]{1,0:T(8,128)S(1)}, u32[]{:S(2)}, u32[]{:S(2)}) %collective-permute-start.34) | collective-permute-done | bytes 131104 | tf_op jit(solution)/shard_map/ppermute | solution.py:297
  130.0 1.6 %collective-permute-done.36 = f32[32,512]{1,0:T(8,128)S(1)} collective-permute-done((f32[32,512]{1,0:T(8,128)S(1)}, f32[32,512]{1,0:T(8,128)S(1)}, u32[]{:S(2)}, u32[]{:S(2)}) %collective-permute-start.36) | collective-permute-done | bytes 65568 | tf_op jit(solution)/shard_map/ppermute | solution.py:297
  131.6 2.4 %collective-permute-start.37 = (f32[32,512]{1,0:T(8,128)S(1)}, f32[32,512]{1,0:T(8,128)S(1)}, u32[]{:S(2)}, u32[]{:S(2)}) collective-permute-start(f32[32,512]{1,0:T(8,128)S(1)} %add.108), channel_id=1, source_target_pairs={{0,12},{4,8},{8,4},{12,0},{1,13},{5,9},{9,5},{13,1},{2,14},{6,10},... | collective-permute-start | bytes 196616 | tf_op jit(solution)/shard_map/ppermute | solution.py:297
  134.0 1.6 %collective-permute-start.40 = (f32[32,512]{1,0:T(8,128)S(1)}, f32[32,512]{1,0:T(8,128)S(1)}, u32[]{:S(2)}, u32[]{:S(2)}) collective-permute-start(f32[32,512]{1,0:T(8,128)S(1)} %add.110), channel_id=1, source_target_pairs={{0,12},{4,8},{8,4},{12,0},{1,13},{5,9},{9,5},{13,1},{2,14},{6,10},... | collective-permute-start | bytes 196616 | tf_op jit(solution)/shard_map/ppermute | solution.py:297
  136.5 1.7 %collective-permute-done.37 = f32[32,512]{1,0:T(8,128)S(1)} collective-permute-done((f32[32,512]{1,0:T(8,128)S(1)}, f32[32,512]{1,0:T(8,128)S(1)}, u32[]{:S(2)}, u32[]{:S(2)}) %collective-permute-start.37) | collective-permute-done | bytes 65568 | tf_op jit(solution)/shard_map/ppermute | solution.py:297
  142.5 2.0 %collective-permute-done.41.refs_1_ = f32[32,512]{1,0:T(8,128)S(1)} collective-permute-done((f32[32,512]{1,0:T(8,128)S(1)}, f32[32,512]{1,0:T(8,128)S(1)}, u32[]{:S(2)}, u32[]{:S(2)}) %collective-permute-start.41) | collective-permute-done | bytes 65568 | tf_op jit(solution)/shard_map/ppermute | solution.py:297
  (136 shorter events, 59.7 us)
Async XLA Ops:
  7.1 6.7 %collective-permute-start.1 = (f32[32,1024]{1,0:T(8,128)S(1)}, f32[32,1024]{1,0:T(8,128)S(1)}, u32[]{:S(2)}, u32[]{:S(2)}) collective-permute-start(f32[32,1024]{1,0:T(8,128)S(1)} %add.84), channel_id=1, source_target_pairs={{0,2},{1,3},{2,0},{3,1},{4,6},{5,7},{6,4},{7,5},{8,10},{9,11},{10,... | collective-permute-start | bytes 393224 | tf_op jit(solution)/shard_map/ppermute | solution.py:297
  16.0 6.1 %collective-permute-start.3 = (f32[32,1024]{1,0:T(8,128)S(1)}, f32[32,1024]{1,0:T(8,128)S(1)}, u32[]{:S(2)}, u32[]{:S(2)}) collective-permute-start(f32[32,1024]{1,0:T(8,128)S(1)} %products.40), channel_id=1, source_target_pairs={{0,4},{4,0},{8,12},{12,8},{1,5},{5,1},{9,13},{13,9},{2,6},{6,2},{1... | collective-permute-start | bytes 393224 | tf_op jit(solution)/shard_map/ppermute | solution.py:297
  22.2 7.6 %collective-permute-start.4 = (f32[32,1024]{1,0:T(8,128)S(1)}, f32[32,1024]{1,0:T(8,128)S(1)}, u32[]{:S(2)}, u32[]{:S(2)}) collective-permute-start(f32[32,1024]{1,0:T(8,128)S(1)} %add.86), channel_id=1, source_target_pairs={{0,12},{4,8},{8,4},{12,0},{1,13},{5,9},{9,5},{13,1},{2,14},{6,10},... | collective-permute-start | bytes 393224 | tf_op jit(solution)/shard_map/ppermute | solution.py:297
  29.8 6.3 %collective-permute-start.5 = (f32[32,1024]{1,0:T(8,128)S(1)}, f32[32,1024]{1,0:T(8,128)S(1)}, u32[]{:S(2)}, u32[]{:S(2)}) collective-permute-start(f32[32,1024]{1,0:T(8,128)S(1)} %sub.15.refs_0_), channel_id=1, source_target_pairs={{0,4},{4,0},{8,12},{12,8},{1,5},{5,1},{9,13},{13,9},{2,6},{6,2},{1... | collective-permute-start | bytes 393224 | tf_op jit(solution)/shard_map/ppermute | solution.py:297
  38.2 5.6 %collective-permute-start.7 = (f32[32,1024]{1,0:T(8,128)S(1)}, f32[32,1024]{1,0:T(8,128)S(1)}, u32[]{:S(2)}, u32[]{:S(2)}) collective-permute-start(f32[32,1024]{1,0:T(8,128)S(1)} %add.88), channel_id=1, source_target_pairs={{0,2},{1,3},{2,0},{3,1},{4,6},{5,7},{6,4},{7,5},{8,10},{9,11},{10,... | collective-permute-start | bytes 393224 | tf_op jit(solution)/shard_map/ppermute | solution.py:297
  45.7 4.7 %collective-permute-start.9 = (f32[32,512]{1,0:T(8,128)S(1)}, f32[32,512]{1,0:T(8,128)S(1)}, u32[]{:S(2)}, u32[]{:S(2)}) collective-permute-start(f32[32,512]{1,0:T(8,128)S(1)} %products.47), channel_id=1, source_target_pairs={{0,4},{4,0},{8,12},{12,8},{1,5},{5,1},{9,13},{13,9},{2,6},{6,2},{1... | collective-permute-start | bytes 196616 | tf_op jit(solution)/shard_map/ppermute | solution.py:297
  47.2 5.9 %collective-permute-start.12 = (f32[32,512]{1,0:T(8,128)S(1)}, f32[32,512]{1,0:T(8,128)S(1)}, u32[]{:S(2)}, u32[]{:S(2)}) collective-permute-start(f32[32,512]{1,0:T(8,128)S(1)} %products.48), channel_id=1, source_target_pairs={{0,4},{4,0},{8,12},{12,8},{1,5},{5,1},{9,13},{13,9},{2,6},{6,2},{1... | collective-permute-start | bytes 196616 | tf_op jit(solution)/shard_map/ppermute | solution.py:297
  50.5 7.5 %collective-permute-start.10 = (f32[32,512]{1,0:T(8,128)S(1)}, f32[32,512]{1,0:T(8,128)S(1)}, u32[]{:S(2)}, u32[]{:S(2)}) collective-permute-start(f32[32,512]{1,0:T(8,128)S(1)} %add.90), channel_id=1, source_target_pairs={{0,12},{4,8},{8,4},{12,0},{1,13},{5,9},{9,5},{13,1},{2,14},{6,10},... | collective-permute-start | bytes 196616 | tf_op jit(solution)/shard_map/ppermute | solution.py:297
  53.2 6.1 %collective-permute-start.13 = (f32[32,512]{1,0:T(8,128)S(1)}, f32[32,512]{1,0:T(8,128)S(1)}, u32[]{:S(2)}, u32[]{:S(2)}) collective-permute-start(f32[32,512]{1,0:T(8,128)S(1)} %add.92), channel_id=1, source_target_pairs={{0,12},{4,8},{8,4},{12,0},{1,13},{5,9},{9,5},{13,1},{2,14},{6,10},... | collective-permute-start | bytes 196616 | tf_op jit(solution)/shard_map/ppermute | solution.py:297
  59.4 4.3 %collective-permute-start.14 = (f32[32,512]{1,0:T(8,128)S(1)}, f32[32,512]{1,0:T(8,128)S(1)}, u32[]{:S(2)}, u32[]{:S(2)}) collective-permute-start(f32[32,512]{1,0:T(8,128)S(1)} %sub.17.refs_0_), channel_id=1, source_target_pairs={{0,4},{4,0},{8,12},{12,8},{1,5},{5,1},{9,13},{13,9},{2,6},{6,2},{1... | collective-permute-start | bytes 196616 | tf_op jit(solution)/shard_map/ppermute | solution.py:297
  59.5 4.9 %collective-permute-start.11 = (f32[32,512]{1,0:T(8,128)S(1)}, f32[32,512]{1,0:T(8,128)S(1)}, u32[]{:S(2)}, u32[]{:S(2)}) collective-permute-start(f32[32,512]{1,0:T(8,128)S(1)} %sub.16.refs_1_), channel_id=1, source_target_pairs={{0,4},{4,0},{8,12},{12,8},{1,5},{5,1},{9,13},{13,9},{2,6},{6,2},{1... | collective-permute-start | bytes 196616 | tf_op jit(solution)/shard_map/ppermute | solution.py:297
  66.3 5.6 %collective-permute-start.16 = (f32[32,1024]{1,0:T(8,128)S(1)}, f32[32,1024]{1,0:T(8,128)S(1)}, u32[]{:S(2)}, u32[]{:S(2)}) collective-permute-start(f32[32,1024]{1,0:T(8,128)S(1)} %add.94), channel_id=1, source_target_pairs={{0,2},{1,3},{2,0},{3,1},{4,6},{5,7},{6,4},{7,5},{8,10},{9,11},{10,... | collective-permute-start | bytes 393224 | tf_op jit(solution)/shard_map/ppermute | solution.py:297
  73.6 4.3 %collective-permute-start.21 = (f32[32,512]{1,0:T(8,128)S(1)}, f32[32,512]{1,0:T(8,128)S(1)}, u32[]{:S(2)}, u32[]{:S(2)}) collective-permute-start(f32[32,512]{1,0:T(8,128)S(1)} %products.56), channel_id=1, source_target_pairs={{0,4},{4,0},{8,12},{12,8},{1,5},{5,1},{9,13},{13,9},{2,6},{6,2},{1... | collective-permute-start | bytes 196616 | tf_op jit(solution)/shard_map/ppermute | solution.py:297
  75.4 5.7 %collective-permute-start.18 = (f32[32,512]{1,0:T(8,128)S(1)}, f32[32,512]{1,0:T(8,128)S(1)}, u32[]{:S(2)}, u32[]{:S(2)}) collective-permute-start(f32[32,512]{1,0:T(8,128)S(1)} %products.55), channel_id=1, source_target_pairs={{0,4},{4,0},{8,12},{12,8},{1,5},{5,1},{9,13},{13,9},{2,6},{6,2},{1... | collective-permute-start | bytes 196616 | tf_op jit(solution)/shard_map/ppermute | solution.py:297
  77.9 6.6 %collective-permute-start.22 = (f32[32,512]{1,0:T(8,128)S(1)}, f32[32,512]{1,0:T(8,128)S(1)}, u32[]{:S(2)}, u32[]{:S(2)}) collective-permute-start(f32[32,512]{1,0:T(8,128)S(1)} %add.98), channel_id=1, source_target_pairs={{0,12},{4,8},{8,4},{12,0},{1,13},{5,9},{9,5},{13,1},{2,14},{6,10},... | collective-permute-start | bytes 196616 | tf_op jit(solution)/shard_map/ppermute | solution.py:297
  81.2 6.2 %collective-permute-start.19 = (f32[32,512]{1,0:T(8,128)S(1)}, f32[32,512]{1,0:T(8,128)S(1)}, u32[]{:S(2)}, u32[]{:S(2)}) collective-permute-start(f32[32,512]{1,0:T(8,128)S(1)} %add.96), channel_id=1, source_target_pairs={{0,12},{4,8},{8,4},{12,0},{1,13},{5,9},{9,5},{13,1},{2,14},{6,10},... | collective-permute-start | bytes 196616 | tf_op jit(solution)/shard_map/ppermute | solution.py:297
  84.5 4.3 %collective-permute-start.23 = (f32[32,512]{1,0:T(8,128)S(1)}, f32[32,512]{1,0:T(8,128)S(1)}, u32[]{:S(2)}, u32[]{:S(2)}) collective-permute-start(f32[32,512]{1,0:T(8,128)S(1)} %add.99.refs_0_), channel_id=1, source_target_pairs={{0,4},{4,0},{8,12},{12,8},{1,5},{5,1},{9,13},{13,9},{2,6},{6,2},{1... | collective-permute-start | bytes 196616 | tf_op jit(solution)/shard_map/ppermute | solution.py:297
  87.4 4.3 %collective-permute-start.20 = (f32[32,512]{1,0:T(8,128)S(1)}, f32[32,512]{1,0:T(8,128)S(1)}, u32[]{:S(2)}, u32[]{:S(2)}) collective-permute-start(f32[32,512]{1,0:T(8,128)S(1)} %add.97.refs_1_), channel_id=1, source_target_pairs={{0,4},{4,0},{8,12},{12,8},{1,5},{5,1},{9,13},{13,9},{2,6},{6,2},{1... | collective-permute-start | bytes 196616 | tf_op jit(solution)/shard_map/ppermute | solution.py:297
  93.4 5.6 %collective-permute-start.25 = (f32[32,1024]{1,0:T(8,128)S(1)}, f32[32,1024]{1,0:T(8,128)S(1)}, u32[]{:S(2)}, u32[]{:S(2)}) collective-permute-start(f32[32,1024]{1,0:T(8,128)S(1)} %add.100), channel_id=1, source_target_pairs={{0,2},{1,3},{2,0},{3,1},{4,6},{5,7},{6,4},{7,5},{8,10},{9,11},{10,... | collective-permute-start | bytes 393224 | tf_op jit(solution)/shard_map/ppermute | solution.py:297
  100.8 4.9 %collective-permute-start.30 = (f32[32,512]{1,0:T(8,128)S(1)}, f32[32,512]{1,0:T(8,128)S(1)}, u32[]{:S(2)}, u32[]{:S(2)}) collective-permute-start(f32[32,512]{1,0:T(8,128)S(1)} %products.65), channel_id=1, source_target_pairs={{0,4},{4,0},{8,12},{12,8},{1,5},{5,1},{9,13},{13,9},{2,6},{6,2},{1... | collective-permute-start | bytes 196616 | tf_op jit(solution)/shard_map/ppermute | solution.py:297
  101.1 5.8 %collective-permute-start.27 = (f32[32,512]{1,0:T(8,128)S(1)}, f32[32,512]{1,0:T(8,128)S(1)}, u32[]{:S(2)}, u32[]{:S(2)}) collective-permute-start(f32[32,512]{1,0:T(8,128)S(1)} %products.64), channel_id=1, source_target_pairs={{0,4},{4,0},{8,12},{12,8},{1,5},{5,1},{9,13},{13,9},{2,6},{6,2},{1... | collective-permute-start | bytes 196616 | tf_op jit(solution)/shard_map/ppermute | solution.py:297
  105.7 7.5 %collective-permute-start.31 = (f32[32,512]{1,0:T(8,128)S(1)}, f32[32,512]{1,0:T(8,128)S(1)}, u32[]{:S(2)}, u32[]{:S(2)}) collective-permute-start(f32[32,512]{1,0:T(8,128)S(1)} %add.104), channel_id=1, source_target_pairs={{0,12},{4,8},{8,4},{12,0},{1,13},{5,9},{9,5},{13,1},{2,14},{6,10},... | collective-permute-start | bytes 196616 | tf_op jit(solution)/shard_map/ppermute | solution.py:297
  106.9 6.4 %collective-permute-start.28 = (f32[32,512]{1,0:T(8,128)S(1)}, f32[32,512]{1,0:T(8,128)S(1)}, u32[]{:S(2)}, u32[]{:S(2)}) collective-permute-start(f32[32,512]{1,0:T(8,128)S(1)} %add.102), channel_id=1, source_target_pairs={{0,12},{4,8},{8,4},{12,0},{1,13},{5,9},{9,5},{13,1},{2,14},{6,10},... | collective-permute-start | bytes 196616 | tf_op jit(solution)/shard_map/ppermute | solution.py:297
  113.1 4.3 %collective-permute-start.32 = (f32[32,512]{1,0:T(8,128)S(1)}, f32[32,512]{1,0:T(8,128)S(1)}, u32[]{:S(2)}, u32[]{:S(2)}) collective-permute-start(f32[32,512]{1,0:T(8,128)S(1)} %add.105.refs_0_.refs_4_), channel_id=1, source_target_pairs={{0,4},{4,0},{8,12},{12,8},{1,5},{5,1},{9,13},{13,9},{2,6},{6,2},{1... | collective-permute-start | bytes 196616 | tf_op jit(solution)/shard_map/ppermute | solution.py:297
  113.2 4.9 %collective-permute-start.29 = (f32[32,512]{1,0:T(8,128)S(1)}, f32[32,512]{1,0:T(8,128)S(1)}, u32[]{:S(2)}, u32[]{:S(2)}) collective-permute-start(f32[32,512]{1,0:T(8,128)S(1)} %add.103.refs_1_.refs_5_), channel_id=1, source_target_pairs={{0,4},{4,0},{8,12},{12,8},{1,5},{5,1},{9,13},{13,9},{2,6},{6,2},{1... | collective-permute-start | bytes 196616 | tf_op jit(solution)/shard_map/ppermute | solution.py:297
  119.8 5.6 %collective-permute-start.34 = (f32[32,1024]{1,0:T(8,128)S(1)}, f32[32,1024]{1,0:T(8,128)S(1)}, u32[]{:S(2)}, u32[]{:S(2)}) collective-permute-start(f32[32,1024]{1,0:T(8,128)S(1)} %add.106), channel_id=1, source_target_pairs={{0,2},{1,3},{2,0},{3,1},{4,6},{5,7},{6,4},{7,5},{8,10},{9,11},{10,... | collective-permute-start | bytes 393224 | tf_op jit(solution)/shard_map/ppermute | solution.py:297
  127.2 4.4 %collective-permute-start.36 = (f32[32,512]{1,0:T(8,128)S(1)}, f32[32,512]{1,0:T(8,128)S(1)}, u32[]{:S(2)}, u32[]{:S(2)}) collective-permute-start(f32[32,512]{1,0:T(8,128)S(1)} %products.72), channel_id=1, source_target_pairs={{0,4},{4,0},{8,12},{12,8},{1,5},{5,1},{9,13},{13,9},{2,6},{6,2},{1... | collective-permute-start | bytes 196616 | tf_op jit(solution)/shard_map/ppermute | solution.py:297
  128.9 5.1 %collective-permute-start.39 = (f32[32,512]{1,0:T(8,128)S(1)}, f32[32,512]{1,0:T(8,128)S(1)}, u32[]{:S(2)}, u32[]{:S(2)}) collective-permute-start(f32[32,512]{1,0:T(8,128)S(1)} %products.73), channel_id=1, source_target_pairs={{0,4},{4,0},{8,12},{12,8},{1,5},{5,1},{9,13},{13,9},{2,6},{6,2},{1... | collective-permute-start | bytes 196616 | tf_op jit(solution)/shard_map/ppermute | solution.py:297
  131.6 6.5 %collective-permute-start.37 = (f32[32,512]{1,0:T(8,128)S(1)}, f32[32,512]{1,0:T(8,128)S(1)}, u32[]{:S(2)}, u32[]{:S(2)}) collective-permute-start(f32[32,512]{1,0:T(8,128)S(1)} %add.108), channel_id=1, source_target_pairs={{0,12},{4,8},{8,4},{12,0},{1,13},{5,9},{9,5},{13,1},{2,14},{6,10},... | collective-permute-start | bytes 196616 | tf_op jit(solution)/shard_map/ppermute | solution.py:297
  134.0 6.1 %collective-permute-start.40 = (f32[32,512]{1,0:T(8,128)S(1)}, f32[32,512]{1,0:T(8,128)S(1)}, u32[]{:S(2)}, u32[]{:S(2)}) collective-permute-start(f32[32,512]{1,0:T(8,128)S(1)} %add.110), channel_id=1, source_target_pairs={{0,12},{4,8},{8,4},{12,0},{1,13},{5,9},{9,5},{13,1},{2,14},{6,10},... | collective-permute-start | bytes 196616 | tf_op jit(solution)/shard_map/ppermute | solution.py:297
  138.2 4.3 %collective-permute-start.38 = (f32[32,512]{1,0:T(8,128)S(1)}, f32[32,512]{1,0:T(8,128)S(1)}, u32[]{:S(2)}, u32[]{:S(2)}) collective-permute-start(f32[32,512]{1,0:T(8,128)S(1)} %add.109.refs_0_), channel_id=1, source_target_pairs={{0,4},{4,0},{8,12},{12,8},{1,5},{5,1},{9,13},{13,9},{2,6},{6,2},{1... | collective-permute-start | bytes 196616 | tf_op jit(solution)/shard_map/ppermute | solution.py:297
  140.2 4.3 %collective-permute-start.41 = (f32[32,512]{1,0:T(8,128)S(1)}, f32[32,512]{1,0:T(8,128)S(1)}, u32[]{:S(2)}, u32[]{:S(2)}) collective-permute-start(f32[32,512]{1,0:T(8,128)S(1)} %add.111.refs_1_), channel_id=1, source_target_pairs={{0,4},{4,0},{8,12},{12,8},{1,5},{5,1},{9,13},{13,9},{2,6},{6,2},{1... | collective-permute-start | bytes 196616 | tf_op jit(solution)/shard_map/ppermute | solution.py:297
  (11 other events, 21.7 us)

commit v5 on v4

--- a/solution.py
+++ b/solution.py
@@ -37,7 +37,7 @@
         width = extent // 2
         at = lax.axis_index(self.axis)
         if self.axis == "rows":
-            at = at ^ (at >> 1)
+            at = at >> (lax.axis_index("cols") & 1)
         inner = width // self.chunks
         start = ((at & 1) ^ self.away) * width + self.chunk * inner
         return pl.ds(pl.multiple_of(start, LANES), inner)
@@ -64,7 +64,7 @@
     return pltpu.with_memory_space_constraint(blocks, pltpu.HBM)
 
 
-def block_copies(blocks_ref, out_ref, sems, index):
+def block_copies(blocks_ref, out_ref, sems, index, pieces):
     height = out_ref.shape[0] // COPIES
     return [
         pltpu.make_async_copy(
@@ -72,14 +72,22 @@
             out_ref.at[pl.ds(i * height, height), :],
             sems.at[i],
         )
-        for i in range(COPIES)
+        for i in pieces
     ]
 
 
+class Bring(NamedTuple):
+    blocks: jax.Array
+    index: int
+    pieces: range
+    held: list
+
+
 def work(job, bring):
-    operands, in_specs, out_shape, scratch = [], [], [], []
+    operands, in_specs, out_shape, scratch, aliases = [], [], [], [], {}
     if job:
-        operands += [*job.vectors, *(job.given or ()), job.block]
+        known = [j for j, value in enumerate(job.given) if value is not None]
+        operands += [*job.vectors, *(job.given[j] for j in known), job.block]
         in_specs += [IN_VMEM] * len(operands)
         extent = job.block.shape[0 if job.dims is LOWER else 1]
         depth = job.block.shape[1 if job.dims is LOWER else 0]
@@ -88,23 +96,27 @@
             jax.ShapeDtypeStruct((rows, out.width(extent)), jnp.float32) for out in job.outs
         ]
     if bring:
-        operands.append(in_hbm(bring[0]))
-        in_specs.append(IN_HBM)
-        out_shape.append(jax.ShapeDtypeStruct(bring[0].shape[1:], bring[0].dtype))
+        aliases = {len(operands): len(out_shape)} if bring.held else {}
+        operands += [*bring.held, in_hbm(bring.blocks)]
+        in_specs += [IN_VMEM] * len(bring.held) + [IN_HBM]
+        out_shape.append(jax.ShapeDtypeStruct(bring.blocks.shape[1:], bring.blocks.dtype))
         scratch.append(pltpu.SemaphoreType.DMA((COPIES,)))
 
     def kernel(*refs):
         ins, refs = refs[: len(operands)], refs[len(operands) :]
         outs, refs = refs[: len(out_shape)], refs[len(out_shape) :]
-        copies = block_copies(ins[-1], outs[-1], refs[0], bring[1]) if bring else []
+        copies = []
+        if bring:
+            copies = block_copies(ins[-1], outs[-1], refs[0], bring.index, bring.pieces)
         for copy in copies:
             copy.start()
         if job:
             count = len(job.vectors)
             vectors = [ref[...].astype(jnp.bfloat16) for ref in ins[:count]]
-            block_ref = ins[count + len(job.given or ())]
+            given = dict(zip(known, ins[count:]))
+            block_ref = ins[count + len(known)]
             for j, out in enumerate(job.outs):
-                total = ins[count + j][...] if job.given else None
+                total = given[j][...] if j in given else None
                 for vector, place in zip(vectors, job.places):
                     inner, outer = place.span(depth), out.span(extent)
                     part = block_ref[outer, inner] if job.dims is LOWER else block_ref[inner, outer]
@@ -122,6 +134,7 @@
         in_specs=in_specs,
         out_specs=[IN_VMEM] * len(out_shape),
         scratch_shapes=scratch,
+        input_output_aliases=aliases,
         compiler_params=pltpu.CompilerParams(vmem_limit_bytes=2 << 20),
         cost_estimate=SHORT,
         name=("products" if job else "fetch") + ("_fetch" if job and bring else ""),
@@ -149,7 +162,7 @@
             pltpu.make_async_copy(index_ref, index, small_sems.at[0]),
             pltpu.make_async_copy(loads_ref.at[0], table, small_sems.at[1]),
         ]
-        for copy in small + copies[:first]:
+        for copy in small + copies:
             copy.start()
         for copy in small:
             copy.wait()
@@ -166,8 +179,6 @@
         vector_ref[...] = vector
         for copy in copies[:first]:
             copy.wait()
-        for copy in copies[first:]:
-            copy.start()
         part_ref[...] = lax.dot_general(
             vector.astype(blocks.dtype),
             block_ref[pl.ds(pl.multiple_of(start, LANES), height), :],
@@ -268,51 +279,85 @@
 def staged(coupling, diag_inverse, loads, axle_index, sizes):
     order = Order()
     blocks = {}
-    steps = {axis: [1 << i for i in range(1, size.bit_length() - 1)] for axis, size in sizes.items()}
-    steps["rows"] = [3 if step == 2 else step for step in steps["rows"]]
+    def steps(axis, col=0):
+        found = [1 << i for i in range(sizes[axis].bit_length() - 1)]
+        if axis == "rows" and col % 2:
+            found[:2] = [3, 1]
+        return found
 
     def parts(axis, away, chunks):
         return [Part(axis, away, chunk, chunks) for chunk in range(chunks)]
 
-    def source(name):
-        return name and (diag_inverse if name[0] == "diag" else coupling, name[1])
-
-    def products(vectors, places, name, dims, given, outs):
+    def taking(bring):
+        if not bring:
+            return []
+        return [blocks[bring[0]]] if bring[0] in blocks else []
+
+    def source(bring, held):
+        if not bring:
+            return None
+        (kind, index), pieces = bring
+        return Bring(diag_inverse if kind == "diag" else coupling, index, pieces, held)
+
+    def products(vectors, places, name, dims, given, outs, bring=None):
         count = len(vectors)
+        known = [value for value in given or () if value is not None]
+        held = taking(bring)
 
         def call(*values):
-            job = Job(values[:count], places, values[count], dims, values[count + 1 :], outs)
-            return work(job, None)
-
-        return list(order.run(call, *vectors, blocks[name], *(given or ())))
-
-    def fetch(name):
+            left = iter(values[count + 1 :])
+            terms = [None if value is None else next(left) for value in given or ()]
+            job = Job(values[:count], places, values[count], dims, terms, outs)
+            return work(job, source(bring, list(left)))
+
+        result = list(order.run(call, *vectors, blocks[name], *known, *held))
+        if bring:
+            blocks[bring[0]] = result.pop()
+        return result
+
+    def fetch(name, pieces=range(COPIES)):
         def call():
-            (blocks[name],) = order.run(lambda: work(None, source(name)))
+            bring = name, pieces
+            held = taking(bring)
+            (blocks[name],) = order.run(lambda *found: work(None, source(bring, list(found))), *held)
 
         return call
 
-    def permute(value, axis, step):
+    def permute(value, axis, number):
         (value,) = order.after(value)
-        return lax.ppermute(value, axis, [(i, i ^ step) for i in range(sizes[axis])])
+        if axis == "cols":
+            step = steps(axis)[number]
+            return lax.ppermute(value, axis, [(i, i ^ step) for i in range(sizes[axis])])
+        n_cols = sizes["cols"]
+        moves = [
+            (row * n_cols + col, (row ^ steps(axis, col)[number]) * n_cols + col)
+            for row in range(sizes[axis])
+            for col in range(n_cols)
+        ]
+        return lax.ppermute(value, ("rows", "cols"), moves)
 
     def nothing():
         pass
 
-    def phase(axis, chunks, finish, onward, early=nothing, middle=nothing, late=nothing, post=None):
+    def phase(
+        axis, chunks, finish, onward, early=nothing, middle=nothing, late=nothing, post=None, during=None
+    ):
         every = range(chunks)
-        got = [permute(finish([i])[0], axis, 1) for i in every]
-        kept = finish([chunks + i for i in every])
-        early()
-        for step in [*steps[axis], None]:
+        got = [permute(finish([i])[0], axis, 0) for i in every]
+        kept = finish([chunks + i for i in every], during)
+        more = early()
+        if more:
+            kept = [order.run(jnp.add, value, term) for value, term in zip(kept, more)]
+        last = len(steps(axis))
+        for number in range(1, last + 1):
             sent = []
             for i in every:
                 kept[i] = order.run(jnp.add, kept[i], got[i])
-                if step is None and post is not None:
+                if number == last and post is not None:
                     kept[i] = order.run(jnp.subtract, post()[i], kept[i])
-                sent.append(permute(kept[i], axis, step or 1))
+                sent.append(permute(kept[i], axis, number % last))
             got = sent
-            if step is not None:
+            if number < last:
                 middle()
                 middle = nothing
         own, others = parts(axis, 0, chunks), parts(axis, 1, chunks)
@@ -322,16 +367,18 @@
         name, dims, next_chunks, given = onward
         away = "cols" if axis == "rows" else "rows"
         outs = parts(away, 1, next_chunks) + parts(away, 0, next_chunks)
-        given = products(kept, own, name, dims, given and given(), outs)
+        extra = given and given()
+        given = products(kept, own, name, dims, extra and extra + [None] * (len(outs) - len(extra)), outs)
         late()
         for i in every[:-1]:
             (got[i],) = order.after(got[i])
             given = products(got[i : i + 1], others[i : i + 1], name, dims, given, outs)
         (got[-1],) = order.after(got[-1])
 
-        def rest(which):
+        def rest(which, bring=None):
+            terms = [given[i] for i in which]
             return products(
-                got[-1:], others[-1:], name, dims, [given[i] for i in which], [outs[i] for i in which]
+                got[-1:], others[-1:], name, dims, terms, [outs[i] for i in which], bring
             )
 
         return kept, got, rest
@@ -345,7 +392,7 @@
     )
     rhs, solved, answers, skipped, done = {}, {}, {}, {}, {}
 
-    def first_finish(which):
+    def first_finish(which, bring=None):
         if which == [0]:
             return [first]
         return products([vector], [Whole()], ("diag", 0), LOWER, None, [Part("cols", 0)])
@@ -356,11 +403,15 @@
         rhs.update(order.run(lambda a, b: select(a, b, wanted), selector, loads))
         fetch(pair(1, 0))()
 
-    def skip_forward():
-        outs = parts("rows", 1, CHUNKS) + parts("rows", 0, CHUNKS)
-        skipped[LOWER] = products(
-            sum(solved[0], []), parts("cols", 0, 1) + parts("cols", 1, 1), pair(2, 0), LOWER, None, outs
-        )
+    def skip_forward(away, bring=None):
+        def call():
+            places = parts("cols", 0, 1) + parts("cols", 1, 1)
+            skipped[LOWER, away] = products(
+                sum(solved[0], []), places, pair(2, 0), LOWER, None, parts("rows", away, chunks[2]), bring
+            )
+            return skipped[LOWER, away]
+
+        return call
 
     def skip_backward():
         outs = parts("cols", 1, 1) + parts("cols", 0, 1)
@@ -392,15 +443,16 @@
     )
     *_, finish = phase(
         "rows", chunks[1], finish, (("diag", 1), LOWER, 1, None),
-        fetch(("diag", 1)), fetch(pair(2, 0)), skip_forward, lambda: rhs[1],
+        middle=fetch(pair(2, 0)), late=skip_forward(1), post=lambda: rhs[1],
+        during=(("diag", 1), range(COPIES)),
     )
     *solved[1], finish = phase(
-        "cols", 1, finish, (pair(2, 1), LOWER, chunks[2], lambda: skipped[LOWER]),
+        "cols", 1, finish, (pair(2, 1), LOWER, chunks[2], lambda: skipped[LOWER, 1]),
         middle=fetch(pair(2, 1)),
     )
     *_, finish = phase(
         "rows", chunks[2], finish, (("diag", 2), LOWER, 1, None),
-        middle=fetch(("diag", 2)), post=lambda: rhs[2],
+        early=skip_forward(0), middle=fetch(("diag", 2)), post=lambda: rhs[2],
     )
     *solved[2], finish = phase("cols", 1, finish, (("diag", 2), UPPER, CHUNKS, None))
     *answers[2], finish = phase("rows", CHUNKS, finish, (pair(2, 1), UPPER, 1, None))
@@ -456,7 +508,8 @@
     if (
         power_of_two(n_rows)
         and power_of_two(n_cols)
-        and min(n_rows, n_cols) > 1
+        and n_rows > 2
+        and n_cols > 1
         and over_cols % (2 * CHUNKS * LANES) == 0
         and over_rows % (2 * LANES) == 0
     ):

time: 145 us -> 143 us (0.986)
  starting transfers between devices: 48.8 us -> 44.9 us
  waiting for transfers between devices: 39.9 us -> 42.7 us
    ppermute x42 -> x15, starting transfers between devices: 48.8 us -> 13.4 us  [permute(): lax.ppermute(value, axis, [(i, i ^ step) for i in range(sizes[axis])])]
    ppermute x0 -> x27, starting transfers between devices: none -> 31.6 us  [permute(): return lax.ppermute(value, ('rows', 'cols'), moves)]
    ppermute x0 -> x27, waiting for transfers between devices: none -> 27.1 us  [permute(): return lax.ppermute(value, ('rows', 'cols'), moves)]
    ppermute x42 -> x15, waiting for transfers between devices: 39.9 us -> 15.6 us  [permute(): lax.ppermute(value, axis, [(i, i ^ step) for i in range(sizes[axis])])]
  transfers between devices with their start and end apart: 42 -> 42, of which waited for: 29 -> 32; matrix products, arithmetic and copies ran while one was open for 0% -> 0% of each run, Pallas kernels for 32% -> 32%
where the time goes in v5:
time: 143 us
  Pallas kernels  53.5 us (37%)
  starting transfers between devices  44.9 us (31%)
  waiting for transfers between devices  42.7 us (30%)
    pallas_call x43, Pallas kernels, work(): pl.pallas_call(kernel, out_shape=out_shape, in_specs=in_specs, out_specs=...  46.4 us
    ppermute x27, starting transfers between devices, permute(): return lax.ppermute(value, ('rows', 'cols'), moves)  31.6 us
    ppermute x27, waiting for transfers between devices, permute(): return lax.ppermute(value, ('rows', 'cols'), moves)  27.1 us
    ppermute x15, waiting for transfers between devices, permute(): lax.ppermute(value, axis, [(i, i ^ step) for i in range(sizes[axis])])  15.6 us
    ppermute x15, starting transfers between devices, permute(): lax.ppermute(value, axis, [(i, i ^ step) for i in range(sizes[axis])])  13.4 us
    pallas_call x1, Pallas kernels, begin(): pl.pallas_call(kernel, out_shape=(jax.ShapeDtypeStruct((count, positions)...  3.78 us
    pallas_call x4, Pallas kernels, place(): pl.pallas_call(kernel, out_shape=jax.ShapeDtypeStruct((LEVELS, rows, widt...  3.1 us
  transfers between devices with their start and end apart: 42, of which 32 were waited for; matrix products, arithmetic and copies ran while one was open for 0% of the time, Pallas kernels for 32%

profile of v5, /device:TPU:0, one launch (start us, length us, event | category | flops | bytes accessed | tf_op | source)
XLA Modules:
  0.0 142.9 jit_solution(17427448527657990754)
XLA Ops:
  0.6 3.8 %begin.1 = (f32[32,128]{1,0:T(8,128)S(1)}, f32[32,2048]{1,0:T(8,128)S(1)}, f32[32,1024]{1,0:T(8,128)S(1)}, bf16[2048,2048]{1,0:T(8,128)(2,1)S(1)}) custom-call(s32[32]{0:T(128)} %index_ref.1, bf16[3,128,2048]{2,1,0:T(8,128)(2,1)} %loads_ref.2, bf16[3,2048,2048]{2,1,0:T(8,128)(2,1)} %refs_0_.9), custom_call_target="tpu_custom_call" | custom-call | tf_op jit(solution)/shard_map/begin/pallas_call | solution.py:191
  6.3 2.6 %collective-permute-start.1 = (f32[32,1024]{1,0:T(8,128)S(1)}, f32[32,1024]{1,0:T(8,128)S(1)}, u32[]{:S(2)}, u32[]{:S(2)}) collective-permute-start(f32[32,1024]{1,0:T(8,128)S(1)} %add.90), channel_id=1, source_target_pairs={{0,2},{1,3},{2,0},{3,1},{4,6},{5,7},{6,4},{7,5},{8,10},{9,11},{10,... | collective-permute-start | bytes 393224 | tf_op jit(solution)/shard_map/ppermute | solution.py:330
  8.9 3.5 %fetch.5.refs_1_.refs_2_.refs_4_.refs_3_ = bf16[2048,2048]{1,0:T(8,128)(2,1)S(1)} custom-call(bf16[3,2048,2048]{2,1,0:T(8,128)(2,1)} %refs_0_.7), custom_call_target="tpu_custom_call" | custom-call | tf_op jit(solution)/shard_map/fetch/pallas_call | solution.py:131
  15.2 1.9 %collective-permute-start.3 = (f32[32,1024]{1,0:T(8,128)S(1)}, f32[32,1024]{1,0:T(8,128)S(1)}, u32[]{:S(2)}, u32[]{:S(2)}) collective-permute-start(f32[32,1024]{1,0:T(8,128)S(1)} %products.39), channel_id=1, source_target_pairs={{0,4},{1,13},{2,6},{3,15},{4,0},{5,9},{6,2},{7,11},{8,12},{9,5},{1... | collective-permute-start | bytes 393224 | tf_op jit(solution)/shard_map/ppermute | solution.py:337
  17.1 3.6 %products_fetch.1 = (f32[32,1024]{1,0:T(8,128)S(1)}, bf16[2048,2048]{1,0:T(8,128)(2,1)S(1)}) custom-call(f32[32,1024]{1,0:T(8,128)S(1)} %collective-permute-done.2.refs_0_.refs_1_, f32[32,1024]{1,0:T(8,128)S(1)} %get-tuple-element.332.refs_1_, bf16[2048,2048]{1,0:T(8,128)(2,1)S(1)} %fetch.5.refs_1_.refs_2_.refs_4_.refs_3_, bf16[3,2048,2048]{2,1,0:T(8,128)(2,1)} %refs_0_.9), custom_call_target="tpu_custom_call" | custom-call | tf_op jit(solution)/shard_map/products_fetch/pallas_call | solution.py:131
  20.7 3.2 %collective-permute-start.4 = (f32[32,1024]{1,0:T(8,128)S(1)}, f32[32,1024]{1,0:T(8,128)S(1)}, u32[]{:S(2)}, u32[]{:S(2)}) collective-permute-start(f32[32,1024]{1,0:T(8,128)S(1)} %add.92), channel_id=1, source_target_pairs={{0,8},{1,5},{2,10},{3,7},{4,12},{5,1},{6,14},{7,3},{8,0},{9,13},{1... | collective-permute-start | bytes 393224 | tf_op jit(solution)/shard_map/ppermute | solution.py:337
  23.9 3.5 %fetch.6.refs_2_.refs_4_ = bf16[2048,2048]{1,0:T(8,128)(2,1)S(1)} custom-call(bf16[3,2048,2048]{2,1,0:T(8,128)(2,1)} %refs_0_.7), custom_call_target="tpu_custom_call" | custom-call | tf_op jit(solution)/shard_map/fetch/pallas_call | solution.py:131
  32.0 1.8 %collective-permute-done.5.refs_0_ = f32[32,1024]{1,0:T(8,128)S(1)} collective-permute-done((f32[32,1024]{1,0:T(8,128)S(1)}, f32[32,1024]{1,0:T(8,128)S(1)}, u32[]{:S(2)}, u32[]{:S(2)}) %collective-permute-start.5) | collective-permute-done | bytes 131104 | tf_op jit(solution)/shard_map/ppermute | solution.py:337
  36.5 1.6 %collective-permute-start.7 = (f32[32,1024]{1,0:T(8,128)S(1)}, f32[32,1024]{1,0:T(8,128)S(1)}, u32[]{:S(2)}, u32[]{:S(2)}) collective-permute-start(f32[32,1024]{1,0:T(8,128)S(1)} %add.94), channel_id=1, source_target_pairs={{0,2},{1,3},{2,0},{3,1},{4,6},{5,7},{6,4},{7,5},{8,10},{9,11},{10,... | collective-permute-start | bytes 393224 | tf_op jit(solution)/shard_map/ppermute | solution.py:330
  38.1 3.5 %fetch.7.refs_3_.refs_2_ = bf16[2048,2048]{1,0:T(8,128)(2,1)S(1)} custom-call(bf16[3,2048,2048]{2,1,0:T(8,128)(2,1)} %refs_0_.7), custom_call_target="tpu_custom_call" | custom-call | tf_op jit(solution)/shard_map/fetch/pallas_call | solution.py:131
  48.9 1.9 %collective-permute-start.10 = (f32[32,512]{1,0:T(8,128)S(1)}, f32[32,512]{1,0:T(8,128)S(1)}, u32[]{:S(2)}, u32[]{:S(2)}) collective-permute-start(f32[32,512]{1,0:T(8,128)S(1)} %add.98), channel_id=1, source_target_pairs={{0,8},{1,5},{2,10},{3,7},{4,12},{5,1},{6,14},{7,3},{8,0},{9,13},{1... | collective-permute-start | bytes 196616 | tf_op jit(solution)/shard_map/ppermute | solution.py:337
  50.8 2.0 %collective-permute-start.13 = (f32[32,512]{1,0:T(8,128)S(1)}, f32[32,512]{1,0:T(8,128)S(1)}, u32[]{:S(2)}, u32[]{:S(2)}) collective-permute-start(f32[32,512]{1,0:T(8,128)S(1)} %add.100), channel_id=1, source_target_pairs={{0,8},{1,5},{2,10},{3,7},{4,12},{5,1},{6,14},{7,3},{8,0},{9,13},{1... | collective-permute-start | bytes 196616 | tf_op jit(solution)/shard_map/ppermute | solution.py:337
  52.8 3.5 %fetch.8.refs_2_.refs_3_.refs_1_ = bf16[2048,2048]{1,0:T(8,128)(2,1)S(1)} custom-call(bf16[3,2048,2048]{2,1,0:T(8,128)(2,1)} %refs_0_.9), custom_call_target="tpu_custom_call" | custom-call | tf_op jit(solution)/shard_map/fetch/pallas_call | solution.py:131
  56.3 2.0 %collective-permute-start.14 = (f32[32,512]{1,0:T(8,128)S(1)}, f32[32,512]{1,0:T(8,128)S(1)}, u32[]{:S(2)}, u32[]{:S(2)}) collective-permute-start(f32[32,512]{1,0:T(8,128)S(1)} %sub.17.refs_0_), channel_id=1, source_target_pairs={{0,4},{1,13},{2,6},{3,15},{4,0},{5,9},{6,2},{7,11},{8,12},{9,5},{1... | collective-permute-start | bytes 196616 | tf_op jit(solution)/shard_map/ppermute | solution.py:337
  65.3 1.6 %collective-permute-start.16 = (f32[32,1024]{1,0:T(8,128)S(1)}, f32[32,1024]{1,0:T(8,128)S(1)}, u32[]{:S(2)}, u32[]{:S(2)}) collective-permute-start(f32[32,1024]{1,0:T(8,128)S(1)} %add.102), channel_id=1, source_target_pairs={{0,2},{1,3},{2,0},{3,1},{4,6},{5,7},{6,4},{7,5},{8,10},{9,11},{10,... | collective-permute-start | bytes 393224 | tf_op jit(solution)/shard_map/ppermute | solution.py:330
  66.9 4.3 %collective-permute-done.16 = f32[32,1024]{1,0:T(8,128)S(1)} collective-permute-done((f32[32,1024]{1,0:T(8,128)S(1)}, f32[32,1024]{1,0:T(8,128)S(1)}, u32[]{:S(2)}, u32[]{:S(2)}) %collective-permute-start.16) | collective-permute-done | bytes 131104 | tf_op jit(solution)/shard_map/ppermute | solution.py:330
  80.5 2.9 %collective-permute-done.22 = f32[32,512]{1,0:T(8,128)S(1)} collective-permute-done((f32[32,512]{1,0:T(8,128)S(1)}, f32[32,512]{1,0:T(8,128)S(1)}, u32[]{:S(2)}, u32[]{:S(2)}) %collective-permute-start.22) | collective-permute-done | bytes 65568 | tf_op jit(solution)/shard_map/ppermute | solution.py:337
  91.4 1.6 %collective-permute-start.25 = (f32[32,1024]{1,0:T(8,128)S(1)}, f32[32,1024]{1,0:T(8,128)S(1)}, u32[]{:S(2)}, u32[]{:S(2)}) collective-permute-start(f32[32,1024]{1,0:T(8,128)S(1)} %add.108), channel_id=1, source_target_pairs={{0,2},{1,3},{2,0},{3,1},{4,6},{5,7},{6,4},{7,5},{8,10},{9,11},{10,... | collective-permute-start | bytes 393224 | tf_op jit(solution)/shard_map/ppermute | solution.py:330
  92.9 1.5 %products.61 = (f32[32,1024]{1,0:T(8,128)S(1)}, f32[32,1024]{1,0:T(8,128)S(1)}) custom-call(f32[32,512]{1,0:T(8,128)S(1)} %add.107.refs_0_, f32[32,512]{1,0:T(8,128)S(1)} %add.105.refs_1_, f32[32,512]{1,0:T(8,128)S(1)} %collective-permute-done.23.refs_0_.refs_2_, f32[32,512]{1,0:T(8,128)S(1)} %collective-permute-done.20.refs_0_.refs_3_, ...), custom_call_target="tpu_custom_call" | custom-call | tf_op jit(solution)/shard_map/products/pallas_call | solution.py:131
  94.5 2.7 %collective-permute-done.25 = f32[32,1024]{1,0:T(8,128)S(1)} collective-permute-done((f32[32,1024]{1,0:T(8,128)S(1)}, f32[32,1024]{1,0:T(8,128)S(1)}, u32[]{:S(2)}, u32[]{:S(2)}) %collective-permute-start.25) | collective-permute-done | bytes 131104 | tf_op jit(solution)/shard_map/ppermute | solution.py:330
  99.8 1.5 %collective-permute-start.27 = (f32[32,512]{1,0:T(8,128)S(1)}, f32[32,512]{1,0:T(8,128)S(1)}, u32[]{:S(2)}, u32[]{:S(2)}) collective-permute-start(f32[32,512]{1,0:T(8,128)S(1)} %products.64), channel_id=1, source_target_pairs={{0,4},{1,13},{2,6},{3,15},{4,0},{5,9},{6,2},{7,11},{8,12},{9,5},{1... | collective-permute-start | bytes 196616 | tf_op jit(solution)/shard_map/ppermute | solution.py:337
  104.8 1.6 %collective-permute-start.28 = (f32[32,512]{1,0:T(8,128)S(1)}, f32[32,512]{1,0:T(8,128)S(1)}, u32[]{:S(2)}, u32[]{:S(2)}) collective-permute-start(f32[32,512]{1,0:T(8,128)S(1)} %add.110), channel_id=1, source_target_pairs={{0,8},{1,5},{2,10},{3,7},{4,12},{5,1},{6,14},{7,3},{8,0},{9,13},{1... | collective-permute-start | bytes 196616 | tf_op jit(solution)/shard_map/ppermute | solution.py:337
  106.3 3.5 %fetch.9.refs_1_.refs_3_.refs_2_ = bf16[2048,2048]{1,0:T(8,128)(2,1)S(1)} custom-call(bf16[3,2048,2048]{2,1,0:T(8,128)(2,1)} %refs_0_.9), custom_call_target="tpu_custom_call" | custom-call | tf_op jit(solution)/shard_map/fetch/pallas_call | solution.py:131
  118.2 1.6 %collective-permute-start.34 = (f32[32,1024]{1,0:T(8,128)S(1)}, f32[32,1024]{1,0:T(8,128)S(1)}, u32[]{:S(2)}, u32[]{:S(2)}) collective-permute-start(f32[32,1024]{1,0:T(8,128)S(1)} %add.114), channel_id=1, source_target_pairs={{0,2},{1,3},{2,0},{3,1},{4,6},{5,7},{6,4},{7,5},{8,10},{9,11},{10,... | collective-permute-start | bytes 393224 | tf_op jit(solution)/shard_map/ppermute | solution.py:330
  120.7 3.3 %collective-permute-done.34 = f32[32,1024]{1,0:T(8,128)S(1)} collective-permute-done((f32[32,1024]{1,0:T(8,128)S(1)}, f32[32,1024]{1,0:T(8,128)S(1)}, u32[]{:S(2)}, u32[]{:S(2)}) %collective-permute-start.34) | collective-permute-done | bytes 131104 | tf_op jit(solution)/shard_map/ppermute | solution.py:330
  126.1 2.0 %collective-permute-start.39 = (f32[32,512]{1,0:T(8,128)S(1)}, f32[32,512]{1,0:T(8,128)S(1)}, u32[]{:S(2)}, u32[]{:S(2)}) collective-permute-start(f32[32,512]{1,0:T(8,128)S(1)} %products.73), channel_id=1, source_target_pairs={{0,4},{1,13},{2,6},{3,15},{4,0},{5,9},{6,2},{7,11},{8,12},{9,5},{1... | collective-permute-start | bytes 196616 | tf_op jit(solution)/shard_map/ppermute | solution.py:337
  128.6 1.5 %collective-permute-done.36 = f32[32,512]{1,0:T(8,128)S(1)} collective-permute-done((f32[32,512]{1,0:T(8,128)S(1)}, f32[32,512]{1,0:T(8,128)S(1)}, u32[]{:S(2)}, u32[]{:S(2)}) %collective-permute-start.36) | collective-permute-done | bytes 65568 | tf_op jit(solution)/shard_map/ppermute | solution.py:337
  131.5 1.7 %collective-permute-start.40 = (f32[32,512]{1,0:T(8,128)S(1)}, f32[32,512]{1,0:T(8,128)S(1)}, u32[]{:S(2)}, u32[]{:S(2)}) collective-permute-start(f32[32,512]{1,0:T(8,128)S(1)} %add.118), channel_id=1, source_target_pairs={{0,8},{1,5},{2,10},{3,7},{4,12},{5,1},{6,14},{7,3},{8,0},{9,13},{1... | collective-permute-start | bytes 196616 | tf_op jit(solution)/shard_map/ppermute | solution.py:337
  134.0 1.7 %collective-permute-done.37 = f32[32,512]{1,0:T(8,128)S(1)} collective-permute-done((f32[32,512]{1,0:T(8,128)S(1)}, f32[32,512]{1,0:T(8,128)S(1)}, u32[]{:S(2)}, u32[]{:S(2)}) %collective-permute-start.37) | collective-permute-done | bytes 65568 | tf_op jit(solution)/shard_map/ppermute | solution.py:337
  135.8 1.6 %collective-permute-done.40 = f32[32,512]{1,0:T(8,128)S(1)} collective-permute-done((f32[32,512]{1,0:T(8,128)S(1)}, f32[32,512]{1,0:T(8,128)S(1)}, u32[]{:S(2)}, u32[]{:S(2)}) %collective-permute-start.40) | collective-permute-done | bytes 65568 | tf_op jit(solution)/shard_map/ppermute | solution.py:337
  138.6 1.5 %collective-permute-done.38.refs_0_ = f32[32,512]{1,0:T(8,128)S(1)} collective-permute-done((f32[32,512]{1,0:T(8,128)S(1)}, f32[32,512]{1,0:T(8,128)S(1)}, u32[]{:S(2)}, u32[]{:S(2)}) %collective-permute-start.38) | collective-permute-done | bytes 65568 | tf_op jit(solution)/shard_map/ppermute | solution.py:337
  140.1 1.9 %collective-permute-done.41.refs_1_ = f32[32,512]{1,0:T(8,128)S(1)} collective-permute-done((f32[32,512]{1,0:T(8,128)S(1)}, f32[32,512]{1,0:T(8,128)S(1)}, u32[]{:S(2)}, u32[]{:S(2)}) %collective-permute-start.41) | collective-permute-done | bytes 65568 | tf_op jit(solution)/shard_map/ppermute | solution.py:337
  (138 shorter events, 65.6 us)
Async XLA Ops:
  6.3 6.7 %collective-permute-start.1 = (f32[32,1024]{1,0:T(8,128)S(1)}, f32[32,1024]{1,0:T(8,128)S(1)}, u32[]{:S(2)}, u32[]{:S(2)}) collective-permute-start(f32[32,1024]{1,0:T(8,128)S(1)} %add.90), channel_id=1, source_target_pairs={{0,2},{1,3},{2,0},{3,1},{4,6},{5,7},{6,4},{7,5},{8,10},{9,11},{10,... | collective-permute-start | bytes 393224 | tf_op jit(solution)/shard_map/ppermute | solution.py:330
  15.2 5.5 %collective-permute-start.3 = (f32[32,1024]{1,0:T(8,128)S(1)}, f32[32,1024]{1,0:T(8,128)S(1)}, u32[]{:S(2)}, u32[]{:S(2)}) collective-permute-start(f32[32,1024]{1,0:T(8,128)S(1)} %products.39), channel_id=1, source_target_pairs={{0,4},{1,13},{2,6},{3,15},{4,0},{5,9},{6,2},{7,11},{8,12},{9,5},{1... | collective-permute-start | bytes 393224 | tf_op jit(solution)/shard_map/ppermute | solution.py:337
  20.7 7.1 %collective-permute-start.4 = (f32[32,1024]{1,0:T(8,128)S(1)}, f32[32,1024]{1,0:T(8,128)S(1)}, u32[]{:S(2)}, u32[]{:S(2)}) collective-permute-start(f32[32,1024]{1,0:T(8,128)S(1)} %add.92), channel_id=1, source_target_pairs={{0,8},{1,5},{2,10},{3,7},{4,12},{5,1},{6,14},{7,3},{8,0},{9,13},{1... | collective-permute-start | bytes 393224 | tf_op jit(solution)/shard_map/ppermute | solution.py:337
  27.9 5.8 %collective-permute-start.5 = (f32[32,1024]{1,0:T(8,128)S(1)}, f32[32,1024]{1,0:T(8,128)S(1)}, u32[]{:S(2)}, u32[]{:S(2)}) collective-permute-start(f32[32,1024]{1,0:T(8,128)S(1)} %sub.15.refs_0_), channel_id=1, source_target_pairs={{0,4},{1,13},{2,6},{3,15},{4,0},{5,9},{6,2},{7,11},{8,12},{9,5},{1... | collective-permute-start | bytes 393224 | tf_op jit(solution)/shard_map/ppermute | solution.py:337
  36.5 5.8 %collective-permute-start.7 = (f32[32,1024]{1,0:T(8,128)S(1)}, f32[32,1024]{1,0:T(8,128)S(1)}, u32[]{:S(2)}, u32[]{:S(2)}) collective-permute-start(f32[32,1024]{1,0:T(8,128)S(1)} %add.94), channel_id=1, source_target_pairs={{0,2},{1,3},{2,0},{3,1},{4,6},{5,7},{6,4},{7,5},{8,10},{9,11},{10,... | collective-permute-start | bytes 393224 | tf_op jit(solution)/shard_map/ppermute | solution.py:330
  44.2 4.6 %collective-permute-start.9 = (f32[32,512]{1,0:T(8,128)S(1)}, f32[32,512]{1,0:T(8,128)S(1)}, u32[]{:S(2)}, u32[]{:S(2)}) collective-permute-start(f32[32,512]{1,0:T(8,128)S(1)} %products.47), channel_id=1, source_target_pairs={{0,4},{1,13},{2,6},{3,15},{4,0},{5,9},{6,2},{7,11},{8,12},{9,5},{1... | collective-permute-start | bytes 196616 | tf_op jit(solution)/shard_map/ppermute | solution.py:337
  45.7 5.1 %collective-permute-start.12 = (f32[32,512]{1,0:T(8,128)S(1)}, f32[32,512]{1,0:T(8,128)S(1)}, u32[]{:S(2)}, u32[]{:S(2)}) collective-permute-start(f32[32,512]{1,0:T(8,128)S(1)} %products.48), channel_id=1, source_target_pairs={{0,4},{1,13},{2,6},{3,15},{4,0},{5,9},{6,2},{7,11},{8,12},{9,5},{1... | collective-permute-start | bytes 196616 | tf_op jit(solution)/shard_map/ppermute | solution.py:337
  48.9 7.4 %collective-permute-start.10 = (f32[32,512]{1,0:T(8,128)S(1)}, f32[32,512]{1,0:T(8,128)S(1)}, u32[]{:S(2)}, u32[]{:S(2)}) collective-permute-start(f32[32,512]{1,0:T(8,128)S(1)} %add.98), channel_id=1, source_target_pairs={{0,8},{1,5},{2,10},{3,7},{4,12},{5,1},{6,14},{7,3},{8,0},{9,13},{1... | collective-permute-start | bytes 196616 | tf_op jit(solution)/shard_map/ppermute | solution.py:337
  50.8 5.5 %collective-permute-start.13 = (f32[32,512]{1,0:T(8,128)S(1)}, f32[32,512]{1,0:T(8,128)S(1)}, u32[]{:S(2)}, u32[]{:S(2)}) collective-permute-start(f32[32,512]{1,0:T(8,128)S(1)} %add.100), channel_id=1, source_target_pairs={{0,8},{1,5},{2,10},{3,7},{4,12},{5,1},{6,14},{7,3},{8,0},{9,13},{1... | collective-permute-start | bytes 196616 | tf_op jit(solution)/shard_map/ppermute | solution.py:337
  56.3 4.5 %collective-permute-start.14 = (f32[32,512]{1,0:T(8,128)S(1)}, f32[32,512]{1,0:T(8,128)S(1)}, u32[]{:S(2)}, u32[]{:S(2)}) collective-permute-start(f32[32,512]{1,0:T(8,128)S(1)} %sub.17.refs_0_), channel_id=1, source_target_pairs={{0,4},{1,13},{2,6},{3,15},{4,0},{5,9},{6,2},{7,11},{8,12},{9,5},{1... | collective-permute-start | bytes 196616 | tf_op jit(solution)/shard_map/ppermute | solution.py:337
  58.3 4.5 %collective-permute-start.11 = (f32[32,512]{1,0:T(8,128)S(1)}, f32[32,512]{1,0:T(8,128)S(1)}, u32[]{:S(2)}, u32[]{:S(2)}) collective-permute-start(f32[32,512]{1,0:T(8,128)S(1)} %sub.16.refs_1_), channel_id=1, source_target_pairs={{0,4},{1,13},{2,6},{3,15},{4,0},{5,9},{6,2},{7,11},{8,12},{9,5},{1... | collective-permute-start | bytes 196616 | tf_op jit(solution)/shard_map/ppermute | solution.py:337
  65.3 5.8 %collective-permute-start.16 = (f32[32,1024]{1,0:T(8,128)S(1)}, f32[32,1024]{1,0:T(8,128)S(1)}, u32[]{:S(2)}, u32[]{:S(2)}) collective-permute-start(f32[32,1024]{1,0:T(8,128)S(1)} %add.102), channel_id=1, source_target_pairs={{0,2},{1,3},{2,0},{3,1},{4,6},{5,7},{6,4},{7,5},{8,10},{9,11},{10,... | collective-permute-start | bytes 393224 | tf_op jit(solution)/shard_map/ppermute | solution.py:330
  73.0 4.3 %collective-permute-start.21 = (f32[32,512]{1,0:T(8,128)S(1)}, f32[32,512]{1,0:T(8,128)S(1)}, u32[]{:S(2)}, u32[]{:S(2)}) collective-permute-start(f32[32,512]{1,0:T(8,128)S(1)} %products.56), channel_id=1, source_target_pairs={{0,4},{1,13},{2,6},{3,15},{4,0},{5,9},{6,2},{7,11},{8,12},{9,5},{1... | collective-permute-start | bytes 196616 | tf_op jit(solution)/shard_map/ppermute | solution.py:337
  74.2 4.8 %collective-permute-start.18 = (f32[32,512]{1,0:T(8,128)S(1)}, f32[32,512]{1,0:T(8,128)S(1)}, u32[]{:S(2)}, u32[]{:S(2)}) collective-permute-start(f32[32,512]{1,0:T(8,128)S(1)} %products.55), channel_id=1, source_target_pairs={{0,4},{1,13},{2,6},{3,15},{4,0},{5,9},{6,2},{7,11},{8,12},{9,5},{1... | collective-permute-start | bytes 196616 | tf_op jit(solution)/shard_map/ppermute | solution.py:337
  77.3 6.0 %collective-permute-start.22 = (f32[32,512]{1,0:T(8,128)S(1)}, f32[32,512]{1,0:T(8,128)S(1)}, u32[]{:S(2)}, u32[]{:S(2)}) collective-permute-start(f32[32,512]{1,0:T(8,128)S(1)} %add.106), channel_id=1, source_target_pairs={{0,8},{1,5},{2,10},{3,7},{4,12},{5,1},{6,14},{7,3},{8,0},{9,13},{1... | collective-permute-start | bytes 196616 | tf_op jit(solution)/shard_map/ppermute | solution.py:337
  79.0 6.0 %collective-permute-start.19 = (f32[32,512]{1,0:T(8,128)S(1)}, f32[32,512]{1,0:T(8,128)S(1)}, u32[]{:S(2)}, u32[]{:S(2)}) collective-permute-start(f32[32,512]{1,0:T(8,128)S(1)} %add.104), channel_id=1, source_target_pairs={{0,8},{1,5},{2,10},{3,7},{4,12},{5,1},{6,14},{7,3},{8,0},{9,13},{1... | collective-permute-start | bytes 196616 | tf_op jit(solution)/shard_map/ppermute | solution.py:337
  83.4 4.3 %collective-permute-start.23 = (f32[32,512]{1,0:T(8,128)S(1)}, f32[32,512]{1,0:T(8,128)S(1)}, u32[]{:S(2)}, u32[]{:S(2)}) collective-permute-start(f32[32,512]{1,0:T(8,128)S(1)} %add.107.refs_0_), channel_id=1, source_target_pairs={{0,4},{1,13},{2,6},{3,15},{4,0},{5,9},{6,2},{7,11},{8,12},{9,5},{1... | collective-permute-start | bytes 196616 | tf_op jit(solution)/shard_map/ppermute | solution.py:337
  85.0 4.6 %collective-permute-start.20 = (f32[32,512]{1,0:T(8,128)S(1)}, f32[32,512]{1,0:T(8,128)S(1)}, u32[]{:S(2)}, u32[]{:S(2)}) collective-permute-start(f32[32,512]{1,0:T(8,128)S(1)} %add.105.refs_1_), channel_id=1, source_target_pairs={{0,4},{1,13},{2,6},{3,15},{4,0},{5,9},{6,2},{7,11},{8,12},{9,5},{1... | collective-permute-start | bytes 196616 | tf_op jit(solution)/shard_map/ppermute | solution.py:337
  91.4 5.8 %collective-permute-start.25 = (f32[32,1024]{1,0:T(8,128)S(1)}, f32[32,1024]{1,0:T(8,128)S(1)}, u32[]{:S(2)}, u32[]{:S(2)}) collective-permute-start(f32[32,1024]{1,0:T(8,128)S(1)} %add.108), channel_id=1, source_target_pairs={{0,2},{1,3},{2,0},{3,1},{4,6},{5,7},{6,4},{7,5},{8,10},{9,11},{10,... | collective-permute-start | bytes 393224 | tf_op jit(solution)/shard_map/ppermute | solution.py:330
  98.9 4.3 %collective-permute-start.30 = (f32[32,512]{1,0:T(8,128)S(1)}, f32[32,512]{1,0:T(8,128)S(1)}, u32[]{:S(2)}, u32[]{:S(2)}) collective-permute-start(f32[32,512]{1,0:T(8,128)S(1)} %products.65), channel_id=1, source_target_pairs={{0,4},{1,13},{2,6},{3,15},{4,0},{5,9},{6,2},{7,11},{8,12},{9,5},{1... | collective-permute-start | bytes 196616 | tf_op jit(solution)/shard_map/ppermute | solution.py:337
  99.8 5.0 %collective-permute-start.27 = (f32[32,512]{1,0:T(8,128)S(1)}, f32[32,512]{1,0:T(8,128)S(1)}, u32[]{:S(2)}, u32[]{:S(2)}) collective-permute-start(f32[32,512]{1,0:T(8,128)S(1)} %products.64), channel_id=1, source_target_pairs={{0,4},{1,13},{2,6},{3,15},{4,0},{5,9},{6,2},{7,11},{8,12},{9,5},{1... | collective-permute-start | bytes 196616 | tf_op jit(solution)/shard_map/ppermute | solution.py:337
  103.2 6.6 %collective-permute-start.31 = (f32[32,512]{1,0:T(8,128)S(1)}, f32[32,512]{1,0:T(8,128)S(1)}, u32[]{:S(2)}, u32[]{:S(2)}) collective-permute-start(f32[32,512]{1,0:T(8,128)S(1)} %add.112), channel_id=1, source_target_pairs={{0,8},{1,5},{2,10},{3,7},{4,12},{5,1},{6,14},{7,3},{8,0},{9,13},{1... | collective-permute-start | bytes 196616 | tf_op jit(solution)/shard_map/ppermute | solution.py:337
  104.8 6.2 %collective-permute-start.28 = (f32[32,512]{1,0:T(8,128)S(1)}, f32[32,512]{1,0:T(8,128)S(1)}, u32[]{:S(2)}, u32[]{:S(2)}) collective-permute-start(f32[32,512]{1,0:T(8,128)S(1)} %add.110), channel_id=1, source_target_pairs={{0,8},{1,5},{2,10},{3,7},{4,12},{5,1},{6,14},{7,3},{8,0},{9,13},{1... | collective-permute-start | bytes 196616 | tf_op jit(solution)/shard_map/ppermute | solution.py:337
  109.9 4.3 %collective-permute-start.32 = (f32[32,512]{1,0:T(8,128)S(1)}, f32[32,512]{1,0:T(8,128)S(1)}, u32[]{:S(2)}, u32[]{:S(2)}) collective-permute-start(f32[32,512]{1,0:T(8,128)S(1)} %add.113.refs_0_.refs_4_), channel_id=1, source_target_pairs={{0,4},{1,13},{2,6},{3,15},{4,0},{5,9},{6,2},{7,11},{8,12},{9,5},{1... | collective-permute-start | bytes 196616 | tf_op jit(solution)/shard_map/ppermute | solution.py:337
  111.0 4.9 %collective-permute-start.29 = (f32[32,512]{1,0:T(8,128)S(1)}, f32[32,512]{1,0:T(8,128)S(1)}, u32[]{:S(2)}, u32[]{:S(2)}) collective-permute-start(f32[32,512]{1,0:T(8,128)S(1)} %add.111.refs_1_.refs_5_), channel_id=1, source_target_pairs={{0,4},{1,13},{2,6},{3,15},{4,0},{5,9},{6,2},{7,11},{8,12},{9,5},{1... | collective-permute-start | bytes 196616 | tf_op jit(solution)/shard_map/ppermute | solution.py:337
  118.2 5.8 %collective-permute-start.34 = (f32[32,1024]{1,0:T(8,128)S(1)}, f32[32,1024]{1,0:T(8,128)S(1)}, u32[]{:S(2)}, u32[]{:S(2)}) collective-permute-start(f32[32,1024]{1,0:T(8,128)S(1)} %add.114), channel_id=1, source_target_pairs={{0,2},{1,3},{2,0},{3,1},{4,6},{5,7},{6,4},{7,5},{8,10},{9,11},{10,... | collective-permute-start | bytes 393224 | tf_op jit(solution)/shard_map/ppermute | solution.py:330
  125.8 4.3 %collective-permute-start.36 = (f32[32,512]{1,0:T(8,128)S(1)}, f32[32,512]{1,0:T(8,128)S(1)}, u32[]{:S(2)}, u32[]{:S(2)}) collective-permute-start(f32[32,512]{1,0:T(8,128)S(1)} %products.72), channel_id=1, source_target_pairs={{0,4},{1,13},{2,6},{3,15},{4,0},{5,9},{6,2},{7,11},{8,12},{9,5},{1... | collective-permute-start | bytes 196616 | tf_op jit(solution)/shard_map/ppermute | solution.py:337
  126.1 5.4 %collective-permute-start.39 = (f32[32,512]{1,0:T(8,128)S(1)}, f32[32,512]{1,0:T(8,128)S(1)}, u32[]{:S(2)}, u32[]{:S(2)}) collective-permute-start(f32[32,512]{1,0:T(8,128)S(1)} %products.73), channel_id=1, source_target_pairs={{0,4},{1,13},{2,6},{3,15},{4,0},{5,9},{6,2},{7,11},{8,12},{9,5},{1... | collective-permute-start | bytes 196616 | tf_op jit(solution)/shard_map/ppermute | solution.py:337
  130.1 5.7 %collective-permute-start.37 = (f32[32,512]{1,0:T(8,128)S(1)}, f32[32,512]{1,0:T(8,128)S(1)}, u32[]{:S(2)}, u32[]{:S(2)}) collective-permute-start(f32[32,512]{1,0:T(8,128)S(1)} %add.116), channel_id=1, source_target_pairs={{0,8},{1,5},{2,10},{3,7},{4,12},{5,1},{6,14},{7,3},{8,0},{9,13},{1... | collective-permute-start | bytes 196616 | tf_op jit(solution)/shard_map/ppermute | solution.py:337
  131.5 5.9 %collective-permute-start.40 = (f32[32,512]{1,0:T(8,128)S(1)}, f32[32,512]{1,0:T(8,128)S(1)}, u32[]{:S(2)}, u32[]{:S(2)}) collective-permute-start(f32[32,512]{1,0:T(8,128)S(1)} %add.118), channel_id=1, source_target_pairs={{0,8},{1,5},{2,10},{3,7},{4,12},{5,1},{6,14},{7,3},{8,0},{9,13},{1... | collective-permute-start | bytes 196616 | tf_op jit(solution)/shard_map/ppermute | solution.py:337
  135.7 4.4 %collective-permute-start.38 = (f32[32,512]{1,0:T(8,128)S(1)}, f32[32,512]{1,0:T(8,128)S(1)}, u32[]{:S(2)}, u32[]{:S(2)}) collective-permute-start(f32[32,512]{1,0:T(8,128)S(1)} %add.117.refs_0_), channel_id=1, source_target_pairs={{0,4},{1,13},{2,6},{3,15},{4,0},{5,9},{6,2},{7,11},{8,12},{9,5},{1... | collective-permute-start | bytes 196616 | tf_op jit(solution)/shard_map/ppermute | solution.py:337
  137.4 4.6 %collective-permute-start.41 = (f32[32,512]{1,0:T(8,128)S(1)}, f32[32,512]{1,0:T(8,128)S(1)}, u32[]{:S(2)}, u32[]{:S(2)}) collective-permute-start(f32[32,512]{1,0:T(8,128)S(1)} %add.119.refs_1_), channel_id=1, source_target_pairs={{0,4},{1,13},{2,6},{3,15},{4,0},{5,9},{6,2},{7,11},{8,12},{9,5},{1... | collective-permute-start | bytes 196616 | tf_op jit(solution)/shard_map/ppermute | solution.py:337
  (11 other events, 23.2 us)

commit v6 on v5

--- a/solution.py
+++ b/solution.py
@@ -12,6 +12,7 @@
 COPIES = 8
 LANES = 128
 CHUNKS = 2
+FIRST = 2
 IN_VMEM = pl.BlockSpec(memory_space=pltpu.VMEM)
 IN_HBM = pl.BlockSpec(memory_space=pltpu.HBM)
 SHORT = pl.CostEstimate(flops=0, transcendentals=0, bytes_accessed=0)
@@ -27,28 +28,29 @@
     return size & (size - 1) == 0
 
 
-class Part(NamedTuple):
-    axis: str
+class Half(NamedTuple):
     away: int
-    chunk: int = 0
-    chunks: int = 1
 
     def span(self, extent):
-        width = extent // 2
-        at = lax.axis_index(self.axis)
-        if self.axis == "rows":
-            at = at >> (lax.axis_index("cols") & 1)
-        inner = width // self.chunks
-        start = ((at & 1) ^ self.away) * width + self.chunk * inner
-        return pl.ds(pl.multiple_of(start, LANES), inner)
+        width = self.width(extent)
+        at = (lax.axis_index("cols") & 1) ^ self.away
+        return pl.ds(pl.multiple_of(at * width, LANES), width)
 
     def width(self, extent):
-        return extent // (2 * self.chunks)
-
-
-class Whole(NamedTuple):
+        return extent // 2
+
+
+class Chunk(NamedTuple):
+    number: int
+    count: int
+
     def span(self, extent):
-        return pl.ds(0, extent)
+        return pl.ds(self.number * (extent - self.width(extent)), self.width(extent))
+
+    def width(self, extent):
+        if self.count == 1:
+            return extent
+        return extent // 2 + (1 * LANES if self.number == 0 else -1 * LANES)
 
 
 class Job(NamedTuple):
@@ -135,7 +137,7 @@
         out_specs=[IN_VMEM] * len(out_shape),
         scratch_shapes=scratch,
         input_output_aliases=aliases,
-        compiler_params=pltpu.CompilerParams(vmem_limit_bytes=2 << 20),
+        compiler_params=pltpu.CompilerParams(vmem_limit_bytes=6 << 20),
         cost_estimate=SHORT,
         name=("products" if job else "fetch") + ("_fetch" if job and bring else ""),
     )(*operands)
@@ -143,7 +145,7 @@
 
 def begin(axle_index, loads, blocks, out):
     rows, cols = blocks.shape[1:]
-    height = rows // 2
+    height = out.width(rows)
     count, positions = axle_index.shape[0], loads.shape[1]
     piece = rows // COPIES
     first = height // piece
@@ -204,7 +206,7 @@
             pltpu.SemaphoreType.DMA((2,)),
             pltpu.SemaphoreType.DMA((COPIES,)),
         ],
-        compiler_params=pltpu.CompilerParams(vmem_limit_bytes=3 << 20),
+        compiler_params=pltpu.CompilerParams(vmem_limit_bytes=6 << 20),
         cost_estimate=SHORT,
         name="begin",
     )(in_hbm(axle_index), in_hbm(loads), in_hbm(blocks))
@@ -229,7 +231,7 @@
         ],
         in_specs=[IN_VMEM, IN_VMEM],
         out_specs=[IN_VMEM] * len(found),
-        compiler_params=pltpu.CompilerParams(vmem_limit_bytes=2 << 20),
+        compiler_params=pltpu.CompilerParams(vmem_limit_bytes=6 << 20),
         cost_estimate=SHORT,
         name="select",
     )(selector, loads)
@@ -257,7 +259,7 @@
         out_specs=IN_HBM,
         scratch_shapes=[pltpu.SemaphoreType.DMA((len(pieces),))],
         input_output_aliases={len(pieces): 0} if held else {},
-        compiler_params=pltpu.CompilerParams(vmem_limit_bytes=2 << 20),
+        compiler_params=pltpu.CompilerParams(vmem_limit_bytes=6 << 20),
         cost_estimate=SHORT,
         name="place",
     )(*pieces, *held)
@@ -285,8 +287,10 @@
             found[:2] = [3, 1]
         return found
 
-    def parts(axis, away, chunks):
-        return [Part(axis, away, chunk, chunks) for chunk in range(chunks)]
+    own, away = Half(0), Half(1)
+
+    def pieces_of(count):
+        return [Chunk(number, count) for number in range(count)]
 
     def taking(bring):
         if not bring:
@@ -339,137 +343,141 @@
     def nothing():
         pass
 
-    def phase(
-        axis, chunks, finish, onward, early=nothing, middle=nothing, late=nothing, post=None, during=None
-    ):
-        every = range(chunks)
-        got = [permute(finish([i])[0], axis, 0) for i in every]
-        kept = finish([chunks + i for i in every], during)
-        more = early()
-        if more:
-            kept = [order.run(jnp.add, value, term) for value, term in zip(kept, more)]
-        last = len(steps(axis))
+    def settle(found):
+        value, place = found[-1]
+        if callable(value):
+            found[-1] = value(), place
+        return found
+
+    def onto(found, onward, late=nothing):
+        name, dims, outs, given = onward
+        given = given and given()
+        if given:
+            given = given + [None] * (len(outs) - len(given))
+        for vector, place in found[:-1]:
+            (vector,) = order.after(vector)
+            given = products([vector], [place], name, dims, given, outs)
+            late()
+            late = nothing
+        late()
+        settle(found)
+        (vector,), (place,) = order.after(found[-1][0]), found[-1][1:]
+
+        def finish(which, bring=None):
+            terms = given and [given[i] for i in which]
+            return products([vector], [place], name, dims, terms, [outs[i] for i in which], bring)
+
+        return finish
+
+    def cols_sum(finish, middle=nothing, post=None):
+        got = permute(finish([0])[0], "cols", 0)
+        (kept,) = finish([1])
+        last = len(steps("cols"))
         for number in range(1, last + 1):
-            sent = []
-            for i in every:
-                kept[i] = order.run(jnp.add, kept[i], got[i])
-                if number == last and post is not None:
-                    kept[i] = order.run(jnp.subtract, post()[i], kept[i])
-                sent.append(permute(kept[i], axis, number % last))
-            got = sent
+            kept = order.run(jnp.add, kept, got)
+            if number == last and post is not None:
+                kept = order.run(jnp.subtract, post(), kept)
+            got = permute(kept, "cols", number % last)
             if number < last:
                 middle()
                 middle = nothing
-        own, others = parts(axis, 0, chunks), parts(axis, 1, chunks)
-        if onward is None:
-            late(kept)
-            return kept, got, None
-        name, dims, next_chunks, given = onward
-        away = "cols" if axis == "rows" else "rows"
-        outs = parts(away, 1, next_chunks) + parts(away, 0, next_chunks)
-        extra = given and given()
-        given = products(kept, own, name, dims, extra and extra + [None] * (len(outs) - len(extra)), outs)
-        late()
-        for i in every[:-1]:
-            (got[i],) = order.after(got[i])
-            given = products(got[i : i + 1], others[i : i + 1], name, dims, given, outs)
-        (got[-1],) = order.after(got[-1])
-
-        def rest(which, bring=None):
-            terms = [given[i] for i in which]
-            return products(
-                got[-1:], others[-1:], name, dims, terms, [outs[i] for i in which], bring
-            )
-
-        return kept, got, rest
+        return [(kept, own), (got, away)]
+
+    def rows_sum(finish, count, early=nothing, middle=nothing, post=None, during=None):
+        every = range(count)
+        kept, got = [], []
+        for i in every:
+            kept += finish([i], during if i == count - 1 else None)
+            got.append(permute(kept[i], "rows", 0))
+        more = early()
+        last = len(steps("rows"))
+        for number in range(1, last + 1):
+            for i in every[:-1] if number == last else every:
+                if more and number == 1:
+                    kept[i] = order.run(jnp.add, kept[i], more[i])
+                kept[i] = order.run(jnp.add, kept[i], got[i])
+                if number < last:
+                    got[i] = permute(kept[i], "rows", number)
+                elif post is not None:
+                    kept[i] = order.run(jnp.subtract, post()[i], kept[i])
+            if number < last:
+                middle()
+                middle = nothing
+
+        def rest():
+            value = order.run(jnp.add, kept[-1], got[-1])
+            return value if post is None else order.run(jnp.subtract, post()[-1], value)
+
+        return list(zip(kept[:-1] + [rest], pieces_of(count)))
 
     def pair(high, low):
         return "coupling", pair_index(high, low)
 
-    chunks = {level: 1 if level == 1 else CHUNKS for level in range(1, LEVELS)}
+    chunks = {level: FIRST if level == 1 else CHUNKS for level in range(1, LEVELS)}
     selector, vector, first, blocks["diag", 0] = order.run(
-        lambda: begin(axle_index, loads, diag_inverse, Part("cols", 1))
+        lambda: begin(axle_index, loads, diag_inverse, away)
     )
     rhs, solved, answers, skipped, done = {}, {}, {}, {}, {}
 
-    def first_finish(which, bring=None):
+    def first_finish(which):
         if which == [0]:
             return [first]
-        return products([vector], [Whole()], ("diag", 0), LOWER, None, [Part("cols", 0)])
+        return products([vector], pieces_of(1), ("diag", 0), LOWER, None, [own])
 
     def prepare():
         del blocks["diag", 0]
-        wanted = {level: parts("rows", 0, count) for level, count in chunks.items()}
+        wanted = {level: pieces_of(count) for level, count in chunks.items()}
         rhs.update(order.run(lambda a, b: select(a, b, wanted), selector, loads))
         fetch(pair(1, 0))()
 
-    def skip_forward(away, bring=None):
-        def call():
-            places = parts("cols", 0, 1) + parts("cols", 1, 1)
-            skipped[LOWER, away] = products(
-                sum(solved[0], []), places, pair(2, 0), LOWER, None, parts("rows", away, chunks[2]), bring
-            )
-            return skipped[LOWER, away]
-
-        return call
+    def skip(found, dims, outs):
+        vectors, places = zip(*found)
+        skipped[dims] = products(list(vectors), list(places), pair(2, 0), dims, None, outs)
+
+    def skip_forward():
+        skip(solved[0], LOWER, pieces_of(chunks[2]))
 
     def skip_backward():
-        outs = parts("cols", 1, 1) + parts("cols", 0, 1)
-        places = parts("rows", 0, CHUNKS) + parts("rows", 1, CHUNKS)
-        skipped[UPPER] = products(sum(answers[2], []), places, pair(2, 0), UPPER, None, outs)
-
-    def put(found, levels, axis, count, halves=(0, 1), held=()):
-        width = diag_inverse.shape[2 if axis == "rows" else 1]
-        pieces = [piece for level in levels for half in halves for piece in found[level][half]]
-        targets = [
-            (level, part) for level in levels for half in halves for part in parts(axis, half, count)
-        ]
-        number = len(pieces)
+        skip(answers[2], UPPER, [away, own])
+
+    def put(found, levels, width, held=()):
+        flat = [(value, (level, part)) for level in levels for value, part in found[level]]
+        values, targets = zip(*flat)
+        number = len(values)
         return order.run(
-            lambda *values: place(values[:number], targets, width, values[number:]), *pieces, *held
+            lambda *values: place(values[:number], targets, width, values[number:]), *values, *held
         )
 
     def put_forward():
-        done["forward"] = put(solved, range(LEVELS), "cols", 1)
+        done["forward"] = put(solved, range(LEVELS), diag_inverse.shape[1])
 
     def put_early():
-        done["early"] = put(answers, [2, 1], "rows", CHUNKS)
-
-    def put_own(kept):
-        done["own"] = put({0: [kept]}, [0], "rows", CHUNKS, [0], [done["early"]])
-
-    *solved[0], finish = phase(
-        "cols", 1, first_finish, (pair(1, 0), LOWER, chunks[1], None), middle=prepare
+        done["early"] = put(answers, [2, 1], diag_inverse.shape[2])
+
+    halves = [away, own]
+    solved[0] = cols_sum(first_finish, prepare)
+    finish = onto(solved[0], (pair(1, 0), LOWER, pieces_of(chunks[1]), None))
+    whole = range(COPIES)
+    found = rows_sum(
+        finish, chunks[1], nothing, fetch(pair(2, 0)), lambda: rhs[1], (("diag", 1), whole)
     )
-    *_, finish = phase(
-        "rows", chunks[1], finish, (("diag", 1), LOWER, 1, None),
-        middle=fetch(pair(2, 0)), late=skip_forward(1), post=lambda: rhs[1],
-        during=(("diag", 1), range(COPIES)),
-    )
-    *solved[1], finish = phase(
-        "cols", 1, finish, (pair(2, 1), LOWER, chunks[2], lambda: skipped[LOWER, 1]),
-        middle=fetch(pair(2, 1)),
-    )
-    *_, finish = phase(
-        "rows", chunks[2], finish, (("diag", 2), LOWER, 1, None),
-        early=skip_forward(0), middle=fetch(("diag", 2)), post=lambda: rhs[2],
-    )
-    *solved[2], finish = phase("cols", 1, finish, (("diag", 2), UPPER, CHUNKS, None))
-    *answers[2], finish = phase("rows", CHUNKS, finish, (pair(2, 1), UPPER, 1, None))
-    *_, finish = phase(
-        "cols", 1, finish, (("diag", 1), UPPER, CHUNKS, None),
-        middle=skip_backward, post=lambda: solved[1][0],
-    )
-    *answers[1], finish = phase(
-        "rows", CHUNKS, finish, (pair(1, 0), UPPER, 1, lambda: skipped[UPPER]),
-        middle=fetch(("diag", 0)),
-    )
-    *_, finish = phase(
-        "cols", 1, finish, (("diag", 0), UPPER, CHUNKS, None),
-        middle=put_forward, post=lambda: solved[0][0],
-    )
-    *answers[0], _ = phase("rows", CHUNKS, finish, None, middle=put_early, late=put_own)
-    influence = put(answers, [0], "rows", CHUNKS, [1], [done["own"]])
+    finish = onto(found, (("diag", 1), LOWER, halves, None), skip_forward)
+    solved[1] = cols_sum(finish, fetch(pair(2, 1)))
+    finish = onto(solved[1], (pair(2, 1), LOWER, pieces_of(chunks[2]), lambda: skipped[LOWER]))
+    found = rows_sum(finish, chunks[2], nothing, fetch(("diag", 2)), lambda: rhs[2])
+    finish = onto(found, (("diag", 2), LOWER, halves, None))
+    solved[2] = cols_sum(finish)
+    finish = onto(solved[2], (("diag", 2), UPPER, pieces_of(CHUNKS), None))
+    answers[2] = rows_sum(finish, CHUNKS)
+    finish = onto(answers[2], (pair(2, 1), UPPER, halves, None))
+    found = cols_sum(finish, skip_backward, lambda: solved[1][0][0])
+    finish = onto(found, (("diag", 1), UPPER, pieces_of(CHUNKS), None))
+    answers[1] = rows_sum(finish, CHUNKS, middle=fetch(("diag", 0)))
+    finish = onto(answers[1], (pair(1, 0), UPPER, halves, lambda: skipped[UPPER]))
+    found = cols_sum(finish, put_forward, lambda: solved[0][0][0])
+    finish = onto(found, (("diag", 0), UPPER, pieces_of(CHUNKS), None))
+    answers[0] = settle(rows_sum(finish, CHUNKS, middle=put_early))
+    influence = put(answers, [0], diag_inverse.shape[2], [done["early"]])
     return influence, done["forward"]
 
 

time: 143 us -> 142 us (level)
  starting transfers between devices: 44.9 us -> 39.3 us
  waiting for transfers between devices: 42.7 us -> 47.9 us
    ppermute x27 -> x20, waiting for transfers between devices: 27.1 us -> 32.4 us  [permute(): return lax.ppermute(value, ('rows', 'cols'), moves)]
    ppermute x27 -> x20, starting transfers between devices: 31.6 us -> 27.6 us  [permute(): return lax.ppermute(value, ('rows', 'cols'), moves)]
    ppermute x15, starting transfers between devices: 13.4 us -> 11.7 us  [permute(): lax.ppermute(value, axis, [(i, i ^ step) for i in range(sizes[axis])])]
    pallas_call x4 -> x3, Pallas kernels: 3.1 us -> 2.45 us  [place(): pl.pallas_call(kernel, out_shape=jax.ShapeDtypeStruct((LEVELS, rows, widt...]
    pallas_call x43 -> x35, Pallas kernels: 46.4 us -> 45.9 us  [work(): pl.pallas_call(kernel, out_shape=out_shape, in_specs=in_specs, out_specs=...]
  transfers between devices with their start and end apart: 42 -> 35, of which waited for: 32 -> 27; matrix products, arithmetic and copies ran while one was open for 0% -> 0% of each run, Pallas kernels for 32% -> 30%
where the time goes in v6:
time: 142 us; the launch traced here: 141 us
  Pallas kernels  52.4 us (37%)
  waiting for transfers between devices  47.9 us (34%)
  starting transfers between devices  39.3 us (28%)
    pallas_call x35, Pallas kernels, work(): pl.pallas_call(kernel, out_shape=out_shape, in_specs=in_specs, out_specs=...  45.9 us
    ppermute x20, waiting for transfers between devices, permute(): return lax.ppermute(value, ('rows', 'cols'), moves)  32.4 us
    ppermute x20, starting transfers between devices, permute(): return lax.ppermute(value, ('rows', 'cols'), moves)  27.6 us
    ppermute x15, waiting for transfers between devices, permute(): lax.ppermute(value, axis, [(i, i ^ step) for i in range(sizes[axis])])  15.4 us
    ppermute x15, starting transfers between devices, permute(): lax.ppermute(value, axis, [(i, i ^ step) for i in range(sizes[axis])])  11.7 us
    pallas_call x1, Pallas kernels, begin(): pl.pallas_call(kernel, out_shape=(jax.ShapeDtypeStruct((count, positions)...  3.78 us
  transfers between devices with their start and end apart: 35, of which 27 were waited for; matrix products, arithmetic and copies ran while one was open for 0% of the time, Pallas kernels for 30%

profile of v6, /device:TPU:0, one launch (start us, length us, event | category | flops | bytes accessed | tf_op | source)
XLA Modules:
  0.0 141.5 jit_solution(3167906483485930736)
XLA Ops:
  0.6 3.8 %begin.1 = (f32[32,128]{1,0:T(8,128)S(1)}, f32[32,2048]{1,0:T(8,128)S(1)}, f32[32,1024]{1,0:T(8,128)S(1)}, bf16[2048,2048]{1,0:T(8,128)(2,1)S(1)}) custom-call(s32[32]{0:T(128)} %index_ref.1, bf16[3,128,2048]{2,1,0:T(8,128)(2,1)} %loads_ref.2, bf16[3,2048,2048]{2,1,0:T(8,128)(2,1)} %refs_0_.9), custom_call_target="tpu_custom_call" | custom-call | tf_op jit(solution)/shard_map/begin/pallas_call | solution.py:193
  6.3 2.6 %collective-permute-start.1 = (f32[32,1024]{1,0:T(8,128)S(1)}, f32[32,1024]{1,0:T(8,128)S(1)}, u32[]{:S(2)}, u32[]{:S(2)}) collective-permute-start(f32[32,1024]{1,0:T(8,128)S(1)} %add.90), channel_id=1, source_target_pairs={{0,2},{1,3},{2,0},{3,1},{4,6},{5,7},{6,4},{7,5},{8,10},{9,11},{10,... | collective-permute-start | bytes 393224 | tf_op jit(solution)/shard_map/ppermute | solution.py:334
  8.9 3.5 %fetch.5.refs_1_.refs_2_.refs_3_ = bf16[2048,2048]{1,0:T(8,128)(2,1)S(1)} custom-call(bf16[3,2048,2048]{2,1,0:T(8,128)(2,1)} %refs_0_.7), custom_call_target="tpu_custom_call" | custom-call | tf_op jit(solution)/shard_map/fetch/pallas_call | solution.py:133
  15.3 1.9 %collective-permute-start.5 = (f32[32,1152]{1,0:T(8,128)S(1)}, f32[32,1152]{1,0:T(8,128)S(1)}, u32[]{:S(2)}, u32[]{:S(2)}) collective-permute-start(f32[32,1152]{1,0:T(8,128)S(1)} %products.31), channel_id=1, source_target_pairs={{0,4},{1,13},{2,6},{3,15},{4,0},{5,9},{6,2},{7,11},{8,12},{9,5},{1... | collective-permute-start | bytes 442376 | tf_op jit(solution)/shard_map/ppermute | solution.py:341
  17.1 3.6 %products_fetch.1 = (f32[32,896]{1,0:T(8,128)S(1)}, bf16[2048,2048]{1,0:T(8,128)(2,1)S(1)}) custom-call(f32[32,1024]{1,0:T(8,128)S(1)} %collective-permute-done.2.refs_0_.refs_1_, f32[32,896]{1,0:T(8,128)S(1)} %get-tuple-element.267.refs_1_, bf16[2048,2048]{1,0:T(8,128)(2,1)S(1)} %fetch.5.refs_1_.refs_2_.refs_3_, bf16[3,2048,2048]{2,1,0:T(8,128)(2,1)} %refs_0_.9), custom_call_target="tpu_custom_call" | custom-call | tf_op jit(solution)/shard_map/products_fetch/pallas_call | solution.py:133
  21.0 3.3 %collective-permute-start.6 = (f32[32,1152]{1,0:T(8,128)S(1)}, f32[32,1152]{1,0:T(8,128)S(1)}, u32[]{:S(2)}, u32[]{:S(2)}) collective-permute-start(f32[32,1152]{1,0:T(8,128)S(1)} %add.93), channel_id=1, source_target_pairs={{0,8},{1,5},{2,10},{3,7},{4,12},{5,1},{6,14},{7,3},{8,0},{9,13},{1... | collective-permute-start | bytes 442376 | tf_op jit(solution)/shard_map/ppermute | solution.py:341
  25.6 2.8 %collective-permute-start.4 = (f32[32,896]{1,0:T(8,128)S(1)}, f32[32,896]{1,0:T(8,128)S(1)}, u32[]{:S(2)}, u32[]{:S(2)}) collective-permute-start(f32[32,896]{1,0:T(8,128)S(1)} %add.92), channel_id=1, source_target_pairs={{0,8},{1,5},{2,10},{3,7},{4,12},{5,1},{6,14},{7,3},{8,0},{9,13},{1... | collective-permute-start | bytes 344072 | tf_op jit(solution)/shard_map/ppermute | solution.py:341
  28.5 3.5 %fetch.6.refs_2_ = bf16[2048,2048]{1,0:T(8,128)(2,1)S(1)} custom-call(bf16[3,2048,2048]{2,1,0:T(8,128)(2,1)} %refs_0_.7), custom_call_target="tpu_custom_call" | custom-call | tf_op jit(solution)/shard_map/fetch/pallas_call | solution.py:133
  33.8 2.5 %products.33 = (f32[32,1152]{1,0:T(8,128)S(1)}, f32[32,896]{1,0:T(8,128)S(1)}) custom-call(f32[32,1024]{1,0:T(8,128)S(1)} %add.91.refs_0_, f32[32,1024]{1,0:T(8,128)S(1)} %collective-permute-done.2.refs_0_.refs_1_, bf16[2048,2048]{1,0:T(8,128)(2,1)S(1)} %fetch.6.refs_2_), custom_call_target="tpu_custom_call" | custom-call | tf_op jit(solution)/shard_map/products/pallas_call | solution.py:133
  37.1 1.7 %collective-permute-start.7 = (f32[32,1024]{1,0:T(8,128)S(1)}, f32[32,1024]{1,0:T(8,128)S(1)}, u32[]{:S(2)}, u32[]{:S(2)}) collective-permute-start(f32[32,1024]{1,0:T(8,128)S(1)} %products.35), channel_id=1, source_target_pairs={{0,1},{1,0},{2,3},{3,2},{4,5},{5,4},{6,7},{7,6},{8,9},{9,8},{10,11... | collective-permute-start | bytes 393224 | tf_op jit(solution)/shard_map/ppermute | solution.py:334
  39.8 1.6 %collective-permute-start.8 = (f32[32,1024]{1,0:T(8,128)S(1)}, f32[32,1024]{1,0:T(8,128)S(1)}, u32[]{:S(2)}, u32[]{:S(2)}) collective-permute-start(f32[32,1024]{1,0:T(8,128)S(1)} %add.96), channel_id=1, source_target_pairs={{0,2},{1,3},{2,0},{3,1},{4,6},{5,7},{6,4},{7,5},{8,10},{9,11},{10,... | collective-permute-start | bytes 393224 | tf_op jit(solution)/shard_map/ppermute | solution.py:334
  41.4 3.5 %fetch.7.refs_3_.refs_2_.refs_1_ = bf16[2048,2048]{1,0:T(8,128)(2,1)S(1)} custom-call(bf16[3,2048,2048]{2,1,0:T(8,128)(2,1)} %refs_0_.7), custom_call_target="tpu_custom_call" | custom-call | tf_op jit(solution)/shard_map/fetch/pallas_call | solution.py:133
  50.7 2.6 %collective-permute-done.12 = f32[32,1152]{1,0:T(8,128)S(1)} collective-permute-done((f32[32,1152]{1,0:T(8,128)S(1)}, f32[32,1152]{1,0:T(8,128)S(1)}, u32[]{:S(2)}, u32[]{:S(2)}) %collective-permute-start.12) | collective-permute-done | bytes 147488 | tf_op jit(solution)/shard_map/ppermute | solution.py:341
  53.4 3.9 %collective-permute-done.10 = f32[32,896]{1,0:T(8,128)S(1)} collective-permute-done((f32[32,896]{1,0:T(8,128)S(1)}, f32[32,896]{1,0:T(8,128)S(1)}, u32[]{:S(2)}, u32[]{:S(2)}) %collective-permute-start.10) | collective-permute-done | bytes 114720 | tf_op jit(solution)/shard_map/ppermute | solution.py:341
  57.4 3.5 %fetch.8.refs_1_.refs_2_ = bf16[2048,2048]{1,0:T(8,128)(2,1)S(1)} custom-call(bf16[3,2048,2048]{2,1,0:T(8,128)(2,1)} %refs_0_.9), custom_call_target="tpu_custom_call" | custom-call | tf_op jit(solution)/shard_map/fetch/pallas_call | solution.py:133
  67.7 4.0 %collective-permute-done.15 = f32[32,1024]{1,0:T(8,128)S(1)} collective-permute-done((f32[32,1024]{1,0:T(8,128)S(1)}, f32[32,1024]{1,0:T(8,128)S(1)}, u32[]{:S(2)}, u32[]{:S(2)}) %collective-permute-start.15) | collective-permute-done | bytes 131104 | tf_op jit(solution)/shard_map/ppermute | solution.py:334
  74.4 1.9 %collective-permute-start.17 = (f32[32,896]{1,0:T(8,128)S(1)}, f32[32,896]{1,0:T(8,128)S(1)}, u32[]{:S(2)}, u32[]{:S(2)}) collective-permute-start(f32[32,896]{1,0:T(8,128)S(1)} %products.43), channel_id=1, source_target_pairs={{0,4},{1,13},{2,6},{3,15},{4,0},{5,9},{6,2},{7,11},{8,12},{9,5},{1... | collective-permute-start | bytes 344072 | tf_op jit(solution)/shard_map/ppermute | solution.py:341
  76.3 3.2 %collective-permute-done.19 = f32[32,1152]{1,0:T(8,128)S(1)} collective-permute-done((f32[32,1152]{1,0:T(8,128)S(1)}, f32[32,1152]{1,0:T(8,128)S(1)}, u32[]{:S(2)}, u32[]{:S(2)}) %collective-permute-start.19) | collective-permute-done | bytes 147488 | tf_op jit(solution)/shard_map/ppermute | solution.py:341
  79.5 2.3 %collective-permute-start.20 = (f32[32,1152]{1,0:T(8,128)S(1)}, f32[32,1152]{1,0:T(8,128)S(1)}, u32[]{:S(2)}, u32[]{:S(2)}) collective-permute-start(f32[32,1152]{1,0:T(8,128)S(1)} %add.105), channel_id=1, source_target_pairs={{0,8},{1,5},{2,10},{3,7},{4,12},{5,1},{6,14},{7,3},{8,0},{9,13},{1... | collective-permute-start | bytes 442376 | tf_op jit(solution)/shard_map/ppermute | solution.py:341
  82.0 2.3 %collective-permute-start.18 = (f32[32,896]{1,0:T(8,128)S(1)}, f32[32,896]{1,0:T(8,128)S(1)}, u32[]{:S(2)}, u32[]{:S(2)}) collective-permute-start(f32[32,896]{1,0:T(8,128)S(1)} %add.104), channel_id=1, source_target_pairs={{0,8},{1,5},{2,10},{3,7},{4,12},{5,1},{6,14},{7,3},{8,0},{9,13},{1... | collective-permute-start | bytes 344072 | tf_op jit(solution)/shard_map/ppermute | solution.py:341
  84.3 2.8 %collective-permute-done.20 = f32[32,1152]{1,0:T(8,128)S(1)} collective-permute-done((f32[32,1152]{1,0:T(8,128)S(1)}, f32[32,1152]{1,0:T(8,128)S(1)}, u32[]{:S(2)}, u32[]{:S(2)}) %collective-permute-start.20) | collective-permute-done | bytes 147488 | tf_op jit(solution)/shard_map/ppermute | solution.py:341
  94.6 2.5 %collective-permute-done.22 = f32[32,1024]{1,0:T(8,128)S(1)} collective-permute-done((f32[32,1024]{1,0:T(8,128)S(1)}, f32[32,1024]{1,0:T(8,128)S(1)}, u32[]{:S(2)}, u32[]{:S(2)}) %collective-permute-start.22) | collective-permute-done | bytes 131104 | tf_op jit(solution)/shard_map/ppermute | solution.py:334
  100.0 1.7 %collective-permute-start.24 = (f32[32,896]{1,0:T(8,128)S(1)}, f32[32,896]{1,0:T(8,128)S(1)}, u32[]{:S(2)}, u32[]{:S(2)}) collective-permute-start(f32[32,896]{1,0:T(8,128)S(1)} %products.50), channel_id=1, source_target_pairs={{0,4},{1,13},{2,6},{3,15},{4,0},{5,9},{6,2},{7,11},{8,12},{9,5},{1... | collective-permute-start | bytes 344072 | tf_op jit(solution)/shard_map/ppermute | solution.py:341
  101.7 3.3 %collective-permute-done.26 = f32[32,1152]{1,0:T(8,128)S(1)} collective-permute-done((f32[32,1152]{1,0:T(8,128)S(1)}, f32[32,1152]{1,0:T(8,128)S(1)}, u32[]{:S(2)}, u32[]{:S(2)}) %collective-permute-start.26) | collective-permute-done | bytes 147488 | tf_op jit(solution)/shard_map/ppermute | solution.py:341
  105.0 1.7 %collective-permute-start.27 = (f32[32,1152]{1,0:T(8,128)S(1)}, f32[32,1152]{1,0:T(8,128)S(1)}, u32[]{:S(2)}, u32[]{:S(2)}) collective-permute-start(f32[32,1152]{1,0:T(8,128)S(1)} %add.111), channel_id=1, source_target_pairs={{0,8},{1,5},{2,10},{3,7},{4,12},{5,1},{6,14},{7,3},{8,0},{9,13},{1... | collective-permute-start | bytes 442376 | tf_op jit(solution)/shard_map/ppermute | solution.py:341
  107.5 1.7 %collective-permute-start.25 = (f32[32,896]{1,0:T(8,128)S(1)}, f32[32,896]{1,0:T(8,128)S(1)}, u32[]{:S(2)}, u32[]{:S(2)}) collective-permute-start(f32[32,896]{1,0:T(8,128)S(1)} %add.110), channel_id=1, source_target_pairs={{0,8},{1,5},{2,10},{3,7},{4,12},{5,1},{6,14},{7,3},{8,0},{9,13},{1... | collective-permute-start | bytes 344072 | tf_op jit(solution)/shard_map/ppermute | solution.py:341
  109.2 3.5 %fetch.9.refs_1_.refs_2_ = bf16[2048,2048]{1,0:T(8,128)(2,1)S(1)} custom-call(bf16[3,2048,2048]{2,1,0:T(8,128)(2,1)} %refs_0_.9), custom_call_target="tpu_custom_call" | custom-call | tf_op jit(solution)/shard_map/fetch/pallas_call | solution.py:133
  119.5 3.1 %collective-permute-done.29 = f32[32,1024]{1,0:T(8,128)S(1)} collective-permute-done((f32[32,1024]{1,0:T(8,128)S(1)}, f32[32,1024]{1,0:T(8,128)S(1)}, u32[]{:S(2)}, u32[]{:S(2)}) %collective-permute-start.29) | collective-permute-done | bytes 131104 | tf_op jit(solution)/shard_map/ppermute | solution.py:334
  125.1 2.1 %collective-permute-start.33 = (f32[32,896]{1,0:T(8,128)S(1)}, f32[32,896]{1,0:T(8,128)S(1)}, u32[]{:S(2)}, u32[]{:S(2)}) collective-permute-start(f32[32,896]{1,0:T(8,128)S(1)} %products.57), channel_id=1, source_target_pairs={{0,4},{1,13},{2,6},{3,15},{4,0},{5,9},{6,2},{7,11},{8,12},{9,5},{1... | collective-permute-start | bytes 344072 | tf_op jit(solution)/shard_map/ppermute | solution.py:341
  127.2 3.3 %collective-permute-done.31 = f32[32,1152]{1,0:T(8,128)S(1)} collective-permute-done((f32[32,1152]{1,0:T(8,128)S(1)}, f32[32,1152]{1,0:T(8,128)S(1)}, u32[]{:S(2)}, u32[]{:S(2)}) %collective-permute-start.31) | collective-permute-done | bytes 147488 | tf_op jit(solution)/shard_map/ppermute | solution.py:341
  135.1 3.0 %collective-permute-done.32 = f32[32,1152]{1,0:T(8,128)S(1)} collective-permute-done((f32[32,1152]{1,0:T(8,128)S(1)}, f32[32,1152]{1,0:T(8,128)S(1)}, u32[]{:S(2)}, u32[]{:S(2)}) %collective-permute-start.32) | collective-permute-done | bytes 147488 | tf_op jit(solution)/shard_map/ppermute | solution.py:341
  138.2 2.4 %collective-permute-done.34 = f32[32,896]{1,0:T(8,128)S(1)} collective-permute-done((f32[32,896]{1,0:T(8,128)S(1)}, f32[32,896]{1,0:T(8,128)S(1)}, u32[]{:S(2)}, u32[]{:S(2)}) %collective-permute-start.34) | collective-permute-done | bytes 114720 | tf_op jit(solution)/shard_map/ppermute | solution.py:341
  (116 shorter events, 51.1 us)
Async XLA Ops:
  4.4 1.9 %collective-permute-start = (f32[32,1024]{1,0:T(8,128)S(1)}, f32[32,1024]{1,0:T(8,128)S(1)}, u32[]{:S(2)}, u32[]{:S(2)}) collective-permute-start(f32[32,1024]{1,0:T(8,128)S(1)} %get-tuple-element.251), channel_id=1, source_target_pairs={{0,1},{1,0},{2,3},{3,2},{4,5},{5,4},{6,7},{7,6},{8,9},{9,8},{10,11... | collective-permute-start | bytes 393224 | tf_op jit(solution)/shard_map/ppermute | solution.py:334
  6.3 6.7 %collective-permute-start.1 = (f32[32,1024]{1,0:T(8,128)S(1)}, f32[32,1024]{1,0:T(8,128)S(1)}, u32[]{:S(2)}, u32[]{:S(2)}) collective-permute-start(f32[32,1024]{1,0:T(8,128)S(1)} %add.90), channel_id=1, source_target_pairs={{0,2},{1,3},{2,0},{3,1},{4,6},{5,7},{6,4},{7,5},{8,10},{9,11},{10,... | collective-permute-start | bytes 393224 | tf_op jit(solution)/shard_map/ppermute | solution.py:334
  13.0 1.4 %collective-permute-start.2 = (f32[32,1024]{1,0:T(8,128)S(1)}, f32[32,1024]{1,0:T(8,128)S(1)}, u32[]{:S(2)}, u32[]{:S(2)}) collective-permute-start(f32[32,1024]{1,0:T(8,128)S(1)} %add.91.refs_0_), channel_id=1, source_target_pairs={{0,1},{1,0},{2,3},{3,2},{4,5},{5,4},{6,7},{7,6},{8,9},{9,8},{10,11... | collective-permute-start | bytes 393224 | tf_op jit(solution)/shard_map/ppermute | solution.py:334
  15.3 5.8 %collective-permute-start.5 = (f32[32,1152]{1,0:T(8,128)S(1)}, f32[32,1152]{1,0:T(8,128)S(1)}, u32[]{:S(2)}, u32[]{:S(2)}) collective-permute-start(f32[32,1152]{1,0:T(8,128)S(1)} %products.31), channel_id=1, source_target_pairs={{0,4},{1,13},{2,6},{3,15},{4,0},{5,9},{6,2},{7,11},{8,12},{9,5},{1... | collective-permute-start | bytes 442376 | tf_op jit(solution)/shard_map/ppermute | solution.py:341
  20.8 4.9 %collective-permute-start.3 = (f32[32,896]{1,0:T(8,128)S(1)}, f32[32,896]{1,0:T(8,128)S(1)}, u32[]{:S(2)}, u32[]{:S(2)}) collective-permute-start(f32[32,896]{1,0:T(8,128)S(1)} %get-tuple-element.272), channel_id=1, source_target_pairs={{0,4},{1,13},{2,6},{3,15},{4,0},{5,9},{6,2},{7,11},{8,12},{9,5},{1... | collective-permute-start | bytes 344072 | tf_op jit(solution)/shard_map/ppermute | solution.py:341
  21.0 11.2 %collective-permute-start.6 = (f32[32,1152]{1,0:T(8,128)S(1)}, f32[32,1152]{1,0:T(8,128)S(1)}, u32[]{:S(2)}, u32[]{:S(2)}) collective-permute-start(f32[32,1152]{1,0:T(8,128)S(1)} %add.93), channel_id=1, source_target_pairs={{0,8},{1,5},{2,10},{3,7},{4,12},{5,1},{6,14},{7,3},{8,0},{9,13},{1... | collective-permute-start | bytes 442376 | tf_op jit(solution)/shard_map/ppermute | solution.py:341
  25.6 10.7 %collective-permute-start.4 = (f32[32,896]{1,0:T(8,128)S(1)}, f32[32,896]{1,0:T(8,128)S(1)}, u32[]{:S(2)}, u32[]{:S(2)}) collective-permute-start(f32[32,896]{1,0:T(8,128)S(1)} %add.92), channel_id=1, source_target_pairs={{0,8},{1,5},{2,10},{3,7},{4,12},{5,1},{6,14},{7,3},{8,0},{9,13},{1... | collective-permute-start | bytes 344072 | tf_op jit(solution)/shard_map/ppermute | solution.py:341
  37.1 2.7 %collective-permute-start.7 = (f32[32,1024]{1,0:T(8,128)S(1)}, f32[32,1024]{1,0:T(8,128)S(1)}, u32[]{:S(2)}, u32[]{:S(2)}) collective-permute-start(f32[32,1024]{1,0:T(8,128)S(1)} %products.35), channel_id=1, source_target_pairs={{0,1},{1,0},{2,3},{3,2},{4,5},{5,4},{6,7},{7,6},{8,9},{9,8},{10,11... | collective-permute-start | bytes 393224 | tf_op jit(solution)/shard_map/ppermute | solution.py:334
  39.8 5.8 %collective-permute-start.8 = (f32[32,1024]{1,0:T(8,128)S(1)}, f32[32,1024]{1,0:T(8,128)S(1)}, u32[]{:S(2)}, u32[]{:S(2)}) collective-permute-start(f32[32,1024]{1,0:T(8,128)S(1)} %add.96), channel_id=1, source_target_pairs={{0,2},{1,3},{2,0},{3,1},{4,6},{5,7},{6,4},{7,5},{8,10},{9,11},{10,... | collective-permute-start | bytes 393224 | tf_op jit(solution)/shard_map/ppermute | solution.py:334
  45.7 1.4 collective-permute-start.9
  47.9 5.4 %collective-permute-start.12 = (f32[32,1152]{1,0:T(8,128)S(1)}, f32[32,1152]{1,0:T(8,128)S(1)}, u32[]{:S(2)}, u32[]{:S(2)}) collective-permute-start(f32[32,1152]{1,0:T(8,128)S(1)} %products.38), channel_id=1, source_target_pairs={{0,4},{1,13},{2,6},{3,15},{4,0},{5,9},{6,2},{7,11},{8,12},{9,5},{1... | collective-permute-start | bytes 442376 | tf_op jit(solution)/shard_map/ppermute | solution.py:341
  50.0 7.3 %collective-permute-start.10 = (f32[32,896]{1,0:T(8,128)S(1)}, f32[32,896]{1,0:T(8,128)S(1)}, u32[]{:S(2)}, u32[]{:S(2)}) collective-permute-start(f32[32,896]{1,0:T(8,128)S(1)} %products.37), channel_id=1, source_target_pairs={{0,4},{1,13},{2,6},{3,15},{4,0},{5,9},{6,2},{7,11},{8,12},{9,5},{1... | collective-permute-start | bytes 344072 | tf_op jit(solution)/shard_map/ppermute | solution.py:341
  53.3 7.6 %collective-permute-start.13 = (f32[32,1152]{1,0:T(8,128)S(1)}, f32[32,1152]{1,0:T(8,128)S(1)}, u32[]{:S(2)}, u32[]{:S(2)}) collective-permute-start(f32[32,1152]{1,0:T(8,128)S(1)} %add.99), channel_id=1, source_target_pairs={{0,8},{1,5},{2,10},{3,7},{4,12},{5,1},{6,14},{7,3},{8,0},{9,13},{1... | collective-permute-start | bytes 442376 | tf_op jit(solution)/shard_map/ppermute | solution.py:341
  57.3 6.7 %collective-permute-start.11 = (f32[32,896]{1,0:T(8,128)S(1)}, f32[32,896]{1,0:T(8,128)S(1)}, u32[]{:S(2)}, u32[]{:S(2)}) collective-permute-start(f32[32,896]{1,0:T(8,128)S(1)} %add.98), channel_id=1, source_target_pairs={{0,8},{1,5},{2,10},{3,7},{4,12},{5,1},{6,14},{7,3},{8,0},{9,13},{1... | collective-permute-start | bytes 344072 | tf_op jit(solution)/shard_map/ppermute | solution.py:341
  66.1 5.6 %collective-permute-start.15 = (f32[32,1024]{1,0:T(8,128)S(1)}, f32[32,1024]{1,0:T(8,128)S(1)}, u32[]{:S(2)}, u32[]{:S(2)}) collective-permute-start(f32[32,1024]{1,0:T(8,128)S(1)} %add.102), channel_id=1, source_target_pairs={{0,2},{1,3},{2,0},{3,1},{4,6},{5,7},{6,4},{7,5},{8,10},{9,11},{10,... | collective-permute-start | bytes 393224 | tf_op jit(solution)/shard_map/ppermute | solution.py:334
  71.7 1.4 collective-permute-start.16
  73.7 5.8 %collective-permute-start.19 = (f32[32,1152]{1,0:T(8,128)S(1)}, f32[32,1152]{1,0:T(8,128)S(1)}, u32[]{:S(2)}, u32[]{:S(2)}) collective-permute-start(f32[32,1152]{1,0:T(8,128)S(1)} %products.44), channel_id=1, source_target_pairs={{0,4},{1,13},{2,6},{3,15},{4,0},{5,9},{6,2},{7,11},{8,12},{9,5},{1... | collective-permute-start | bytes 442376 | tf_op jit(solution)/shard_map/ppermute | solution.py:341
  74.4 7.6 %collective-permute-start.17 = (f32[32,896]{1,0:T(8,128)S(1)}, f32[32,896]{1,0:T(8,128)S(1)}, u32[]{:S(2)}, u32[]{:S(2)}) collective-permute-start(f32[32,896]{1,0:T(8,128)S(1)} %products.43), channel_id=1, source_target_pairs={{0,4},{1,13},{2,6},{3,15},{4,0},{5,9},{6,2},{7,11},{8,12},{9,5},{1... | collective-permute-start | bytes 344072 | tf_op jit(solution)/shard_map/ppermute | solution.py:341
  79.5 7.6 %collective-permute-start.20 = (f32[32,1152]{1,0:T(8,128)S(1)}, f32[32,1152]{1,0:T(8,128)S(1)}, u32[]{:S(2)}, u32[]{:S(2)}) collective-permute-start(f32[32,1152]{1,0:T(8,128)S(1)} %add.105), channel_id=1, source_target_pairs={{0,8},{1,5},{2,10},{3,7},{4,12},{5,1},{6,14},{7,3},{8,0},{9,13},{1... | collective-permute-start | bytes 442376 | tf_op jit(solution)/shard_map/ppermute | solution.py:341
  82.0 7.7 %collective-permute-start.18 = (f32[32,896]{1,0:T(8,128)S(1)}, f32[32,896]{1,0:T(8,128)S(1)}, u32[]{:S(2)}, u32[]{:S(2)}) collective-permute-start(f32[32,896]{1,0:T(8,128)S(1)} %add.104), channel_id=1, source_target_pairs={{0,8},{1,5},{2,10},{3,7},{4,12},{5,1},{6,14},{7,3},{8,0},{9,13},{1... | collective-permute-start | bytes 344072 | tf_op jit(solution)/shard_map/ppermute | solution.py:341
  91.5 5.6 %collective-permute-start.22 = (f32[32,1024]{1,0:T(8,128)S(1)}, f32[32,1024]{1,0:T(8,128)S(1)}, u32[]{:S(2)}, u32[]{:S(2)}) collective-permute-start(f32[32,1024]{1,0:T(8,128)S(1)} %add.108), channel_id=1, source_target_pairs={{0,2},{1,3},{2,0},{3,1},{4,6},{5,7},{6,4},{7,5},{8,10},{9,11},{10,... | collective-permute-start | bytes 393224 | tf_op jit(solution)/shard_map/ppermute | solution.py:334
  97.1 1.4 collective-permute-start.23
  99.1 5.9 %collective-permute-start.26 = (f32[32,1152]{1,0:T(8,128)S(1)}, f32[32,1152]{1,0:T(8,128)S(1)}, u32[]{:S(2)}, u32[]{:S(2)}) collective-permute-start(f32[32,1152]{1,0:T(8,128)S(1)} %products.51), channel_id=1, source_target_pairs={{0,4},{1,13},{2,6},{3,15},{4,0},{5,9},{6,2},{7,11},{8,12},{9,5},{1... | collective-permute-start | bytes 442376 | tf_op jit(solution)/shard_map/ppermute | solution.py:341
  100.0 7.4 %collective-permute-start.24 = (f32[32,896]{1,0:T(8,128)S(1)}, f32[32,896]{1,0:T(8,128)S(1)}, u32[]{:S(2)}, u32[]{:S(2)}) collective-permute-start(f32[32,896]{1,0:T(8,128)S(1)} %products.50), channel_id=1, source_target_pairs={{0,4},{1,13},{2,6},{3,15},{4,0},{5,9},{6,2},{7,11},{8,12},{9,5},{1... | collective-permute-start | bytes 344072 | tf_op jit(solution)/shard_map/ppermute | solution.py:341
  105.0 7.6 %collective-permute-start.27 = (f32[32,1152]{1,0:T(8,128)S(1)}, f32[32,1152]{1,0:T(8,128)S(1)}, u32[]{:S(2)}, u32[]{:S(2)}) collective-permute-start(f32[32,1152]{1,0:T(8,128)S(1)} %add.111), channel_id=1, source_target_pairs={{0,8},{1,5},{2,10},{3,7},{4,12},{5,1},{6,14},{7,3},{8,0},{9,13},{1... | collective-permute-start | bytes 442376 | tf_op jit(solution)/shard_map/ppermute | solution.py:341
  107.5 7.7 %collective-permute-start.25 = (f32[32,896]{1,0:T(8,128)S(1)}, f32[32,896]{1,0:T(8,128)S(1)}, u32[]{:S(2)}, u32[]{:S(2)}) collective-permute-start(f32[32,896]{1,0:T(8,128)S(1)} %add.110), channel_id=1, source_target_pairs={{0,8},{1,5},{2,10},{3,7},{4,12},{5,1},{6,14},{7,3},{8,0},{9,13},{1... | collective-permute-start | bytes 344072 | tf_op jit(solution)/shard_map/ppermute | solution.py:341
  117.0 5.6 %collective-permute-start.29 = (f32[32,1024]{1,0:T(8,128)S(1)}, f32[32,1024]{1,0:T(8,128)S(1)}, u32[]{:S(2)}, u32[]{:S(2)}) collective-permute-start(f32[32,1024]{1,0:T(8,128)S(1)} %add.114), channel_id=1, source_target_pairs={{0,2},{1,3},{2,0},{3,1},{4,6},{5,7},{6,4},{7,5},{8,10},{9,11},{10,... | collective-permute-start | bytes 393224 | tf_op jit(solution)/shard_map/ppermute | solution.py:334
  122.6 1.4 collective-permute-start.30
  124.6 5.9 %collective-permute-start.31 = (f32[32,1152]{1,0:T(8,128)S(1)}, f32[32,1152]{1,0:T(8,128)S(1)}, u32[]{:S(2)}, u32[]{:S(2)}) collective-permute-start(f32[32,1152]{1,0:T(8,128)S(1)} %products.56), channel_id=1, source_target_pairs={{0,4},{1,13},{2,6},{3,15},{4,0},{5,9},{6,2},{7,11},{8,12},{9,5},{1... | collective-permute-start | bytes 442376 | tf_op jit(solution)/shard_map/ppermute | solution.py:341
  125.1 7.8 %collective-permute-start.33 = (f32[32,896]{1,0:T(8,128)S(1)}, f32[32,896]{1,0:T(8,128)S(1)}, u32[]{:S(2)}, u32[]{:S(2)}) collective-permute-start(f32[32,896]{1,0:T(8,128)S(1)} %products.57), channel_id=1, source_target_pairs={{0,4},{1,13},{2,6},{3,15},{4,0},{5,9},{6,2},{7,11},{8,12},{9,5},{1... | collective-permute-start | bytes 344072 | tf_op jit(solution)/shard_map/ppermute | solution.py:341
  130.5 7.7 %collective-permute-start.32 = (f32[32,1152]{1,0:T(8,128)S(1)}, f32[32,1152]{1,0:T(8,128)S(1)}, u32[]{:S(2)}, u32[]{:S(2)}) collective-permute-start(f32[32,1152]{1,0:T(8,128)S(1)} %add.116), channel_id=1, source_target_pairs={{0,8},{1,5},{2,10},{3,7},{4,12},{5,1},{6,14},{7,3},{8,0},{9,13},{1... | collective-permute-start | bytes 442376 | tf_op jit(solution)/shard_map/ppermute | solution.py:341
  132.9 7.6 %collective-permute-start.34 = (f32[32,896]{1,0:T(8,128)S(1)}, f32[32,896]{1,0:T(8,128)S(1)}, u32[]{:S(2)}, u32[]{:S(2)}) collective-permute-start(f32[32,896]{1,0:T(8,128)S(1)} %add.118), channel_id=1, source_target_pairs={{0,8},{1,5},{2,10},{3,7},{4,12},{5,1},{6,14},{7,3},{8,0},{9,13},{1... | collective-permute-start | bytes 344072 | tf_op jit(solution)/shard_map/ppermute | solution.py:341
  (4 other events, 10.5 us)
